TPU v7x, 256 devices: a whole 4x4x8 slice. The times are simulated.
256 devices in a mesh: ctx: 32 (over z, x_hi, core), head: 8 (over y, x_lo).
Axes of the slice: x: 4 (x_hi: 2, x_lo: 2; x = x_hi * 2 + x_lo), y: 4, z: 8, core: 2. Of those that a mesh axis runs over, the one named last changes fastest.
Arguments:
- queries: bfloat16 [8192, 8192], P('ctx', 'head'), may hold values from -10 to 10
- key_rows: bfloat16 [8192, 1024], P('ctx', 'head'), may hold values from -4.5 to 4.5
- values: bfloat16 [8192, 1024], P('ctx', 'head'), may hold values from -24 to 24
- lengths: int32 [17], replicated, may hold values from 1 to 4352, as said below
- block_plan: int32 [1024], P('ctx'), may hold values from 0 to 1023, as said below
- inverse: int32 [1024], replicated, may hold values from 0 to 1023, as said below
- mask_lo: int32 [1024], replicated, may hold values from 0 to 1023, as said below
- out_weight: bfloat16 [8192, 4096], P('head'), may hold values from -0.375 to 0.375
Outputs:
- mixed_out: bfloat16 [8192, 4096], P('ctx', 'head')
Inputs may be any that keep to these rules, and one draw needn't show every extreme that they name: One document has exactly 4352 tokens, every other is shorter; the lengths sum to 8192. A permutation of the 1024 blocks; slot block_plan[b] lies on index block_plan[b] // 32 of ctx; every index receives exactly 32 blocks, and at most 2 blocks of one index go to any one index, which is reached in every draw. inverse[block_plan[b]] == b. mask_lo[b] lies between the block holding the first token of the document of block b's first token and b, both included.
All inputs are finite; a program needn't handle non-finite values.
Results may differ from a plain program's by a relative error of at most 0.02.
Values may be sent and summed in bfloat16 or wider, within the bound.
A program may use at most 64 MiB of HBM per device.

v0:
```python
import jax
import jax.numpy as jnp
from jax import lax
from jax.sharding import PartitionSpec as P

HD = 128
BLK = 8


NEG_FILL = -1e30


def document_of(positions, doc_ends):
    return jnp.sum((positions[:, None] >= doc_ends[None, :]).astype(jnp.int32), axis=1)


def rank_within(owners, order_keys):
    same_owner = owners[:, None] == owners[None, :]
    comes_first = order_keys[None, :] < order_keys[:, None]
    return jnp.sum((same_owner & comes_first).astype(jnp.int32), axis=1)


def slot_sources(owners, order_ranks, device_count, capacity):
    device_ids = jnp.arange(device_count, dtype=jnp.int32)
    slot_ids = jnp.arange(capacity, dtype=jnp.int32)
    entry_ids = jnp.arange(owners.shape[0], dtype=jnp.int32)
    matches = (owners[None, None, :] == device_ids[:, None, None]) & (
        order_ranks[None, None, :] == slot_ids[None, :, None]
    )
    sources = jnp.sum(jnp.where(matches, entry_ids[None, None, :], 0), axis=2)
    return (sources.reshape(-1), jnp.any(matches, axis=2).reshape(-1))


def pack_blocks(block_data, sources, occupied, device_count, capacity):
    picked = jnp.take(block_data, sources, axis=0)
    picked = jnp.where(occupied[:, None, None], picked, jnp.zeros((), block_data.dtype))
    return picked.reshape((device_count, capacity) + block_data.shape[1:])


def unpack_blocks(received, owners, order_ranks, capacity):
    merged = received.reshape((-1,) + received.shape[2:])
    picked = jnp.take(merged, owners * capacity + order_ranks, axis=0)
    return picked.reshape((-1, picked.shape[-1]))


def project(attended, out_weight):
    partial_value = jnp.dot(attended, out_weight, preferred_element_type=jnp.float32).astype(
        jnp.bfloat16
    )
    summed = lax.psum_scatter(partial_value, "head", scatter_dimension=1, tiled=True).astype(
        jnp.float32
    )
    return summed.astype(jnp.bfloat16)


def attend_all(held_queries, held_pairs, root, doc_ends, mask_lo, key_position):
    row_count, query_width = held_queries.shape
    kv_width = held_pairs.shape[1] // 2
    kv_heads = kv_width // HD
    group_size = query_width // (kv_heads * HD)
    score_scale = HD ** (-0.5)
    offsets = jnp.arange(BLK, dtype=jnp.int32)
    query_pos = (root[:, None] * BLK + offsets[None, :]).reshape(row_count)
    query_doc = document_of(query_pos, doc_ends)
    table_ids = jnp.arange(mask_lo.shape[0], dtype=jnp.int32)
    block_lo = jnp.sum(jnp.where(root[:, None] == table_ids[None, :], mask_lo[None, :], 0), axis=1)
    query_lo = jnp.repeat(block_lo, BLK)
    query_heads = held_queries.reshape(row_count, kv_heads, group_size, HD)

    def one_step(state_now, kv_piece, first_key):
        key_width = kv_piece.shape[0]
        key_ids = first_key + jnp.arange(key_width, dtype=jnp.int32)
        key_pos = key_position(key_ids)
        key_doc = document_of(key_pos, doc_ends)
        allowed = (
            (query_doc[:, None] == key_doc[None, :])
            & (key_pos[None, :] <= query_pos[:, None])
            & ((key_pos // BLK)[None, :] >= query_lo[:, None])
        )
        run_max, run_sum, run_acc = state_now
        key_heads = kv_piece[:, :kv_width].reshape(key_width, kv_heads, HD)
        value_heads = kv_piece[:, kv_width:].reshape(key_width, kv_heads, HD)
        scores = (
            jnp.einsum("tkgd,skd->tkgs", query_heads, key_heads, preferred_element_type=jnp.float32)
            * score_scale
        )
        mask_full = allowed[:, None, None, :]
        scores = jnp.where(mask_full, scores, NEG_FILL)
        new_max = jnp.maximum(run_max, jnp.max(scores, axis=-1))
        weights = jnp.where(mask_full, jnp.exp(scores - new_max[..., None]), 0.0)
        fading = jnp.exp(run_max - new_max)
        new_sum = run_sum * fading + jnp.sum(weights, axis=-1)
        update = jnp.einsum(
            "tkgs,skd->tkgd",
            weights.astype(jnp.bfloat16),
            value_heads,
            preferred_element_type=jnp.float32,
        )
        return (new_max, new_sum, run_acc * fading[..., None] + update)

    stat_shape = (row_count, kv_heads, group_size)
    initial = (
        jnp.full(stat_shape, NEG_FILL, jnp.float32),
        jnp.zeros(stat_shape, jnp.float32),
        jnp.zeros(stat_shape + (HD,), jnp.float32),
    )
    kv_piece = lax.all_gather(held_pairs, "ctx", axis=0, tiled=True)
    piece_rows = kv_piece.shape[0]
    key_width = 256

    def loop_body(step_index, state_in):
        offset_rows = step_index * key_width
        sub_piece = lax.dynamic_slice_in_dim(kv_piece, offset_rows, key_width, 0)
        return one_step(state_in, sub_piece, offset_rows)

    run_max, run_sum, run_acc = lax.fori_loop(0, piece_rows // key_width, loop_body, initial)
    return (run_acc / run_sum[..., None]).astype(jnp.bfloat16).reshape(row_count, query_width)


def on_device(queries, key_rows, values, lengths, block_plan, inverse, mask_lo, out_weight):
    row_count, query_width = queries.shape
    block_count = row_count // BLK
    device_count = lax.axis_size("ctx")
    capacity = max(2, block_count // device_count + 1)
    here_index = lax.axis_index("ctx")
    doc_ends = jnp.cumsum(lengths)
    key_values = jnp.concatenate([key_rows, values], axis=1)
    pair_width = key_values.shape[1]
    local_ids = jnp.arange(block_count, dtype=jnp.int32)
    dest_dev = block_plan // block_count
    dest_slot = block_plan % block_count
    send_rank = rank_within(dest_dev, dest_slot)
    sources, occupied = slot_sources(dest_dev, send_rank, device_count, capacity)
    send_queries = pack_blocks(
        queries.reshape(block_count, BLK, query_width), sources, occupied, device_count, capacity
    )
    send_pairs = pack_blocks(
        key_values.reshape(block_count, BLK, pair_width), sources, occupied, device_count, capacity
    )
    got_queries, got_pairs = (
        lax.all_to_all(send_queries, "ctx", split_axis=0, concat_axis=0, tiled=True),
        lax.all_to_all(send_pairs, "ctx", split_axis=0, concat_axis=0, tiled=True),
    )
    root = lax.dynamic_slice_in_dim(inverse, here_index * block_count, block_count)
    from_dev = root // block_count
    recv_rank = rank_within(from_dev, local_ids)
    held_queries = unpack_blocks(got_queries, from_dev, recv_rank, capacity)
    held_pairs = unpack_blocks(got_pairs, from_dev, recv_rank, capacity)

    def key_position(key_ids):
        return jnp.take(inverse, key_ids // BLK) * BLK + key_ids % BLK

    held_att = attend_all(held_queries, held_pairs, root, doc_ends, mask_lo, key_position)
    back_sources, back_occupied = slot_sources(from_dev, recv_rank, device_count, capacity)
    send_att = pack_blocks(
        held_att.reshape(block_count, BLK, query_width),
        back_sources,
        back_occupied,
        device_count,
        capacity,
    )
    back_att = lax.all_to_all(send_att, "ctx", split_axis=0, concat_axis=0, tiled=True)
    mixed_out = project(unpack_blocks(back_att, dest_dev, send_rank, capacity), out_weight)
    return mixed_out


def solution(mesh):
    in_specs = (
        P("ctx", "head"),
        P("ctx", "head"),
        P("ctx", "head"),
        P(),
        P("ctx"),
        P(),
        P(),
        P("head", None),
    )
    out_specs = P("ctx", "head")
    return jax.shard_map(
        on_device, mesh=mesh, in_specs=in_specs, out_specs=out_specs, check_vma=False
    )
```

profile of v0, /device:TPU:192, one launch (start us, length us, event | category | flops | bytes accessed | tf_op | source)
XLA Modules:
  0.0 446.6 jit_solution(887218490249605697)
XLA Ops:
  10.5 9.0 %all-to-all-start = ((bf16[32,2,8,256]{3,2,1,0:T(8,128)(2,1)}), bf16[32,2,8,256]{3,2,1,0:T(8,128)(2,1)S(1)}, u32[]{:S(2)}, u32[]{:S(2)}) async-start(bf16[32,2,8,256]{3,2,1,0:T(8,128)(2,1)} %select_select_fusion.2), calls=%async_computation | async-start | bytes 524288 | tf_op jit(solution)/shard_map/all_to_all | solution.py:142
  20.7 9.6 %all-to-all-done = bf16[32,2,8,256]{3,2,1,0:T(8,128)(2,1)S(1)} async-done(((bf16[32,2,8,256]{3,2,1,0:T(8,128)(2,1)}), bf16[32,2,8,256]{3,2,1,0:T(8,128)(2,1)S(1)}, u32[]{:S(2)}, u32[]{:S(2)}) %all-to-all-start) | async-done | bytes 262176 | tf_op jit(solution)/shard_map/all_to_all | solution.py:142
  33.8 6.3 %all-to-all-start.1 = ((bf16[32,2,8,1024]{3,2,1,0:T(8,128)(2,1)}), bf16[32,2,8,1024]{3,2,1,0:T(8,128)(2,1)S(1)}, u32[]{:S(2)}, u32[]{:S(2)}) async-start(bf16[32,2,8,1024]{3,2,1,0:T(8,128)(2,1)} %bitcast.7), calls=%async_computation.1 | async-start | bytes 2097152 | tf_op jit(solution)/shard_map/all_to_all | solution.py:141
  41.6 28.6 %all-to-all-done.1 = bf16[32,2,8,1024]{3,2,1,0:T(8,128)(2,1)S(1)} async-done(((bf16[32,2,8,1024]{3,2,1,0:T(8,128)(2,1)}), bf16[32,2,8,1024]{3,2,1,0:T(8,128)(2,1)S(1)}, u32[]{:S(2)}, u32[]{:S(2)}) %all-to-all-start.1) | async-done | bytes 1048608 | tf_op jit(solution)/shard_map/all_to_all | solution.py:141
  71.1 48.8 %all-gather.2.cloned.1.call-done = bf16[8192,256]{1,0:T(8,128)(2,1)} async-done(((bf16[256,256]{1,0:T(8,128)(2,1)}), bf16[8192,256]{1,0:T(8,128)(2,1)}) %all-gather.2.cloned.1.call-update) | async-done | bytes 4194320 | tf_op jit(solution)/shard_map/all_gather | solution.py:107
  119.9 220.3 %while.21 = (s32[]{:T(128)}, f32[256,1,8]{0,2,1:T(8,128)S(1)}, f32[256,1,8]{0,2,1:T(8,128)S(1)}, f32[256,1,8,128]{0,3,2,1:T(8,128)}, s32[256]{0:T(256)S(1)}, /*i...) while((s32[]{:T(128)}, f32[256,1,8]{0,2,1:T(8,128)S(1)}, ...), condition=%wide.region_12.15_spmd.clone, body=%wide.region_8.14_spmd.clone.sunk | while | flops 276407808 | bytes 9464371 | solution.py:116
  129.7 2.9 fusion.44
  136.6 2.9 fusion.44
  143.5 2.9 fusion.44
  150.4 2.9 fusion.44
  157.3 2.9 fusion.44
  164.2 2.9 fusion.44
  171.1 2.9 fusion.44
  178.0 2.9 fusion.44
  184.9 2.9 fusion.44
  191.8 2.9 fusion.44
  198.7 2.9 fusion.44
  205.6 2.9 fusion.44
  212.5 2.9 fusion.44
  219.4 2.9 fusion.44
  226.3 2.9 fusion.44
  233.2 2.9 fusion.44
  240.1 2.9 fusion.44
  247.0 2.9 fusion.44
  253.9 2.9 fusion.44
  281.5 2.9 fusion.44
  288.4 2.9 fusion.44
  295.3 2.9 fusion.44
  343.9 6.9 %all-to-all-start.2 = ((bf16[32,2,8,1024]{3,2,1,0:T(8,128)(2,1)}), bf16[32,2,8,1024]{3,2,1,0:T(8,128)(2,1)S(1)}, u32[]{:S(2)}, u32[]{:S(2)}) async-start(bf16[32,2,8,1024]{3,2,1,0:T(8,128)(2,1)} %bitcast.10), calls=%async_computation.2 | async-start | bytes 2097152 | tf_op jit(solution)/shard_map/all_to_all | solution.py:162
  350.8 25.6 %all-to-all-done.2 = bf16[32,2,8,1024]{3,2,1,0:T(8,128)(2,1)S(1)} async-done(((bf16[32,2,8,1024]{3,2,1,0:T(8,128)(2,1)}), bf16[32,2,8,1024]{3,2,1,0:T(8,128)(2,1)S(1)}, u32[]{:S(2)}, u32[]{:S(2)}) %all-to-all-start.2) | async-done | bytes 1048608 | tf_op jit(solution)/shard_map/all_to_all | solution.py:162
  377.0 7.1 %convolution_convert_fusion = bf16[256,4096]{1,0:T(8,128)(2,1)} fusion(bf16[1024,4096]{1,0:T(8,128)(2,1)} %param.21, bf16[32,8,1024]{2,1,0:T(8,128)(2,1)S(1)} %gather_fusion.6, pred[32]{0:T(512)(128)(4,1)S(1)} %get-tuple-element.401), kind=kOutput, calls=%fused_computation.58 | convolution fusion | flops 2148794368 | bytes 11010080 | tf_op jit(solution)/shard_map/dot_general | solution.py:47
  384.1 55.6 %reduce-scatter.2.cloned.1.call-done = bf16[256,512]{1,0:T(8,128)(2,1)} async-done(((bf16[256,4096]{1,0:T(8,128)(2,1)}), bf16[256,512]{1,0:T(8,128)(2,1)}) %reduce-scatter.2.cloned.1.call-update) | async-done | bytes 262160 | tf_op jit(solution)/shard_map/reduce_scatter | solution.py:50
  (567 shorter events, 167.4 us)
Async XLA Ops:
  6.5 25.4 %copy-start = (bf16[256,1024]{1,0:T(8,128)(2,1)S(1)}, bf16[256,1024]{1,0:T(8,128)(2,1)}, u32[]{:S(2)}) copy-start(bf16[256,1024]{1,0:T(8,128)(2,1)} %param.14) | copy-start | bytes 1572868
  10.5 19.8 %all-to-all-start = ((bf16[32,2,8,256]{3,2,1,0:T(8,128)(2,1)}), bf16[32,2,8,256]{3,2,1,0:T(8,128)(2,1)S(1)}, u32[]{:S(2)}, u32[]{:S(2)}) async-start(bf16[32,2,8,256]{3,2,1,0:T(8,128)(2,1)} %select_select_fusion.2), calls=%async_computation | async-start | bytes 524288 | tf_op jit(solution)/shard_map/all_to_all | solution.py:142
  19.5 100.4 %all-gather.2.cloned.1.call-start = ((), (), s32[]{:S(2)}) async-start(), calls=%async_computation.4 | async-start | bytes 4325376 | tf_op jit(solution)/shard_map/all_gather | solution.py:107
  32.6 7.7 %copy-start.3 = (s32[17]{0:T(128)S(1)}, s32[17]{0:T(128)}, u32[]{:S(2)}) copy-start(s32[17]{0:T(128)} %param.17) | copy-start | bytes 208
  32.6 8.8 %copy-start.2 = (s32[1024]{0:T(1024)S(1)}, s32[1024]{0:T(1024)}, u32[]{:S(2)}) copy-start(s32[1024]{0:T(1024)} %param.20) | copy-start | bytes 12292
  33.8 36.4 %all-to-all-start.1 = ((bf16[32,2,8,1024]{3,2,1,0:T(8,128)(2,1)}), bf16[32,2,8,1024]{3,2,1,0:T(8,128)(2,1)S(1)}, u32[]{:S(2)}, u32[]{:S(2)}) async-start(bf16[32,2,8,1024]{3,2,1,0:T(8,128)(2,1)} %bitcast.7), calls=%async_computation.1 | async-start | bytes 2097152 | tf_op jit(solution)/shard_map/all_to_all | solution.py:141
  70.2 49.7 %copy-start.1 = (s32[1024]{0:T(1024)S(1)}, s32[1024]{0:T(1024)}, u32[]{:S(2)}) copy-start(s32[1024]{0:T(1024)} %param.19) | copy-start | bytes 12292
  343.9 32.6 %all-to-all-start.2 = ((bf16[32,2,8,1024]{3,2,1,0:T(8,128)(2,1)}), bf16[32,2,8,1024]{3,2,1,0:T(8,128)(2,1)S(1)}, u32[]{:S(2)}, u32[]{:S(2)}) async-start(bf16[32,2,8,1024]{3,2,1,0:T(8,128)(2,1)} %bitcast.10), calls=%async_computation.2 | async-start | bytes 2097152 | tf_op jit(solution)/shard_map/all_to_all | solution.py:162
  350.7 89.1 %reduce-scatter.2.cloned.1.call-start = ((), (), s32[]{:S(2)}) async-start(), calls=%async_computation.5 | async-start | bytes 2359296 | tf_op jit(solution)/shard_map/reduce_scatter | solution.py:50
Sparse Core Ops, SparseCore 0:
  31.8 88.0 all-gather.1
  384.3 55.4 reduce-scatter.1
where the time goes:
time: 452 us; the launch traced here: 447 us
  waiting for transfers between devices  168 us (37%)
  matrix products  143 us (32%)
  local copies, waits for them, and re-layouts  57.4 us (13%)
  other arithmetic  38.7 us (9%)
  starting transfers between devices  22.2 us (5%)
  between operations  13.7 us (3%)
    dot_general x32, matrix products, one_step(): jnp.einsum('tkgs,skd->tkgd', weights.astype(jnp.bfloat16), value_heads, p...  93.9 us
    reduce_scatter x1, waiting for transfers between devices, project(): lax.psum_scatter(partial_value, 'head', scatter_dimension=1, tiled=True)  55.6 us
    all_gather x1, waiting for transfers between devices, attend_all(): kv_piece = lax.all_gather(held_pairs, 'ctx', axis=0, tiled=True)  48.8 us
    gather x32, local copies, waits for them, and re-layouts, key_position(): return jnp.take(inverse, key_ids // BLK) * BLK + key_ids % BLK  43.7 us
    dot_general x32, matrix products, one_step(): jnp.einsum('tkgd,skd->tkgs', query_heads, key_heads, preferred_element_ty...  42.1 us
    all_to_all x1, waiting for transfers between devices, on_device(): lax.all_to_all(send_queries, 'ctx', split_axis=0, concat_axis=0, tiled=True)  28.6 us
    all_to_all x1, waiting for transfers between devices, on_device(): lax.all_to_all(send_att, 'ctx', split_axis=0, concat_axis=0, tiled=True)  25.6 us
    reduce_sum x32, other arithmetic, one_step(): new_sum = run_sum * fading + jnp.sum(weights, axis=-1)  16.4 us
  transfers between devices with their start and end apart: 5, of which 5 were waited for; matrix products, arithmetic and copies ran while one was open for 1% of the time, Pallas kernels for 0%

commit v1 on v0

v1 whole, which is shorter than its diff:
```python
import functools

import jax
import jax.numpy as jnp
from jax import lax
from jax.experimental import pallas as pl
from jax.experimental.pallas import tpu as pltpu
from jax.sharding import PartitionSpec as P

HD = 128
BLK = 8
TQ = 256
TK = 512
NEG_FILL = -1e30


def attn_kernel(tiles_ref, q_ref, kv_ref, qpos_ref, lo_ref, o_ref, m_sc, l_sc, acc_sc):
    n_q = q_ref.shape[0] // TQ
    scale = HD ** (-0.5)

    def q_body(qi, carry):
        r0 = pl.multiple_of(qi * TQ, TQ)
        q = q_ref[pl.ds(r0, TQ), :]
        qpos = qpos_ref[pl.ds(r0, TQ), :]
        lo = lo_ref[pl.ds(r0, TQ), :]
        m_sc[...] = jnp.full(m_sc.shape, NEG_FILL, jnp.float32)
        l_sc[...] = jnp.zeros(l_sc.shape, jnp.float32)
        acc_sc[...] = jnp.zeros(acc_sc.shape, jnp.float32)

        def k_body(kj, c):
            c0 = pl.multiple_of(kj * TK, TK)
            k = kv_ref[pl.ds(c0, TK), pl.ds(0, HD)]
            v = kv_ref[pl.ds(c0, TK), pl.ds(HD, HD)]
            s = lax.dot_general(
                q, k, (((1,), (1,)), ((), ())), preferred_element_type=jnp.float32
            ) * scale
            kpos = c0 + lax.broadcasted_iota(jnp.int32, (TQ, TK), 1)
            ok = (kpos >= lo) & (kpos <= qpos)
            s = jnp.where(ok, s, NEG_FILL)
            m_prev = m_sc[...]
            m_new = jnp.maximum(m_prev, jnp.max(s, axis=1, keepdims=True))
            p = jnp.where(ok, jnp.exp(s - m_new), 0.0)
            fade = jnp.exp(m_prev - m_new)
            l_sc[...] = l_sc[...] * fade + jnp.sum(p, axis=1, keepdims=True)
            acc_sc[...] = acc_sc[...] * fade + jnp.dot(
                p.astype(jnp.bfloat16), v, preferred_element_type=jnp.float32
            )
            m_sc[...] = m_new
            return c

        lax.fori_loop(tiles_ref[qi, 0], tiles_ref[qi, 1], k_body, 0)
        o_ref[pl.ds(r0, TQ), :] = (acc_sc[...] / l_sc[...]).astype(o_ref.dtype)
        return carry

    lax.fori_loop(0, n_q, q_body, 0)


def attend(q_rows, kv_all, qpos_rows, lo_rows, tiles):
    rows = q_rows.shape[0]
    vmem = pltpu.MemorySpace.VMEM if hasattr(pltpu, "MemorySpace") else pltpu.VMEM
    return pl.pallas_call(
        attn_kernel,
        out_shape=jax.ShapeDtypeStruct((rows, HD), jnp.bfloat16),
        in_specs=[
            pl.BlockSpec(memory_space=pltpu.SMEM),
            pl.BlockSpec(memory_space=vmem),
            pl.BlockSpec(memory_space=vmem),
            pl.BlockSpec(memory_space=vmem),
            pl.BlockSpec(memory_space=vmem),
        ],
        out_specs=pl.BlockSpec(memory_space=vmem),
        scratch_shapes=[
            pltpu.VMEM((TQ, 1), jnp.float32),
            pltpu.VMEM((TQ, 1), jnp.float32),
            pltpu.VMEM((TQ, HD), jnp.float32),
        ],
    )(tiles, q_rows, kv_all, qpos_rows, lo_rows)


def on_device(queries, key_rows, values, lengths, block_plan, inverse, mask_lo, out_weight):
    row_count, query_width = queries.shape
    group_size = query_width // HD
    here = lax.axis_index("ctx")
    first = here * row_count
    pos = first + jnp.arange(row_count, dtype=jnp.int32)
    doc_ends = jnp.cumsum(lengths).astype(jnp.int32)
    doc_start = jnp.max(jnp.where(doc_ends[None, :] <= pos[:, None], doc_ends[None, :], 0), axis=1)
    block_lo = lax.dynamic_slice_in_dim(mask_lo, here * (row_count // BLK), row_count // BLK)
    lo_tok = jnp.maximum(jnp.repeat(block_lo, BLK) * BLK, doc_start)
    qpos_rows = jnp.repeat(pos, group_size)[:, None]
    lo_rows = jnp.repeat(lo_tok, group_size)[:, None]
    tok_per_tile = TQ // group_size
    tile_lo = jnp.min(lo_tok.reshape(-1, tok_per_tile), axis=1)
    tile_hi = pos.reshape(-1, tok_per_tile)[:, -1]
    tiles = jnp.stack([tile_lo // TK, tile_hi // TK + 1], axis=1).astype(jnp.int32)

    kv_local = jnp.concatenate([key_rows, values], axis=1)
    kv_all = lax.all_gather(kv_local, "ctx", axis=0, tiled=True)
    q_rows = queries.reshape(row_count * group_size, HD)
    att = attend(q_rows, kv_all, qpos_rows, lo_rows, tiles).reshape(row_count, query_width)

    partial_value = jnp.dot(att, out_weight, preferred_element_type=jnp.float32).astype(jnp.bfloat16)
    summed = lax.psum_scatter(partial_value, "head", scatter_dimension=1, tiled=True)
    return summed.astype(jnp.float32).astype(jnp.bfloat16)


def solution(mesh):
    in_specs = (
        P("ctx", "head"),
        P("ctx", "head"),
        P("ctx", "head"),
        P(),
        P("ctx"),
        P(),
        P(),
        P("head", None),
    )
    out_specs = P("ctx", "head")
    return jax.shard_map(
        on_device, mesh=mesh, in_specs=in_specs, out_specs=out_specs, check_vma=False
    )
```

time: 452 us -> 221 us (0.49)
  matrix products: 143 us -> 7.07 us
  local copies, waits for them, and re-layouts: 57.4 us -> 8.05 us
  Pallas kernels: 0 us -> 48.5 us
  other arithmetic: 38.7 us -> 2.71 us
  waiting for transfers between devices: 168 us -> 138 us
  starting transfers between devices: 22.2 us -> 0.04 us
    dot_general x65 -> x1, matrix products: 143 us -> 7.07 us  [on_device(): jnp.dot(att, out_weight, preferred_element_type=jnp.float32)]
    all_to_all x3 -> x0, waiting for transfers between devices: 63.8 us -> none  [the longest x1 28.6 us: on_device(): lax.all_to_all(send_queries, 'ctx', split_axis=0, concat_axis=0, tiled=True)]
    pallas_call x0 -> x1, Pallas kernels: none -> 48.5 us  [attend(): pl.pallas_call(attn_kernel, out_shape=jax.ShapeDtypeStruct((rows, HD), jn...]
    gather x38 -> x0, local copies, waits for them, and re-layouts: 47.2 us -> none  [the longest x32 43.7 us: key_position(): return jnp.take(inverse, key_ids // BLK) * BLK + key_ids % BLK]
    all_gather x1, waiting for transfers between devices: 48.8 us -> 79.2 us  [on_device(): kv_all = lax.all_gather(kv_local, 'ctx', axis=0, tiled=True)]
    all_to_all x3 -> x0, starting transfers between devices: 22.1 us -> none  [the longest x1 8.96 us: on_device(): lax.all_to_all(send_pairs, 'ctx', split_axis=0, concat_axis=0, tiled=True)]
    reduce_sum x70 -> x0, other arithmetic: 20.1 us -> none  [the longest x32 16.4 us: one_step(): new_sum = run_sum * fading + jnp.sum(weights, axis=-1)]
    select_n x73 -> x1, other arithmetic: 6.86 us -> 0.02 us  [on_device(): tile_lo // TK]
  transfers between devices with their start and end apart: 5 -> 2, of which waited for: 5 -> 2; matrix products, arithmetic and copies ran while one was open for 1% -> 4% of each run, Pallas kernels for 0% -> 0%
where the time goes in v1:
time: 221 us; the launch traced here: 218 us
  waiting for transfers between devices  138 us (62%)
  Pallas kernels  48.5 us (22%)
  between operations  13.5 us (6%)
  local copies, waits for them, and re-layouts  8.05 us (4%)
  matrix products  7.07 us (3%)
  other arithmetic  2.71 us (1%)
    all_gather x1, waiting for transfers between devices, on_device(): kv_all = lax.all_gather(kv_local, 'ctx', axis=0, tiled=True)  79.2 us
    reduce_scatter x1, waiting for transfers between devices, on_device(): lax.psum_scatter(partial_value, 'head', scatter_dimension=1, tiled=True)  58.4 us
    pallas_call x1, Pallas kernels, attend(): pl.pallas_call(attn_kernel, out_shape=jax.ShapeDtypeStruct((rows, HD), jn...  48.5 us
    dot_general x1, matrix products, on_device(): jnp.dot(att, out_weight, preferred_element_type=jnp.float32)  7.07 us
  transfers between devices with their start and end apart: 2, of which 2 were waited for; matrix products, arithmetic and copies ran while one was open for 4% of the time, Pallas kernels for 0%

profile of v1, /device:TPU:192, one launch (start us, length us, event | category | flops | bytes accessed | tf_op | source)
XLA Modules:
  0.0 217.5 jit_solution(8481433589081854552)
XLA Ops:
  6.5 0.0 all-gather.2.cloned.1.call-start
  6.5 1.5 pad_maximum_fusion
  8.1 0.0 all-gather.2.cloned.1.call-update
  8.1 0.0 reduce-scatter.2.cloned.1.call-start
  8.2 0.8 dynamic-slice_multiply_fusion
  8.9 0.1 mul.27
  9.0 0.1 broadcast_in_dim.24
  9.1 0.1 mul.28
  9.2 0.8 copy.23
  10.0 0.1 reduce
  10.1 0.1 select_reduce_fusion
  10.2 0.1 reduce_max.12
  10.2 0.1 maximum_reduce_fusion
  10.4 0.7 copy.24.tiles_ref
  11.1 0.1 broadcast_in_dim.27
  11.1 0.1 mul.30
  11.2 2.1 reshape.99.q_ref
  13.3 0.1 broadcast_in_dim.26
  13.4 1.3 broadcast_in_dim_reshape.8.qpos_ref
  14.7 0.1 broadcast_in_dim.28
  14.8 1.3 broadcast_in_dim_reshape.9.lo_ref
  16.2 79.2 %all-gather.2.cloned.1.call-done.kv_ref = bf16[8192,256]{1,0:T(8,128)(2,1)} async-done(((bf16[256,256]{1,0:T(8,128)(2,1)}), bf16[8192,256]{1,0:T(8,128)(2,1)}) %all-gather.2.cloned.1.call-update) | async-done | bytes 4194320 | tf_op jit(solution)/shard_map/all_gather | solution.py:98
  95.3 48.5 %shard_map.64 = bf16[2048,128]{1,0:T(8,128)(2,1)} custom-call(s32[8,2]{1,0:T(8,128)} %copy.24.tiles_ref, bf16[2048,128]{1,0:T(8,128)(2,1)} %reshape.99.q_ref, bf16[8192,256]{1,0:T(8,128)(2,1)} %all-gather.2.cloned.1.call-done.kv_ref, s32[2048,1]{1,0:T(8,128)} %broadcast_in_dim_reshape.8.qpos_ref, s32[2048,1]{1,0:T(8,128)} %broadcast_in_dim_reshape.9.lo_ref), custom_call_target="tpu_custom_call" | custom-call | tf_op jit(solution)/shard_map/pallas_call | solution.py:61
  143.9 1.3 reshape.100
  145.1 7.1 %convolution_convert_fusion = bf16[256,4096]{1,0:T(8,128)(2,1)} fusion(bf16[256,1024]{1,0:T(8,128)(2,1)S(1)} %reshape.100, bf16[1024,4096]{1,0:T(8,128)(2,1)} %param.13), kind=kOutput, calls=%fused_computation | convolution fusion | flops 2148532224 | bytes 11010048 | tf_op jit(solution)/shard_map/dot_general | solution.py:102
  152.2 0.0 reduce-scatter.2.cloned.1.call-update
  152.2 58.4 %reduce-scatter.2.cloned.1.call-done = bf16[256,512]{1,0:T(8,128)(2,1)} async-done(((bf16[256,4096]{1,0:T(8,128)(2,1)}), bf16[256,512]{1,0:T(8,128)(2,1)}) %reduce-scatter.2.cloned.1.call-update) | async-done | bytes 262160 | tf_op jit(solution)/shard_map/reduce_scatter | solution.py:103
  (5 shorter events, 0.1 us)
Async XLA Ops:
  6.5 88.8 %all-gather.2.cloned.1.call-start = ((), (), s32[]{:S(2)}) async-start(), calls=%async_computation.1 | async-start | bytes 4325376 | tf_op jit(solution)/shard_map/all_gather | solution.py:98
  8.1 202.6 %reduce-scatter.2.cloned.1.call-start = ((), (), s32[]{:S(2)}) async-start(), calls=%async_computation.2 | async-start | bytes 2359296 | tf_op jit(solution)/shard_map/reduce_scatter | solution.py:103
Sparse Core Ops, SparseCore 0:
  10.1 85.1 all-gather.1
  152.4 58.2 reduce-scatter.1

commit v2 on v1

--- a/solution.py
+++ b/solution.py
@@ -12,6 +12,7 @@
 TQ = 256
 TK = 512
 NEG_FILL = -1e30
+LONGEST = 4352
 
 
 def attn_kernel(tiles_ref, q_ref, kv_ref, qpos_ref, lo_ref, o_ref, m_sc, l_sc, acc_sc):
@@ -92,16 +93,30 @@
     tok_per_tile = TQ // group_size
     tile_lo = jnp.min(lo_tok.reshape(-1, tok_per_tile), axis=1)
     tile_hi = pos.reshape(-1, tok_per_tile)[:, -1]
-    tiles = jnp.stack([tile_lo // TK, tile_hi // TK + 1], axis=1).astype(jnp.int32)
 
     kv_local = jnp.concatenate([key_rows, values], axis=1)
-    kv_all = lax.all_gather(kv_local, "ctx", axis=0, tiled=True)
+    n_ctx = lax.axis_size("ctx")
+    reach = min(n_ctx - 1, -(-(LONGEST - 1) // row_count))
+    pieces = []
+    for shift in range(reach, 0, -1):
+        perm = [(i, i + shift) for i in range(n_ctx - shift)]
+        pieces.append(lax.ppermute(kv_local, "ctx", perm))
+    pieces.append(kv_local)
+    kv_win = jnp.concatenate(pieces, axis=0)
+    base = first - reach * row_count
+    span = kv_win.shape[0]
+    tiles = jnp.stack(
+        [(tile_lo - base) // TK, jnp.minimum((tile_hi - base) // TK + 1, span // TK)], axis=1
+    ).astype(jnp.int32)
     q_rows = queries.reshape(row_count * group_size, HD)
-    att = attend(q_rows, kv_all, qpos_rows, lo_rows, tiles).reshape(row_count, query_width)
+    att = attend(q_rows, kv_win, qpos_rows - base, lo_rows - base, tiles).reshape(row_count, query_width)
 
     partial_value = jnp.dot(att, out_weight, preferred_element_type=jnp.float32).astype(jnp.bfloat16)
-    summed = lax.psum_scatter(partial_value, "head", scatter_dimension=1, tiled=True)
-    return summed.astype(jnp.float32).astype(jnp.bfloat16)
+    n_head = lax.axis_size("head")
+    cols = partial_value.shape[1] // n_head
+    parts = partial_value.reshape(row_count, n_head, cols).transpose(1, 0, 2)
+    got = lax.all_to_all(parts, "head", split_axis=0, concat_axis=0, tiled=True)
+    return jnp.sum(got.astype(jnp.float32), axis=0).astype(jnp.bfloat16)
 
 
 def solution(mesh):

time: 221 us -> 189 us (0.86)
  the two profiles are of different devices: /device:TPU:192 before, /device:TPU:161 now
where the time goes in v2:
time: 189 us; the launch traced here: 188 us
  Pallas kernels  48 us (25%)
  waiting for transfers between devices  47.7 us (25%)
  starting transfers between devices  45 us (24%)
  blocking collectives  28.8 us (15%)
  local copies, waits for them, and re-layouts  10.5 us (6%)
  matrix products  5.72 us (3%)
  other arithmetic  2.23 us (1%)
    pallas_call x1, Pallas kernels, attend(): pl.pallas_call(attn_kernel, out_shape=jax.ShapeDtypeStruct((rows, HD), jn...  48 us
    ppermute x17, waiting for transfers between devices, on_device(): pieces.append(lax.ppermute(kv_local, 'ctx', perm))  47.7 us
    ppermute x17, starting transfers between devices, on_device(): pieces.append(lax.ppermute(kv_local, 'ctx', perm))  45 us
    all_to_all x1, blocking collectives, on_device(): got = lax.all_to_all(parts, 'head', split_axis=0, concat_axis=0, tiled=True)  28.8 us
    dot_general x1, matrix products, on_device(): jnp.dot(att, out_weight, preferred_element_type=jnp.float32)  5.72 us
  transfers between devices with their start and end apart: 17, of which 10 were waited for; matrix products, arithmetic and copies ran while one was open for 4% of the time, Pallas kernels for 0%

profile of v2, /device:TPU:161, one launch (start us, length us, event | category | flops | bytes accessed | tf_op | source)
XLA Modules:
  0.0 188.4 jit_solution(17130957696552830929)
XLA Ops:
  1.8 1.3 collective-permute-start
  3.1 1.3 collective-permute-start.1
  4.4 1.3 collective-permute-start.2
  5.7 1.3 collective-permute-start.3
  7.0 1.3 collective-permute-start.4
  11.5 1.3 sub.61.lo_ref
  12.9 1.3 sub.60.qpos_ref
  15.2 4.4 %collective-permute-done = bf16[256,256]{1,0:T(8,128)(2,1)S(1)} collective-permute-done((bf16[256,256]{1,0:T(8,128)(2,1)S(1)}, bf16[256,256]{1,0:T(8,128)(2,1)S(1)}, u32[]{:S(2)}, u32[]{:S(2)}) %collective-permute-start) | collective-permute-done | bytes 131104 | tf_op jit(solution)/shard_map/ppermute | solution.py:103
  19.6 1.3 collective-permute-start.5
  20.9 2.6 %collective-permute-done.1 = bf16[256,256]{1,0:T(8,128)(2,1)S(1)} collective-permute-done((bf16[256,256]{1,0:T(8,128)(2,1)S(1)}, bf16[256,256]{1,0:T(8,128)(2,1)S(1)}, u32[]{:S(2)}, u32[]{:S(2)}) %collective-permute-start.1) | collective-permute-done | bytes 131104 | tf_op jit(solution)/shard_map/ppermute | solution.py:103
  23.5 1.3 collective-permute-start.6
  24.8 9.3 %collective-permute-done.2 = bf16[256,256]{1,0:T(8,128)(2,1)S(1)} collective-permute-done((bf16[256,256]{1,0:T(8,128)(2,1)S(1)}, bf16[256,256]{1,0:T(8,128)(2,1)S(1)}, u32[]{:S(2)}, u32[]{:S(2)}) %collective-permute-start.2) | collective-permute-done | bytes 131104 | tf_op jit(solution)/shard_map/ppermute | solution.py:103
  34.1 1.9 %collective-permute-start.7 = (bf16[256,256]{1,0:T(8,128)(2,1)S(1)}, bf16[256,256]{1,0:T(8,128)(2,1)S(1)}, u32[]{:S(2)}, u32[]{:S(2)}) collective-permute-start(bf16[256,256]{1,0:T(8,128)(2,1)S(1)} %constant_dynamic-update-slice_fusion), channel_id=1, source_target_pairs={{0,80},{8,88},{16,96},{24,104},{32,112},{40,120},{48,128},{56,136}... | collective-permute-start | bytes 393224 | tf_op jit(solution)/shard_map/ppermute | solution.py:103
  36.3 1.9 %collective-permute-start.8 = (bf16[256,256]{1,0:T(8,128)(2,1)S(1)}, bf16[256,256]{1,0:T(8,128)(2,1)S(1)}, u32[]{:S(2)}, u32[]{:S(2)}) collective-permute-start(bf16[256,256]{1,0:T(8,128)(2,1)S(1)} %constant_dynamic-update-slice_fusion), channel_id=1, source_target_pairs={{0,72},{8,80},{16,88},{24,96},{32,104},{40,112},{48,120},{56,128},... | collective-permute-start | bytes 393224 | tf_op jit(solution)/shard_map/ppermute | solution.py:103
  38.2 16.4 %collective-permute-done.4 = bf16[256,256]{1,0:T(8,128)(2,1)S(1)} collective-permute-done((bf16[256,256]{1,0:T(8,128)(2,1)S(1)}, bf16[256,256]{1,0:T(8,128)(2,1)S(1)}, u32[]{:S(2)}, u32[]{:S(2)}) %collective-permute-start.4) | collective-permute-done | bytes 131104 | tf_op jit(solution)/shard_map/ppermute | solution.py:103
  54.6 1.9 %collective-permute-start.9 = (bf16[256,256]{1,0:T(8,128)(2,1)S(1)}, bf16[256,256]{1,0:T(8,128)(2,1)S(1)}, u32[]{:S(2)}, u32[]{:S(2)}) collective-permute-start(bf16[256,256]{1,0:T(8,128)(2,1)S(1)} %constant_dynamic-update-slice_fusion), channel_id=1, source_target_pairs={{0,64},{8,72},{16,80},{24,88},{32,96},{40,104},{48,112},{56,120},{... | collective-permute-start | bytes 393224 | tf_op jit(solution)/shard_map/ppermute | solution.py:103
  56.6 3.2 %collective-permute-done.5 = bf16[256,256]{1,0:T(8,128)(2,1)S(1)} collective-permute-done((bf16[256,256]{1,0:T(8,128)(2,1)S(1)}, bf16[256,256]{1,0:T(8,128)(2,1)S(1)}, u32[]{:S(2)}, u32[]{:S(2)}) %collective-permute-start.5) | collective-permute-done | bytes 131104 | tf_op jit(solution)/shard_map/ppermute | solution.py:103
  59.7 1.9 %collective-permute-start.10 = (bf16[256,256]{1,0:T(8,128)(2,1)S(1)}, bf16[256,256]{1,0:T(8,128)(2,1)S(1)}, u32[]{:S(2)}, u32[]{:S(2)}) collective-permute-start(bf16[256,256]{1,0:T(8,128)(2,1)S(1)} %constant_dynamic-update-slice_fusion), channel_id=1, source_target_pairs={{0,56},{8,64},{16,72},{24,80},{32,88},{40,96},{48,104},{56,112},{6... | collective-permute-start | bytes 393224 | tf_op jit(solution)/shard_map/ppermute | solution.py:103
  61.7 6.5 %collective-permute-start.11 = (bf16[256,256]{1,0:T(8,128)(2,1)S(1)}, bf16[256,256]{1,0:T(8,128)(2,1)S(1)}, u32[]{:S(2)}, u32[]{:S(2)}) collective-permute-start(bf16[256,256]{1,0:T(8,128)(2,1)S(1)} %constant_dynamic-update-slice_fusion), channel_id=1, source_target_pairs={{0,48},{8,56},{16,64},{24,72},{32,80},{40,88},{48,96},{56,104},{64... | collective-permute-start | bytes 393224 | tf_op jit(solution)/shard_map/ppermute | solution.py:103
  68.2 11.5 %collective-permute-start.12 = (bf16[256,256]{1,0:T(8,128)(2,1)S(1)}, bf16[256,256]{1,0:T(8,128)(2,1)S(1)}, u32[]{:S(2)}, u32[]{:S(2)}) collective-permute-start(bf16[256,256]{1,0:T(8,128)(2,1)S(1)} %constant_dynamic-update-slice_fusion), channel_id=1, source_target_pairs={{0,40},{8,48},{16,56},{24,64},{32,72},{40,80},{48,88},{56,96},{64,... | collective-permute-start | bytes 393224 | tf_op jit(solution)/shard_map/ppermute | solution.py:103
  79.7 1.9 %collective-permute-start.13 = (bf16[256,256]{1,0:T(8,128)(2,1)S(1)}, bf16[256,256]{1,0:T(8,128)(2,1)S(1)}, u32[]{:S(2)}, u32[]{:S(2)}) collective-permute-start(bf16[256,256]{1,0:T(8,128)(2,1)S(1)} %constant_dynamic-update-slice_fusion), channel_id=1, source_target_pairs={{0,32},{8,40},{16,48},{24,56},{32,64},{40,72},{48,80},{56,88},{64,... | collective-permute-start | bytes 393224 | tf_op jit(solution)/shard_map/ppermute | solution.py:103
  81.7 3.3 %collective-permute-done.9 = bf16[256,256]{1,0:T(8,128)(2,1)S(1)} collective-permute-done((bf16[256,256]{1,0:T(8,128)(2,1)S(1)}, bf16[256,256]{1,0:T(8,128)(2,1)S(1)}, u32[]{:S(2)}, u32[]{:S(2)}) %collective-permute-start.9) | collective-permute-done | bytes 131104 | tf_op jit(solution)/shard_map/ppermute | solution.py:103
  85.0 1.9 %collective-permute-start.14 = (bf16[256,256]{1,0:T(8,128)(2,1)S(1)}, bf16[256,256]{1,0:T(8,128)(2,1)S(1)}, u32[]{:S(2)}, u32[]{:S(2)}) collective-permute-start(bf16[256,256]{1,0:T(8,128)(2,1)S(1)} %constant_dynamic-update-slice_fusion), channel_id=1, source_target_pairs={{0,24},{8,32},{16,40},{24,48},{32,56},{40,64},{48,72},{56,80},{64,... | collective-permute-start | bytes 393224 | tf_op jit(solution)/shard_map/ppermute | solution.py:103
  87.4 1.9 %collective-permute-start.15 = (bf16[256,256]{1,0:T(8,128)(2,1)S(1)}, bf16[256,256]{1,0:T(8,128)(2,1)S(1)}, u32[]{:S(2)}, u32[]{:S(2)}) collective-permute-start(bf16[256,256]{1,0:T(8,128)(2,1)S(1)} %constant_dynamic-update-slice_fusion), channel_id=1, source_target_pairs={{0,16},{8,24},{16,32},{24,40},{32,48},{40,56},{48,64},{56,72},{64,... | collective-permute-start | bytes 393224 | tf_op jit(solution)/shard_map/ppermute | solution.py:103
  89.4 4.6 %collective-permute-start.16 = (bf16[256,256]{1,0:T(8,128)(2,1)S(1)}, bf16[256,256]{1,0:T(8,128)(2,1)S(1)}, u32[]{:S(2)}, u32[]{:S(2)}) collective-permute-start(bf16[256,256]{1,0:T(8,128)(2,1)S(1)} %constant_dynamic-update-slice_fusion), channel_id=1, source_target_pairs={{0,8},{8,16},{16,24},{24,32},{32,40},{40,48},{48,56},{56,64},{64,7... | collective-permute-start | bytes 393224 | tf_op jit(solution)/shard_map/ppermute | solution.py:103
  94.1 4.8 %collective-permute-done.14 = bf16[256,256]{1,0:T(8,128)(2,1)S(1)} collective-permute-done((bf16[256,256]{1,0:T(8,128)(2,1)S(1)}, bf16[256,256]{1,0:T(8,128)(2,1)S(1)}, u32[]{:S(2)}, u32[]{:S(2)}) %collective-permute-start.14) | collective-permute-done | bytes 131104 | tf_op jit(solution)/shard_map/ppermute | solution.py:103
  98.9 3.0 %collective-permute-done.15 = bf16[256,256]{1,0:T(8,128)(2,1)S(1)} collective-permute-done((bf16[256,256]{1,0:T(8,128)(2,1)S(1)}, bf16[256,256]{1,0:T(8,128)(2,1)S(1)}, u32[]{:S(2)}, u32[]{:S(2)}) %collective-permute-start.15) | collective-permute-done | bytes 131104 | tf_op jit(solution)/shard_map/ppermute | solution.py:103
  102.0 1.4 copy-done
  103.4 48.0 %shard_map.64 = bf16[2048,128]{1,0:T(8,128)(2,1)} custom-call(s32[8,2]{1,0:T(8,128)} %copy.25.tiles_ref, bf16[2048,128]{1,0:T(8,128)(2,1)} %reshape.135.q_ref, bf16[4608,256]{1,0:T(8,128)(2,1)} %copy-done, s32[2048,1]{1,0:T(8,128)} %sub.60.qpos_ref, s32[2048,1]{1,0:T(8,128)} %sub.61.lo_ref), custom_call_target="tpu_custom_call" | custom-call | tf_op jit(solution)/shard_map/pallas_call | solution.py:62
  151.4 1.3 reshape.136
  152.7 5.7 %convolution_convert_fusion = bf16[256,4096]{1,0:T(8,128)(2,1)S(1)} fusion(bf16[256,1024]{1,0:T(8,128)(2,1)S(1)} %reshape.136, bf16[1024,4096]{1,0:T(8,128)(2,1)} %param.13), kind=kOutput, calls=%fused_computation | convolution fusion | flops 2148532224 | bytes 11010048 | tf_op jit(solution)/shard_map/dot_general | solution.py:114
  158.6 28.8 %all_to_all.5 = bf16[8,256,512]{2,1,0:T(8,128)(2,1)S(1)} all-to-all(bf16[8,256,512]{2,1,0:T(8,128)(2,1)S(1)} %bitcast.18), channel_id=1, replica_groups=mesh['ctx'=32,'head'=8] {'head'}, dimensions={0} | all-to-all | bytes 4194304 | tf_op jit(solution)/shard_map/all_to_all | solution.py:118
  (60 shorter events, 8.3 us)
Async XLA Ops:
  0.0 14.2 %copy-start.1 = (bf16[256,1024]{1,0:T(8,128)(2,1)S(1)}, bf16[256,1024]{1,0:T(8,128)(2,1)}, u32[]{:S(2)}) copy-start(bf16[256,1024]{1,0:T(8,128)(2,1)} %param.8) | copy-start | bytes 1572868
  1.8 17.8 %collective-permute-start = (bf16[256,256]{1,0:T(8,128)(2,1)S(1)}, bf16[256,256]{1,0:T(8,128)(2,1)S(1)}, u32[]{:S(2)}, u32[]{:S(2)}) collective-permute-start(bf16[256,256]{1,0:T(8,128)(2,1)S(1)} %constant_dynamic-update-slice_fusion), channel_id=1, source_target_pairs={{0,136},{8,144},{16,152},{24,160},{32,168},{40,176},{48,184},{56,1... | collective-permute-start | bytes 393224 | tf_op jit(solution)/shard_map/ppermute | solution.py:103
  3.1 20.4 %collective-permute-start.1 = (bf16[256,256]{1,0:T(8,128)(2,1)S(1)}, bf16[256,256]{1,0:T(8,128)(2,1)S(1)}, u32[]{:S(2)}, u32[]{:S(2)}) collective-permute-start(bf16[256,256]{1,0:T(8,128)(2,1)S(1)} %constant_dynamic-update-slice_fusion), channel_id=1, source_target_pairs={{0,128},{8,136},{16,144},{24,152},{32,160},{40,168},{48,176},{56,1... | collective-permute-start | bytes 393224 | tf_op jit(solution)/shard_map/ppermute | solution.py:103
  4.4 29.7 %collective-permute-start.2 = (bf16[256,256]{1,0:T(8,128)(2,1)S(1)}, bf16[256,256]{1,0:T(8,128)(2,1)S(1)}, u32[]{:S(2)}, u32[]{:S(2)}) collective-permute-start(bf16[256,256]{1,0:T(8,128)(2,1)S(1)} %constant_dynamic-update-slice_fusion), channel_id=1, source_target_pairs={{0,120},{8,128},{16,136},{24,144},{32,152},{40,160},{48,168},{56,1... | collective-permute-start | bytes 393224 | tf_op jit(solution)/shard_map/ppermute | solution.py:103
  5.7 30.6 %collective-permute-start.3 = (bf16[256,256]{1,0:T(8,128)(2,1)S(1)}, bf16[256,256]{1,0:T(8,128)(2,1)S(1)}, u32[]{:S(2)}, u32[]{:S(2)}) collective-permute-start(bf16[256,256]{1,0:T(8,128)(2,1)S(1)} %constant_dynamic-update-slice_fusion), channel_id=1, source_target_pairs={{0,112},{8,120},{16,128},{24,136},{32,144},{40,152},{48,160},{56,1... | collective-permute-start | bytes 393224 | tf_op jit(solution)/shard_map/ppermute | solution.py:103
  7.0 47.7 %collective-permute-start.4 = (bf16[256,256]{1,0:T(8,128)(2,1)S(1)}, bf16[256,256]{1,0:T(8,128)(2,1)S(1)}, u32[]{:S(2)}, u32[]{:S(2)}) collective-permute-start(bf16[256,256]{1,0:T(8,128)(2,1)S(1)} %constant_dynamic-update-slice_fusion), channel_id=1, source_target_pairs={{0,104},{8,112},{16,120},{24,128},{32,136},{40,144},{48,152},{56,1... | collective-permute-start | bytes 393224 | tf_op jit(solution)/shard_map/ppermute | solution.py:103
  15.2 86.7 %copy-start.2 = (bf16[256,128]{1,0:T(8,128)(2,1)S(1)}, bf16[256,128]{1,0:T(8,128)(2,1)}, u32[]{:S(2)}) copy-start(bf16[256,128]{1,0:T(8,128)(2,1)} %param.9) | copy-start | bytes 196612
  15.2 86.8 %copy-start.3 = (bf16[256,128]{1,0:T(8,128)(2,1)S(1)}, bf16[256,128]{1,0:T(8,128)(2,1)}, u32[]{:S(2)}) copy-start(bf16[256,128]{1,0:T(8,128)(2,1)} %param.10) | copy-start | bytes 196612
  19.6 40.1 %collective-permute-start.5 = (bf16[256,256]{1,0:T(8,128)(2,1)S(1)}, bf16[256,256]{1,0:T(8,128)(2,1)S(1)}, u32[]{:S(2)}, u32[]{:S(2)}) collective-permute-start(bf16[256,256]{1,0:T(8,128)(2,1)S(1)} %constant_dynamic-update-slice_fusion), channel_id=1, source_target_pairs={{0,96},{8,104},{16,112},{24,120},{32,128},{40,136},{48,144},{56,15... | collective-permute-start | bytes 393224 | tf_op jit(solution)/shard_map/ppermute | solution.py:103
  23.5 38.2 %collective-permute-start.6 = (bf16[256,256]{1,0:T(8,128)(2,1)S(1)}, bf16[256,256]{1,0:T(8,128)(2,1)S(1)}, u32[]{:S(2)}, u32[]{:S(2)}) collective-permute-start(bf16[256,256]{1,0:T(8,128)(2,1)S(1)} %constant_dynamic-update-slice_fusion), channel_id=1, source_target_pairs={{0,88},{8,96},{16,104},{24,112},{32,120},{40,128},{48,136},{56,144... | collective-permute-start | bytes 393224 | tf_op jit(solution)/shard_map/ppermute | solution.py:103
  34.1 34.1 %collective-permute-start.7 = (bf16[256,256]{1,0:T(8,128)(2,1)S(1)}, bf16[256,256]{1,0:T(8,128)(2,1)S(1)}, u32[]{:S(2)}, u32[]{:S(2)}) collective-permute-start(bf16[256,256]{1,0:T(8,128)(2,1)S(1)} %constant_dynamic-update-slice_fusion), channel_id=1, source_target_pairs={{0,80},{8,88},{16,96},{24,104},{32,112},{40,120},{48,128},{56,136}... | collective-permute-start | bytes 393224 | tf_op jit(solution)/shard_map/ppermute | solution.py:103
  36.3 43.4 %collective-permute-start.8 = (bf16[256,256]{1,0:T(8,128)(2,1)S(1)}, bf16[256,256]{1,0:T(8,128)(2,1)S(1)}, u32[]{:S(2)}, u32[]{:S(2)}) collective-permute-start(bf16[256,256]{1,0:T(8,128)(2,1)S(1)} %constant_dynamic-update-slice_fusion), channel_id=1, source_target_pairs={{0,72},{8,80},{16,88},{24,96},{32,104},{40,112},{48,120},{56,128},... | collective-permute-start | bytes 393224 | tf_op jit(solution)/shard_map/ppermute | solution.py:103
  54.6 30.3 %collective-permute-start.9 = (bf16[256,256]{1,0:T(8,128)(2,1)S(1)}, bf16[256,256]{1,0:T(8,128)(2,1)S(1)}, u32[]{:S(2)}, u32[]{:S(2)}) collective-permute-start(bf16[256,256]{1,0:T(8,128)(2,1)S(1)} %constant_dynamic-update-slice_fusion), channel_id=1, source_target_pairs={{0,64},{8,72},{16,80},{24,88},{32,96},{40,104},{48,112},{56,120},{... | collective-permute-start | bytes 393224 | tf_op jit(solution)/shard_map/ppermute | solution.py:103
  59.7 27.7 %collective-permute-start.10 = (bf16[256,256]{1,0:T(8,128)(2,1)S(1)}, bf16[256,256]{1,0:T(8,128)(2,1)S(1)}, u32[]{:S(2)}, u32[]{:S(2)}) collective-permute-start(bf16[256,256]{1,0:T(8,128)(2,1)S(1)} %constant_dynamic-update-slice_fusion), channel_id=1, source_target_pairs={{0,56},{8,64},{16,72},{24,80},{32,88},{40,96},{48,104},{56,112},{6... | collective-permute-start | bytes 393224 | tf_op jit(solution)/shard_map/ppermute | solution.py:103
  61.7 27.7 %collective-permute-start.11 = (bf16[256,256]{1,0:T(8,128)(2,1)S(1)}, bf16[256,256]{1,0:T(8,128)(2,1)S(1)}, u32[]{:S(2)}, u32[]{:S(2)}) collective-permute-start(bf16[256,256]{1,0:T(8,128)(2,1)S(1)} %constant_dynamic-update-slice_fusion), channel_id=1, source_target_pairs={{0,48},{8,56},{16,64},{24,72},{32,80},{40,88},{48,96},{56,104},{64... | collective-permute-start | bytes 393224 | tf_op jit(solution)/shard_map/ppermute | solution.py:103
  68.2 25.9 %collective-permute-start.12 = (bf16[256,256]{1,0:T(8,128)(2,1)S(1)}, bf16[256,256]{1,0:T(8,128)(2,1)S(1)}, u32[]{:S(2)}, u32[]{:S(2)}) collective-permute-start(bf16[256,256]{1,0:T(8,128)(2,1)S(1)} %constant_dynamic-update-slice_fusion), channel_id=1, source_target_pairs={{0,40},{8,48},{16,56},{24,64},{32,72},{40,80},{48,88},{56,96},{64,... | collective-permute-start | bytes 393224 | tf_op jit(solution)/shard_map/ppermute | solution.py:103
  79.7 14.4 %collective-permute-start.13 = (bf16[256,256]{1,0:T(8,128)(2,1)S(1)}, bf16[256,256]{1,0:T(8,128)(2,1)S(1)}, u32[]{:S(2)}, u32[]{:S(2)}) collective-permute-start(bf16[256,256]{1,0:T(8,128)(2,1)S(1)} %constant_dynamic-update-slice_fusion), channel_id=1, source_target_pairs={{0,32},{8,40},{16,48},{24,56},{32,64},{40,72},{48,80},{56,88},{64,... | collective-permute-start | bytes 393224 | tf_op jit(solution)/shard_map/ppermute | solution.py:103
  85.0 14.0 %collective-permute-start.14 = (bf16[256,256]{1,0:T(8,128)(2,1)S(1)}, bf16[256,256]{1,0:T(8,128)(2,1)S(1)}, u32[]{:S(2)}, u32[]{:S(2)}) collective-permute-start(bf16[256,256]{1,0:T(8,128)(2,1)S(1)} %constant_dynamic-update-slice_fusion), channel_id=1, source_target_pairs={{0,24},{8,32},{16,40},{24,48},{32,56},{40,64},{48,72},{56,80},{64,... | collective-permute-start | bytes 393224 | tf_op jit(solution)/shard_map/ppermute | solution.py:103
  87.4 14.5 %collective-permute-start.15 = (bf16[256,256]{1,0:T(8,128)(2,1)S(1)}, bf16[256,256]{1,0:T(8,128)(2,1)S(1)}, u32[]{:S(2)}, u32[]{:S(2)}) collective-permute-start(bf16[256,256]{1,0:T(8,128)(2,1)S(1)} %constant_dynamic-update-slice_fusion), channel_id=1, source_target_pairs={{0,16},{8,24},{16,32},{24,40},{32,48},{40,56},{48,64},{56,72},{64,... | collective-permute-start | bytes 393224 | tf_op jit(solution)/shard_map/ppermute | solution.py:103
  89.4 12.5 %collective-permute-start.16 = (bf16[256,256]{1,0:T(8,128)(2,1)S(1)}, bf16[256,256]{1,0:T(8,128)(2,1)S(1)}, u32[]{:S(2)}, u32[]{:S(2)}) collective-permute-start(bf16[256,256]{1,0:T(8,128)(2,1)S(1)} %constant_dynamic-update-slice_fusion), channel_id=1, source_target_pairs={{0,8},{8,16},{16,24},{24,32},{32,40},{40,48},{48,56},{56,64},{64,7... | collective-permute-start | bytes 393224 | tf_op jit(solution)/shard_map/ppermute | solution.py:103
  102.0 1.4 copy-start

commit v3 on v1

--- a/solution.py
+++ b/solution.py
@@ -27,28 +27,40 @@
         l_sc[...] = jnp.zeros(l_sc.shape, jnp.float32)
         acc_sc[...] = jnp.zeros(acc_sc.shape, jnp.float32)
 
-        def k_body(kj, c):
+        def k_step(kj, masked):
             c0 = pl.multiple_of(kj * TK, TK)
             k = kv_ref[pl.ds(c0, TK), pl.ds(0, HD)]
             v = kv_ref[pl.ds(c0, TK), pl.ds(HD, HD)]
             s = lax.dot_general(
                 q, k, (((1,), (1,)), ((), ())), preferred_element_type=jnp.float32
             ) * scale
-            kpos = c0 + lax.broadcasted_iota(jnp.int32, (TQ, TK), 1)
-            ok = (kpos >= lo) & (kpos <= qpos)
-            s = jnp.where(ok, s, NEG_FILL)
+            if masked:
+                kpos = c0 + lax.broadcasted_iota(jnp.int32, (TQ, TK), 1)
+                ok = (kpos >= lo) & (kpos <= qpos)
+                s = jnp.where(ok, s, NEG_FILL)
             m_prev = m_sc[...]
             m_new = jnp.maximum(m_prev, jnp.max(s, axis=1, keepdims=True))
-            p = jnp.where(ok, jnp.exp(s - m_new), 0.0)
+            p = jnp.exp(s - m_new)
+            if masked:
+                p = jnp.where(ok, p, 0.0)
             fade = jnp.exp(m_prev - m_new)
             l_sc[...] = l_sc[...] * fade + jnp.sum(p, axis=1, keepdims=True)
             acc_sc[...] = acc_sc[...] * fade + jnp.dot(
                 p.astype(jnp.bfloat16), v, preferred_element_type=jnp.float32
             )
             m_sc[...] = m_new
+
+        def masked_body(kj, c):
+            k_step(kj, True)
             return c
 
-        lax.fori_loop(tiles_ref[qi, 0], tiles_ref[qi, 1], k_body, 0)
+        def open_body(kj, c):
+            k_step(kj, False)
+            return c
+
+        lax.fori_loop(tiles_ref[qi, 0], tiles_ref[qi, 1], masked_body, 0)
+        lax.fori_loop(tiles_ref[qi, 1], tiles_ref[qi, 2], open_body, 0)
+        lax.fori_loop(tiles_ref[qi, 2], tiles_ref[qi, 3], masked_body, 0)
         o_ref[pl.ds(r0, TQ), :] = (acc_sc[...] / l_sc[...]).astype(o_ref.dtype)
         return carry
 
@@ -92,16 +104,25 @@
     tok_per_tile = TQ // group_size
     tile_lo = jnp.min(lo_tok.reshape(-1, tok_per_tile), axis=1)
     tile_hi = pos.reshape(-1, tok_per_tile)[:, -1]
-    tiles = jnp.stack([tile_lo // TK, tile_hi // TK + 1], axis=1).astype(jnp.int32)
+    tile_lo_max = jnp.max(lo_tok.reshape(-1, tok_per_tile), axis=1)
+    tile_hi_min = pos.reshape(-1, tok_per_tile)[:, 0]
 
     kv_local = jnp.concatenate([key_rows, values], axis=1)
     kv_all = lax.all_gather(kv_local, "ctx", axis=0, tiled=True)
+    t0 = tile_lo // TK
+    t3 = tile_hi // TK + 1
+    t1 = jnp.clip((tile_lo_max + TK - 1) // TK, t0, t3)
+    t2 = jnp.clip((tile_hi_min + 1) // TK, t1, t3)
+    tiles = jnp.stack([t0, t1, t2, t3], axis=1).astype(jnp.int32)
     q_rows = queries.reshape(row_count * group_size, HD)
     att = attend(q_rows, kv_all, qpos_rows, lo_rows, tiles).reshape(row_count, query_width)
 
     partial_value = jnp.dot(att, out_weight, preferred_element_type=jnp.float32).astype(jnp.bfloat16)
-    summed = lax.psum_scatter(partial_value, "head", scatter_dimension=1, tiled=True)
-    return summed.astype(jnp.float32).astype(jnp.bfloat16)
+    n_head = lax.axis_size("head")
+    cols = partial_value.shape[1] // n_head
+    parts = partial_value.reshape(row_count, n_head, cols).transpose(1, 0, 2)
+    got = lax.all_to_all(parts, "head", split_axis=0, concat_axis=0, tiled=True)
+    return jnp.sum(got.astype(jnp.float32), axis=0).astype(jnp.bfloat16)
 
 
 def solution(mesh):

time: 221 us -> 188 us (0.85); the launches traced: 218 us -> 187 us
  waiting for transfers between devices: 138 us -> 79 us
  blocking collectives: 0 us -> 27.3 us
    reduce_scatter x1 -> x0, waiting for transfers between devices: 58.4 us -> none  [on_device(): lax.psum_scatter(partial_value, 'head', scatter_dimension=1, tiled=True)]
    all_to_all x0 -> x1, blocking collectives: none -> 27.3 us  [on_device(): got = lax.all_to_all(parts, 'head', split_axis=0, concat_axis=0, tiled=True)]
  transfers between devices with their start and end apart: 2 -> 1, of which waited for: 2 -> 1; matrix products, arithmetic and copies ran while one was open for 4% -> 4% of each run, Pallas kernels for 0% -> 0%
where the time goes in v3:
time: 188 us; the launch traced here: 187 us
  waiting for transfers between devices  79 us (42%)
  Pallas kernels  49.7 us (26%)
  blocking collectives  27.3 us (15%)
  between operations  13.5 us (7%)
  local copies, waits for them, and re-layouts  7.73 us (4%)
  matrix products  5.72 us (3%)
  other arithmetic  4.53 us (2%)
    all_gather x1, waiting for transfers between devices, on_device(): kv_all = lax.all_gather(kv_local, 'ctx', axis=0, tiled=True)  79 us
    pallas_call x1, Pallas kernels, attend(): pl.pallas_call(attn_kernel, out_shape=jax.ShapeDtypeStruct((rows, HD), jn...  49.7 us
    all_to_all x1, blocking collectives, on_device(): got = lax.all_to_all(parts, 'head', split_axis=0, concat_axis=0, tiled=True)  27.3 us
    dot_general x1, matrix products, on_device(): jnp.dot(att, out_weight, preferred_element_type=jnp.float32)  5.72 us
  transfers between devices with their start and end apart: 1, of which 1 were waited for; matrix products, arithmetic and copies ran while one was open for 4% of the time, Pallas kernels for 0%

profile of v3, /device:TPU:192, one launch (start us, length us, event | category | flops | bytes accessed | tf_op | source)
XLA Modules:
  0.0 187.4 jit_solution(11492897845371047000)
XLA Ops:
  6.5 0.0 all-gather.2.cloned.1.call-start
  6.5 1.5 pad_maximum_fusion
  8.1 0.0 all-gather.2.cloned.1.call-update
  8.1 0.8 dynamic-slice_multiply_fusion
  8.9 0.1 mul.27
  9.0 0.1 broadcast_in_dim.24
  9.0 0.1 mul.28
  9.1 0.8 copy.39
  9.9 0.1 reduce.1
  10.0 0.1 select_reduce_fusion
  10.1 0.1 reduce_max.21
  10.2 0.2 maximum_reduce_fusion.1
  10.4 0.1 copy.44
  10.4 0.1 copy.40
  10.5 0.1 broadcast_in_dim.27
  10.6 0.1 mul.30
  10.7 2.1 %reshape.167.q_ref = bf16[2048,128]{1,0:T(8,128)(2,1)} reshape(bf16[256,1024]{1,0:T(8,128)(2,1)} %param.8) | data formatting | bytes 1048576 | tf_op jit(solution)/shard_map/reshape | solution.py:117
  12.8 0.1 broadcast_in_dim.26
  12.9 1.3 broadcast_in_dim_reshape.8.qpos_ref
  14.2 0.1 broadcast_in_dim.28
  14.3 1.3 broadcast_in_dim_reshape.9.lo_ref
  15.6 0.1 fusion.8
  15.7 0.7 pad_add_fusion.tiles_ref
  16.4 79.0 %all-gather.2.cloned.1.call-done.kv_ref = bf16[8192,256]{1,0:T(8,128)(2,1)} async-done(((bf16[256,256]{1,0:T(8,128)(2,1)}), bf16[8192,256]{1,0:T(8,128)(2,1)}) %all-gather.2.cloned.1.call-update) | async-done | bytes 4194320 | tf_op jit(solution)/shard_map/all_gather | solution.py:111
  95.3 49.7 %shard_map.64 = bf16[2048,128]{1,0:T(8,128)(2,1)} custom-call(s32[8,4]{1,0:T(8,128)} %pad_add_fusion.tiles_ref, bf16[2048,128]{1,0:T(8,128)(2,1)} %reshape.167.q_ref, bf16[8192,256]{1,0:T(8,128)(2,1)} %all-gather.2.cloned.1.call-done.kv_ref, s32[2048,1]{1,0:T(8,128)} %broadcast_in_dim_reshape.8.qpos_ref, s32[2048,1]{1,0:T(8,128)} %broadcast_in_dim_reshape.9.lo_ref), custom_call_target="tpu_custom_call" | custom-call | tf_op jit(solution)/shard_map/pallas_call | solution.py:73
  145.1 1.3 reshape.168
  146.3 5.7 %convolution_convert_fusion = bf16[256,4096]{1,0:T(8,128)(2,1)S(1)} fusion(bf16[256,1024]{1,0:T(8,128)(2,1)S(1)} %reshape.168, bf16[1024,4096]{1,0:T(8,128)(2,1)} %param.13), kind=kOutput, calls=%fused_computation | convolution fusion | flops 2148532224 | bytes 11010048 | tf_op jit(solution)/shard_map/dot_general | solution.py:120
  152.1 0.2 copy.53
  152.3 27.3 %all_to_all.5 = bf16[8,256,512]{2,1,0:T(8,128)(2,1)S(1)} all-to-all(bf16[8,256,512]{2,1,0:T(8,128)(2,1)S(1)} %bitcast.13), channel_id=1, replica_groups=mesh['ctx'=32,'head'=8] {'head'}, dimensions={0} | all-to-all | bytes 4194304 | tf_op jit(solution)/shard_map/all_to_all | solution.py:124
  179.5 1.0 reduce_sum.12
  (5 shorter events, 0.1 us)
Async XLA Ops:
  6.5 88.8 %all-gather.2.cloned.1.call-start = ((), (), s32[]{:S(2)}) async-start(), calls=%async_computation.1 | async-start | bytes 4325376 | tf_op jit(solution)/shard_map/all_gather | solution.py:111
Sparse Core Ops, SparseCore 0:
  10.1 85.1 all-gather.1

commit v4 on v3

--- a/solution.py
+++ b/solution.py
@@ -12,6 +12,7 @@
 TQ = 256
 TK = 512
 NEG_FILL = -1e30
+LONGEST = 4352
 
 
 def attn_kernel(tiles_ref, q_ref, kv_ref, qpos_ref, lo_ref, o_ref, m_sc, l_sc, acc_sc):
@@ -89,6 +90,131 @@
     )(tiles, q_rows, kv_all, qpos_rows, lo_rows)
 
 
+MESH_ID = pl.DeviceIdType.MESH
+
+
+def window_kernel(reach, n_ctx, kv_ref, zero_ref, win_ref, send_sem, recv_sem, local_sem):
+    del zero_ref
+    me = lax.axis_index("ctx")
+    h = lax.axis_index("head")
+    rows = kv_ref.shape[0]
+    barrier = pltpu.get_barrier_semaphore()
+    for d in range(1, reach + 1):
+        @pl.when(me + d < n_ctx)
+        def _():
+            pl.semaphore_signal(barrier, 1, device_id=(me + d, h), device_id_type=MESH_ID)
+
+        @pl.when(me - d >= 0)
+        def _():
+            pl.semaphore_signal(barrier, 1, device_id=(me - d, h), device_id_type=MESH_ID)
+
+    pl.semaphore_wait(barrier, jnp.minimum(reach, n_ctx - 1 - me) + jnp.minimum(reach, me))
+    local = pltpu.make_async_copy(kv_ref, win_ref.at[pl.ds(reach * rows, rows)], local_sem)
+    local.start()
+
+    def push(d):
+        return pltpu.make_async_remote_copy(
+            src_ref=kv_ref,
+            dst_ref=win_ref.at[pl.ds((reach - d) * rows, rows)],
+            send_sem=send_sem.at[d - 1],
+            recv_sem=recv_sem.at[d - 1],
+            device_id=(me + d, h),
+            device_id_type=MESH_ID,
+        )
+
+    for d in range(1, reach + 1):
+        @pl.when(me + d < n_ctx)
+        def _():
+            push(d).start()
+
+    for d in range(1, reach + 1):
+        @pl.when(me + d < n_ctx)
+        def _():
+            push(d).wait_send()
+
+        @pl.when(me - d >= 0)
+        def _():
+            push(d).wait_recv()
+
+    local.wait()
+
+
+def gather_window(kv_local, reach, n_ctx):
+    rows, width = kv_local.shape
+    zero = jnp.zeros(((reach + 1) * rows, width), kv_local.dtype)
+    return pl.pallas_call(
+        functools.partial(window_kernel, reach, n_ctx),
+        out_shape=jax.ShapeDtypeStruct(zero.shape, zero.dtype),
+        in_specs=[pl.BlockSpec(memory_space=pl.ANY), pl.BlockSpec(memory_space=pl.ANY)],
+        out_specs=pl.BlockSpec(memory_space=pl.ANY),
+        scratch_shapes=[
+            pltpu.SemaphoreType.DMA((reach,)),
+            pltpu.SemaphoreType.DMA((reach,)),
+            pltpu.SemaphoreType.DMA(()),
+        ],
+        input_output_aliases={1: 0},
+        compiler_params=pltpu.CompilerParams(collective_id=0, has_side_effects=True),
+    )(kv_local, zero)
+
+
+def swap_kernel(n_head, parts_ref, got_ref, send_sem, recv_sem, local_sem):
+    me = lax.axis_index("head")
+    row = lax.axis_index("ctx")
+    barrier = pltpu.get_barrier_semaphore()
+    for d in range(1, n_head):
+        pl.semaphore_signal(
+            barrier, 1, device_id=(row, lax.rem(me + d, n_head)), device_id_type=MESH_ID
+        )
+    pl.semaphore_wait(barrier, n_head - 1)
+    local = pltpu.make_async_copy(parts_ref.at[me], got_ref.at[me], local_sem)
+    local.start()
+
+    def send(d):
+        dst = lax.rem(me + d, n_head)
+        return pltpu.make_async_remote_copy(
+            src_ref=parts_ref.at[dst],
+            dst_ref=got_ref.at[me],
+            send_sem=send_sem.at[d - 1],
+            recv_sem=recv_sem.at[d - 1],
+            device_id=(row, dst),
+            device_id_type=MESH_ID,
+        )
+
+    def arrival(d):
+        src = lax.rem(me + n_head - d, n_head)
+        return pltpu.make_async_remote_copy(
+            src_ref=parts_ref.at[src],
+            dst_ref=got_ref.at[src],
+            send_sem=send_sem.at[d - 1],
+            recv_sem=recv_sem.at[d - 1],
+            device_id=(row, src),
+            device_id_type=MESH_ID,
+        )
+
+    for d in range(1, n_head):
+        send(d).start()
+    for d in range(1, n_head):
+        send(d).wait_send()
+        arrival(d).wait_recv()
+    local.wait()
+
+
+def swap_parts(parts):
+    n_head = parts.shape[0]
+    return pl.pallas_call(
+        functools.partial(swap_kernel, n_head),
+        out_shape=jax.ShapeDtypeStruct(parts.shape, parts.dtype),
+        in_specs=[pl.BlockSpec(memory_space=pl.ANY)],
+        out_specs=pl.BlockSpec(memory_space=pl.ANY),
+        scratch_shapes=[
+            pltpu.SemaphoreType.DMA((n_head - 1,)),
+            pltpu.SemaphoreType.DMA((n_head - 1,)),
+            pltpu.SemaphoreType.DMA(()),
+        ],
+        compiler_params=pltpu.CompilerParams(collective_id=1, has_side_effects=True),
+    )(parts)
+
+
 def on_device(queries, key_rows, values, lengths, block_plan, inverse, mask_lo, out_weight):
     row_count, query_width = queries.shape
     group_size = query_width // HD
@@ -108,20 +234,24 @@
     tile_hi_min = pos.reshape(-1, tok_per_tile)[:, 0]
 
     kv_local = jnp.concatenate([key_rows, values], axis=1)
-    kv_all = lax.all_gather(kv_local, "ctx", axis=0, tiled=True)
-    t0 = tile_lo // TK
-    t3 = tile_hi // TK + 1
-    t1 = jnp.clip((tile_lo_max + TK - 1) // TK, t0, t3)
-    t2 = jnp.clip((tile_hi_min + 1) // TK, t1, t3)
+    n_ctx = lax.axis_size("ctx")
+    reach = min(n_ctx - 1, -(-(LONGEST - 1) // row_count))
+    kv_win = gather_window(kv_local, reach, n_ctx)
+    base = first - reach * row_count
+    span = kv_win.shape[0]
+    t0 = (tile_lo - base) // TK
+    t3 = jnp.minimum((tile_hi - base) // TK + 1, span // TK)
+    t1 = jnp.clip((tile_lo_max - base + TK - 1) // TK, t0, t3)
+    t2 = jnp.clip((tile_hi_min - base + 1) // TK, t1, t3)
     tiles = jnp.stack([t0, t1, t2, t3], axis=1).astype(jnp.int32)
     q_rows = queries.reshape(row_count * group_size, HD)
-    att = attend(q_rows, kv_all, qpos_rows, lo_rows, tiles).reshape(row_count, query_width)
+    att = attend(q_rows, kv_win, qpos_rows - base, lo_rows - base, tiles).reshape(row_count, query_width)
 
     partial_value = jnp.dot(att, out_weight, preferred_element_type=jnp.float32).astype(jnp.bfloat16)
     n_head = lax.axis_size("head")
     cols = partial_value.shape[1] // n_head
     parts = partial_value.reshape(row_count, n_head, cols).transpose(1, 0, 2)
-    got = lax.all_to_all(parts, "head", split_axis=0, concat_axis=0, tiled=True)
+    got = swap_parts(parts)
     return jnp.sum(got.astype(jnp.float32), axis=0).astype(jnp.bfloat16)
 
 

time: 188 us -> 185 us (0.984)
  the two profiles are of different devices: /device:TPU:192 before, /device:TPU:69 now
where the time goes in v4:
time: 185 us
  Pallas kernels  157 us (85%)
  local copies, waits for them, and re-layouts  14.7 us (8%)
  matrix products  7.07 us (4%)
  other arithmetic  6.15 us (3%)
    pallas_call x1, Pallas kernels, gather_window(): pl.pallas_call(functools.partial(window_kernel, reach, n_ctx), out_shape=...  96.3 us
    pallas_call x1, Pallas kernels, attend(): pl.pallas_call(attn_kernel, out_shape=jax.ShapeDtypeStruct((rows, HD), jn...  34.7 us
    pallas_call x1, Pallas kernels, swap_parts(): pl.pallas_call(functools.partial(swap_kernel, n_head), out_shape=jax.Shap...  26.1 us
    dot_general x1, matrix products, on_device(): jnp.dot(att, out_weight, preferred_element_type=jnp.float32)  7.07 us

profile of v4, /device:TPU:69, one launch (start us, length us, event | category | flops | bytes accessed | tf_op | source)
XLA Modules:
  0.0 185.1 jit_solution(4874500565493922357)
XLA Ops:
  0.0 0.8 dynamic-slice_multiply_fusion
  0.8 0.1 mul.27
  0.8 0.1 broadcast_in_dim.27
  0.9 0.1 mul.28
  1.0 0.8 copy.30
  1.8 0.1 reduce.1
  1.9 0.1 select_reduce_fusion
  2.0 0.1 reduce_max.21
  2.1 0.2 maximum_reduce_fusion.1
  2.3 0.1 copy.35
  2.3 0.1 copy.31
  2.4 0.1 fusion.9
  2.5 0.7 pad_add_fusion.tiles_ref
  3.2 2.1 %reshape.205.q_ref = bf16[2048,128]{1,0:T(8,128)(2,1)} reshape(bf16[256,1024]{1,0:T(8,128)(2,1)} %param.8) | data formatting | bytes 1048576 | tf_op jit(solution)/shard_map/reshape | solution.py:247
  5.3 1.5 pad_maximum_fusion.kv_ref
  6.8 1.6 broadcast_in_dim.29.zero_ref
  8.4 96.3 %shard_map.64.kv_ref = bf16[4608,256]{1,0:T(8,128)(2,1)} custom-call(bf16[256,256]{1,0:T(8,128)(2,1)} %pad_maximum_fusion.kv_ref, bf16[4608,256]{1,0:T(8,128)(2,1)} %broadcast_in_dim.29.zero_ref), custom_call_target="tpu_custom_call", output_to_operand_aliasing={{}: (1, {})} | custom-call | tf_op jit(solution)/shard_map/pallas_call | solution.py:145
  104.6 0.1 broadcast_in_dim.30
  104.7 1.3 sub.102.qpos_ref
  106.0 0.1 broadcast_in_dim.31
  106.1 0.1 mul.30
  106.2 0.1 broadcast_in_dim.32
  106.3 1.3 sub.103.lo_ref
  107.6 34.7 %shard_map.65 = bf16[2048,128]{1,0:T(8,128)(2,1)} custom-call(s32[8,4]{1,0:T(8,128)} %pad_add_fusion.tiles_ref, bf16[2048,128]{1,0:T(8,128)(2,1)} %reshape.205.q_ref, bf16[4608,256]{1,0:T(8,128)(2,1)} %shard_map.64.kv_ref, s32[2048,1]{1,0:T(8,128)} %sub.102.qpos_ref, s32[2048,1]{1,0:T(8,128)} %sub.103.lo_ref), custom_call_target="tpu_custom_call" | custom-call | tf_op jit(solution)/shard_map/pallas_call | solution.py:74
  142.3 1.3 reshape.206
  143.6 7.1 %convolution_convert_fusion = bf16[256,4096]{1,0:T(8,128)(2,1)} fusion(bf16[256,1024]{1,0:T(8,128)(2,1)S(1)} %reshape.206, bf16[1024,4096]{1,0:T(8,128)(2,1)} %param.13), kind=kOutput, calls=%fused_computation | convolution fusion | flops 2148532224 | bytes 11010048 | tf_op jit(solution)/shard_map/dot_general | solution.py:250
  150.6 3.3 %copy.41 = bf16[256,4096]{0,1:T(8,128)(2,1)S(1)} copy(bf16[256,4096]{1,0:T(8,128)(2,1)} %convolution_convert_fusion) | data formatting | bytes 4194304 | tf_op jit(solution)/shard_map/convert_element_type | solution.py:250
  153.9 2.4 %copy.42 = bf16[256,8,512]{2,0,1:T(8,128)(2,1)} copy(bf16[256,8,512]{0,2,1:T(8,128)(2,1)S(1)} %bitcast.9) | data formatting | bytes 4194304 | tf_op jit(solution)/shard_map/reshape | solution.py:253
  156.3 26.1 %shard_map.66 = bf16[8,256,512]{2,1,0:T(8,128)(2,1)} custom-call(bf16[8,256,512]{2,1,0:T(8,128)(2,1)} %bitcast.10), custom_call_target="tpu_custom_call" | custom-call | tf_op jit(solution)/shard_map/pallas_call | solution.py:204
  182.4 2.7 %reduce_sum.12 = bf16[256,512]{1,0:T(8,128)(2,1)} reduce(bf16[8,256,512]{2,1,0:T(8,128)(2,1)} %shard_map.66, bf16[]{:T(256)} %constant.71.clone.1), dimensions={0}, to_apply=%region_4.5 | reduce | flops 917504 | bytes 2359298 | tf_op jit(solution)/shard_map/reduce_sum | solution.py:255
  (6 shorter events, 0.1 us)

commit v5 on v4

--- a/solution.py
+++ b/solution.py
@@ -10,12 +10,13 @@
 HD = 128
 BLK = 8
 TQ = 256
-TK = 512
+TK = 256
 NEG_FILL = -1e30
 LONGEST = 4352
-
-
-def attn_kernel(tiles_ref, q_ref, kv_ref, qpos_ref, lo_ref, o_ref, m_sc, l_sc, acc_sc):
+PLANE = 4
+
+
+def attn_kernel(plane, slots, tiles_ref, q_ref, kv_ref, qpos_ref, lo_ref, o_ref, m_sc, l_sc, acc_sc):
     n_q = q_ref.shape[0] // TQ
     scale = HD ** (-0.5)
 
@@ -30,8 +31,9 @@
 
         def k_step(kj, masked):
             c0 = pl.multiple_of(kj * TK, TK)
-            k = kv_ref[pl.ds(c0, TK), pl.ds(0, HD)]
-            v = kv_ref[pl.ds(c0, TK), pl.ds(HD, HD)]
+            at = pl.multiple_of((lax.rem(kj, plane) * slots + kj // plane) * TK, TK)
+            k = kv_ref[pl.ds(at, TK), pl.ds(0, HD)]
+            v = kv_ref[pl.ds(at, TK), pl.ds(HD, HD)]
             s = lax.dot_general(
                 q, k, (((1,), (1,)), ((), ())), preferred_element_type=jnp.float32
             ) * scale
@@ -68,11 +70,11 @@
     lax.fori_loop(0, n_q, q_body, 0)
 
 
-def attend(q_rows, kv_all, qpos_rows, lo_rows, tiles):
+def attend(q_rows, kv_all, qpos_rows, lo_rows, tiles, plane, slots):
     rows = q_rows.shape[0]
     vmem = pltpu.MemorySpace.VMEM if hasattr(pltpu, "MemorySpace") else pltpu.VMEM
     return pl.pallas_call(
-        attn_kernel,
+        functools.partial(attn_kernel, plane, slots),
         out_shape=jax.ShapeDtypeStruct((rows, HD), jnp.bfloat16),
         in_specs=[
             pl.BlockSpec(memory_space=pltpu.SMEM),
@@ -93,63 +95,88 @@
 MESH_ID = pl.DeviceIdType.MESH
 
 
-def window_kernel(reach, n_ctx, kv_ref, zero_ref, win_ref, send_sem, recv_sem, local_sem):
+def window_kernel(depth, plane, n_ctx, kv_ref, zero_ref, win_ref, send1, recv1, send2, recv2, local_sem):
     del zero_ref
     me = lax.axis_index("ctx")
     h = lax.axis_index("head")
-    rows = kv_ref.shape[0]
+    z = me // plane
+    r = me % plane
+    n_z = n_ctx // plane
     barrier = pltpu.get_barrier_semaphore()
-    for d in range(1, reach + 1):
-        @pl.when(me + d < n_ctx)
-        def _():
-            pl.semaphore_signal(barrier, 1, device_id=(me + d, h), device_id_type=MESH_ID)
-
-        @pl.when(me - d >= 0)
-        def _():
-            pl.semaphore_signal(barrier, 1, device_id=(me - d, h), device_id_type=MESH_ID)
-
-    pl.semaphore_wait(barrier, jnp.minimum(reach, n_ctx - 1 - me) + jnp.minimum(reach, me))
-    local = pltpu.make_async_copy(kv_ref, win_ref.at[pl.ds(reach * rows, rows)], local_sem)
+    for d in range(1, depth + 1):
+        @pl.when(z + d < n_z)
+        def _():
+            pl.semaphore_signal(barrier, 1, device_id=(me + d * plane, h), device_id_type=MESH_ID)
+
+        @pl.when(z - d >= 0)
+        def _():
+            pl.semaphore_signal(barrier, 1, device_id=(me - d * plane, h), device_id_type=MESH_ID)
+
+    for e in range(1, plane):
+        peer = z * plane + lax.rem(r + e, plane)
+        pl.semaphore_signal(barrier, 1, device_id=(peer, h), device_id_type=MESH_ID)
+    pl.semaphore_wait(
+        barrier, jnp.minimum(depth, n_z - 1 - z) + jnp.minimum(depth, z) + (plane - 1)
+    )
+    local = pltpu.make_async_copy(kv_ref, win_ref.at[r, depth], local_sem)
     local.start()
 
-    def push(d):
+    def down(d):
         return pltpu.make_async_remote_copy(
             src_ref=kv_ref,
-            dst_ref=win_ref.at[pl.ds((reach - d) * rows, rows)],
-            send_sem=send_sem.at[d - 1],
-            recv_sem=recv_sem.at[d - 1],
-            device_id=(me + d, h),
+            dst_ref=win_ref.at[r, depth - d],
+            send_sem=send1.at[d - 1],
+            recv_sem=recv1.at[d - 1],
+            device_id=(me + d * plane, h),
             device_id_type=MESH_ID,
         )
 
-    for d in range(1, reach + 1):
-        @pl.when(me + d < n_ctx)
-        def _():
-            push(d).start()
-
-    for d in range(1, reach + 1):
-        @pl.when(me + d < n_ctx)
-        def _():
-            push(d).wait_send()
-
-        @pl.when(me - d >= 0)
-        def _():
-            push(d).wait_recv()
+    for d in range(1, depth + 1):
+        @pl.when(z + d < n_z)
+        def _():
+            down(d).start()
+
+    for d in range(1, depth + 1):
+        @pl.when(z + d < n_z)
+        def _():
+            down(d).wait_send()
+
+        @pl.when(z - d >= 0)
+        def _():
+            down(d).wait_recv()
 
     local.wait()
 
-
-def gather_window(kv_local, reach, n_ctx):
+    def across(e, col):
+        return pltpu.make_async_remote_copy(
+            src_ref=win_ref.at[col],
+            dst_ref=win_ref.at[col],
+            send_sem=send2.at[e - 1],
+            recv_sem=recv2.at[e - 1],
+            device_id=(z * plane + lax.rem(r + e, plane), h),
+            device_id_type=MESH_ID,
+        )
+
+    for e in range(1, plane):
+        across(e, r).start()
+    for e in range(1, plane):
+        across(e, r).wait_send()
+        across(e, lax.rem(r + plane - e, plane)).wait_recv()
+
+
+def gather_window(kv_local, depth, plane, n_ctx):
     rows, width = kv_local.shape
-    zero = jnp.zeros(((reach + 1) * rows, width), kv_local.dtype)
+    zero = jnp.zeros((plane, depth + 1, rows, width), kv_local.dtype)
     return pl.pallas_call(
-        functools.partial(window_kernel, reach, n_ctx),
+        functools.partial(window_kernel, depth, plane, n_ctx),
         out_shape=jax.ShapeDtypeStruct(zero.shape, zero.dtype),
         in_specs=[pl.BlockSpec(memory_space=pl.ANY), pl.BlockSpec(memory_space=pl.ANY)],
         out_specs=pl.BlockSpec(memory_space=pl.ANY),
         scratch_shapes=[
-            pltpu.SemaphoreType.DMA((reach,)),
-            pltpu.SemaphoreType.DMA((reach,)),
+            pltpu.SemaphoreType.DMA((depth,)),
+            pltpu.SemaphoreType.DMA((depth,)),
+            pltpu.SemaphoreType.DMA((plane - 1,)),
+            pltpu.SemaphoreType.DMA((plane - 1,)),
             pltpu.SemaphoreType.DMA(()),
         ],
         input_output_aliases={1: 0},
@@ -235,9 +262,11 @@
 
     kv_local = jnp.concatenate([key_rows, values], axis=1)
     n_ctx = lax.axis_size("ctx")
-    reach = min(n_ctx - 1, -(-(LONGEST - 1) // row_count))
-    kv_win = gather_window(kv_local, reach, n_ctx)
-    base = first - reach * row_count
+    plane = PLANE
+    depth = min(n_ctx // plane - 1, -(-(LONGEST - 1) // (plane * row_count)))
+    kv_win = gather_window(kv_local, depth, plane, n_ctx)
+    kv_win = kv_win.reshape(-1, kv_win.shape[-1])
+    base = (here // plane - depth) * plane * row_count
     span = kv_win.shape[0]
     t0 = (tile_lo - base) // TK
     t3 = jnp.minimum((tile_hi - base) // TK + 1, span // TK)
@@ -245,7 +274,7 @@
     t2 = jnp.clip((tile_hi_min - base + 1) // TK, t1, t3)
     tiles = jnp.stack([t0, t1, t2, t3], axis=1).astype(jnp.int32)
     q_rows = queries.reshape(row_count * group_size, HD)
-    att = attend(q_rows, kv_win, qpos_rows - base, lo_rows - base, tiles).reshape(row_count, query_width)
+    att = attend(q_rows, kv_win, qpos_rows - base, lo_rows - base, tiles, plane, depth + 1).reshape(row_count, query_width)
 
     partial_value = jnp.dot(att, out_weight, preferred_element_type=jnp.float32).astype(jnp.bfloat16)
     n_head = lax.axis_size("head")

time: 185 us -> 194 us (1.049)
  the two profiles are of different devices: /device:TPU:69 before, /device:TPU:199 now
where the time goes in v5:
time: 194 us; the launch traced here: 193 us
  Pallas kernels  165 us (85%)
  local copies, waits for them, and re-layouts  15.2 us (8%)
  matrix products  7.07 us (4%)
  other arithmetic  6.15 us (3%)
    pallas_call x1, Pallas kernels, attend(): pl.pallas_call(functools.partial(attn_kernel, plane, slots), out_shape=ja...  76.7 us
    pallas_call x1, Pallas kernels, gather_window(): pl.pallas_call(functools.partial(window_kernel, depth, plane, n_ctx), out...  64.5 us
    pallas_call x1, Pallas kernels, swap_parts(): pl.pallas_call(functools.partial(swap_kernel, n_head), out_shape=jax.Shap...  23.6 us
    dot_general x1, matrix products, on_device(): jnp.dot(att, out_weight, preferred_element_type=jnp.float32)  7.07 us

profile of v5, /device:TPU:199, one launch (start us, length us, event | category | flops | bytes accessed | tf_op | source)
XLA Modules:
  0.0 193.3 jit_solution(14660407233977819089)
XLA Ops:
  0.0 0.8 dynamic-slice_multiply_fusion
  0.8 0.1 mul.31
  0.8 0.1 broadcast_in_dim.27
  0.9 0.1 mul.32
  1.0 0.8 copy.30
  1.8 0.1 reduce.1
  1.9 0.1 select_reduce_fusion
  2.0 0.1 reduce_max.21
  2.1 0.2 maximum_reduce_fusion.1
  2.3 0.1 copy.35
  2.3 0.1 copy.31
  2.4 0.1 fusion.9
  2.5 0.7 pad_add_fusion.tiles_ref
  3.2 2.1 %reshape.208.q_ref = bf16[2048,128]{1,0:T(8,128)(2,1)} reshape(bf16[256,1024]{1,0:T(8,128)(2,1)} %param.8) | data formatting | bytes 1048576 | tf_op jit(solution)/shard_map/reshape | solution.py:276
  5.3 1.5 pad_maximum_fusion.kv_ref
  6.8 2.0 %broadcast_in_dim.29.zero_ref = bf16[4,6,256,256]{3,2,1,0:T(8,128)(2,1)} broadcast(bf16[]{:T(256)} %constant.84.clone.1), dimensions={} | broadcast | bytes 3145730 | tf_op jit(solution)/shard_map/broadcast_in_dim | solution.py:169
  8.8 64.5 %shard_map.64 = bf16[4,6,256,256]{3,2,1,0:T(8,128)(2,1)} custom-call(bf16[256,256]{1,0:T(8,128)(2,1)} %pad_maximum_fusion.kv_ref, bf16[4,6,256,256]{3,2,1,0:T(8,128)(2,1)} %broadcast_in_dim.29.zero_ref), custom_call_target="tpu_custom_call", output_to_operand_aliasing={{}: (1, {})} | custom-call | tf_op jit(solution)/shard_map/pallas_call | solution.py:170
  73.3 0.1 broadcast_in_dim.30
  73.4 1.3 sub.107.qpos_ref
  74.7 0.1 broadcast_in_dim.31
  74.8 0.1 mul.35
  74.9 0.1 broadcast_in_dim.32
  75.0 1.3 sub.108.lo_ref
  76.3 76.7 %shard_map.65 = bf16[2048,128]{1,0:T(8,128)(2,1)} custom-call(s32[8,4]{1,0:T(8,128)} %pad_add_fusion.tiles_ref, bf16[2048,128]{1,0:T(8,128)(2,1)} %reshape.208.q_ref, bf16[6144,256]{1,0:T(8,128)(2,1)} %bitcast.10, s32[2048,1]{1,0:T(8,128)} %sub.107.qpos_ref, s32[2048,1]{1,0:T(8,128)} %sub.108.lo_ref), custom_call_target="tpu_custom_call" | custom-call | tf_op jit(solution)/shard_map/pallas_call | solution.py:76
  153.0 1.3 reshape.210
  154.3 7.1 %convolution_convert_fusion = bf16[256,4096]{1,0:T(8,128)(2,1)} fusion(bf16[256,1024]{1,0:T(8,128)(2,1)S(1)} %reshape.210, bf16[1024,4096]{1,0:T(8,128)(2,1)} %param.13), kind=kOutput, calls=%fused_computation | convolution fusion | flops 2148532224 | bytes 11010048 | tf_op jit(solution)/shard_map/dot_general | solution.py:279
  161.4 3.3 %copy.41 = bf16[256,4096]{0,1:T(8,128)(2,1)S(1)} copy(bf16[256,4096]{1,0:T(8,128)(2,1)} %convolution_convert_fusion) | data formatting | bytes 4194304 | tf_op jit(solution)/shard_map/convert_element_type | solution.py:279
  164.6 2.4 %copy.42 = bf16[256,8,512]{2,0,1:T(8,128)(2,1)} copy(bf16[256,8,512]{0,2,1:T(8,128)(2,1)S(1)} %bitcast.11) | data formatting | bytes 4194304 | tf_op jit(solution)/shard_map/reshape | solution.py:282
  167.0 23.6 %shard_map.66 = bf16[8,256,512]{2,1,0:T(8,128)(2,1)} custom-call(bf16[8,256,512]{2,1,0:T(8,128)(2,1)} %bitcast.12), custom_call_target="tpu_custom_call" | custom-call | tf_op jit(solution)/shard_map/pallas_call | solution.py:231
  190.7 2.7 %reduce_sum.12 = bf16[256,512]{1,0:T(8,128)(2,1)} reduce(bf16[8,256,512]{2,1,0:T(8,128)(2,1)} %shard_map.66, bf16[]{:T(256)} %constant.84.clone.1), dimensions={0}, to_apply=%region_4.5 | reduce | flops 917504 | bytes 2359298 | tf_op jit(solution)/shard_map/reduce_sum | solution.py:284
  (6 shorter events, 0.1 us)

commit v6 on v5

--- a/solution.py
+++ b/solution.py
@@ -9,47 +9,47 @@
 
 HD = 128
 BLK = 8
-TQ = 256
-TK = 256
+TQ = 1024
+TK = 512
 NEG_FILL = -1e30
 LONGEST = 4352
 PLANE = 4
 
 
-def attn_kernel(plane, slots, tiles_ref, q_ref, kv_ref, qpos_ref, lo_ref, o_ref, m_sc, l_sc, acc_sc):
+def attn_kernel(tiles_ref, q_ref, kv_ref, qpos_ref, lo_ref, o_ref, m_sc, l_sc, acc_sc):
     n_q = q_ref.shape[0] // TQ
     scale = HD ** (-0.5)
 
     def q_body(qi, carry):
         r0 = pl.multiple_of(qi * TQ, TQ)
         q = q_ref[pl.ds(r0, TQ), :]
-        qpos = qpos_ref[pl.ds(r0, TQ), :]
-        lo = lo_ref[pl.ds(r0, TQ), :]
+        qpos = qpos_ref[:, pl.ds(r0, TQ)]
+        lo = lo_ref[:, pl.ds(r0, TQ)]
         m_sc[...] = jnp.full(m_sc.shape, NEG_FILL, jnp.float32)
         l_sc[...] = jnp.zeros(l_sc.shape, jnp.float32)
         acc_sc[...] = jnp.zeros(acc_sc.shape, jnp.float32)
 
         def k_step(kj, masked):
             c0 = pl.multiple_of(kj * TK, TK)
-            at = pl.multiple_of((lax.rem(kj, plane) * slots + kj // plane) * TK, TK)
-            k = kv_ref[pl.ds(at, TK), pl.ds(0, HD)]
-            v = kv_ref[pl.ds(at, TK), pl.ds(HD, HD)]
+            k = kv_ref[pl.ds(c0, TK), pl.ds(0, HD)]
+            v = kv_ref[pl.ds(c0, TK), pl.ds(HD, HD)]
             s = lax.dot_general(
-                q, k, (((1,), (1,)), ((), ())), preferred_element_type=jnp.float32
+                k, q, (((1,), (1,)), ((), ())), preferred_element_type=jnp.float32
             ) * scale
             if masked:
-                kpos = c0 + lax.broadcasted_iota(jnp.int32, (TQ, TK), 1)
+                kpos = c0 + lax.broadcasted_iota(jnp.int32, (TK, TQ), 0)
                 ok = (kpos >= lo) & (kpos <= qpos)
                 s = jnp.where(ok, s, NEG_FILL)
             m_prev = m_sc[...]
-            m_new = jnp.maximum(m_prev, jnp.max(s, axis=1, keepdims=True))
+            m_new = jnp.maximum(m_prev, jnp.max(s, axis=0, keepdims=True))
             p = jnp.exp(s - m_new)
             if masked:
                 p = jnp.where(ok, p, 0.0)
             fade = jnp.exp(m_prev - m_new)
-            l_sc[...] = l_sc[...] * fade + jnp.sum(p, axis=1, keepdims=True)
-            acc_sc[...] = acc_sc[...] * fade + jnp.dot(
-                p.astype(jnp.bfloat16), v, preferred_element_type=jnp.float32
+            l_sc[...] = l_sc[...] * fade + jnp.sum(p, axis=0, keepdims=True)
+            acc_sc[...] = acc_sc[...] * fade + lax.dot_general(
+                v, p.astype(jnp.bfloat16), (((0,), (0,)), ((), ())),
+                preferred_element_type=jnp.float32,
             )
             m_sc[...] = m_new
 
@@ -64,17 +64,17 @@
         lax.fori_loop(tiles_ref[qi, 0], tiles_ref[qi, 1], masked_body, 0)
         lax.fori_loop(tiles_ref[qi, 1], tiles_ref[qi, 2], open_body, 0)
         lax.fori_loop(tiles_ref[qi, 2], tiles_ref[qi, 3], masked_body, 0)
-        o_ref[pl.ds(r0, TQ), :] = (acc_sc[...] / l_sc[...]).astype(o_ref.dtype)
+        o_ref[pl.ds(r0, TQ), :] = (acc_sc[...] / l_sc[...]).T.astype(o_ref.dtype)
         return carry
 
     lax.fori_loop(0, n_q, q_body, 0)
 
 
-def attend(q_rows, kv_all, qpos_rows, lo_rows, tiles, plane, slots):
+def attend(q_rows, kv_all, qpos_rows, lo_rows, tiles):
     rows = q_rows.shape[0]
     vmem = pltpu.MemorySpace.VMEM if hasattr(pltpu, "MemorySpace") else pltpu.VMEM
     return pl.pallas_call(
-        functools.partial(attn_kernel, plane, slots),
+        attn_kernel,
         out_shape=jax.ShapeDtypeStruct((rows, HD), jnp.bfloat16),
         in_specs=[
             pl.BlockSpec(memory_space=pltpu.SMEM),
@@ -85,9 +85,9 @@
         ],
         out_specs=pl.BlockSpec(memory_space=vmem),
         scratch_shapes=[
-            pltpu.VMEM((TQ, 1), jnp.float32),
-            pltpu.VMEM((TQ, 1), jnp.float32),
-            pltpu.VMEM((TQ, HD), jnp.float32),
+            pltpu.VMEM((1, TQ), jnp.float32),
+            pltpu.VMEM((1, TQ), jnp.float32),
+            pltpu.VMEM((HD, TQ), jnp.float32),
         ],
     )(tiles, q_rows, kv_all, qpos_rows, lo_rows)
 
@@ -252,8 +252,8 @@
     doc_start = jnp.max(jnp.where(doc_ends[None, :] <= pos[:, None], doc_ends[None, :], 0), axis=1)
     block_lo = lax.dynamic_slice_in_dim(mask_lo, here * (row_count // BLK), row_count // BLK)
     lo_tok = jnp.maximum(jnp.repeat(block_lo, BLK) * BLK, doc_start)
-    qpos_rows = jnp.repeat(pos, group_size)[:, None]
-    lo_rows = jnp.repeat(lo_tok, group_size)[:, None]
+    qpos_rows = jnp.repeat(pos, group_size)[None, :]
+    lo_rows = jnp.repeat(lo_tok, group_size)[None, :]
     tok_per_tile = TQ // group_size
     tile_lo = jnp.min(lo_tok.reshape(-1, tok_per_tile), axis=1)
     tile_hi = pos.reshape(-1, tok_per_tile)[:, -1]
@@ -265,7 +265,7 @@
     plane = PLANE
     depth = min(n_ctx // plane - 1, -(-(LONGEST - 1) // (plane * row_count)))
     kv_win = gather_window(kv_local, depth, plane, n_ctx)
-    kv_win = kv_win.reshape(-1, kv_win.shape[-1])
+    kv_win = kv_win.transpose(1, 0, 2, 3).reshape(-1, kv_win.shape[-1])
     base = (here // plane - depth) * plane * row_count
     span = kv_win.shape[0]
     t0 = (tile_lo - base) // TK
@@ -274,7 +274,7 @@
     t2 = jnp.clip((tile_hi_min - base + 1) // TK, t1, t3)
     tiles = jnp.stack([t0, t1, t2, t3], axis=1).astype(jnp.int32)
     q_rows = queries.reshape(row_count * group_size, HD)
-    att = attend(q_rows, kv_win, qpos_rows - base, lo_rows - base, tiles, plane, depth + 1).reshape(row_count, query_width)
+    att = attend(q_rows, kv_win, qpos_rows - base, lo_rows - base, tiles).reshape(row_count, query_width)
 
     partial_value = jnp.dot(att, out_weight, preferred_element_type=jnp.float32).astype(jnp.bfloat16)
     n_head = lax.axis_size("head")

time: 194 us -> 149 us (0.77)
  the two profiles are of different devices: /device:TPU:199 before, /device:TPU:192 now
where the time goes in v6:
time: 149 us; the launch traced here: 146 us
  Pallas kernels  116 us (78%)
  local copies, waits for them, and re-layouts  16.9 us (11%)
  matrix products  7.07 us (5%)
  other arithmetic  6.13 us (4%)
    pallas_call x1, Pallas kernels, gather_window(): pl.pallas_call(functools.partial(window_kernel, depth, plane, n_ctx), out...  62.7 us
    pallas_call x1, Pallas kernels, swap_parts(): pl.pallas_call(functools.partial(swap_kernel, n_head), out_shape=jax.Shap...  29.8 us
    pallas_call x1, Pallas kernels, attend(): pl.pallas_call(attn_kernel, out_shape=jax.ShapeDtypeStruct((rows, HD), jn...  23.9 us
    dot_general x1, matrix products, on_device(): jnp.dot(att, out_weight, preferred_element_type=jnp.float32)  7.07 us
    transpose x1, local copies, waits for them, and re-layouts, on_device(): kv_win = kv_win.transpose(1, 0, 2, 3).reshape(-1, kv_win.shape[-1])  3.92 us
    convert_element_type x1, local copies, waits for them, and re-layouts, on_device(): jnp.dot(att, out_weight, preferred_element_type=jnp.float32)  3.27 us

profile of v6, /device:TPU:192, one launch (start us, length us, event | category | flops | bytes accessed | tf_op | source)
XLA Modules:
  0.0 146.5 jit_solution(9127254482210536752)
XLA Ops:
  0.0 0.7 copy.30
  0.8 0.1 reduce.1
  0.9 0.1 select_reduce_fusion
  1.0 0.8 dynamic-slice_multiply_fusion
  1.8 0.1 broadcast_in_dim.31
  1.8 0.1 mul.35
  1.9 0.1 broadcast_in_dim.32
  2.0 0.7 sub.106.lo_ref
  2.8 0.1 broadcast_in_dim.30
  2.8 0.7 sub.104.qpos_ref
  3.6 0.1 mul.31
  3.6 0.1 broadcast_in_dim.27
  3.7 0.1 mul.32
  3.8 0.2 fusion
  4.0 0.1 copy.31
  4.1 0.1 copy.35
  4.2 0.1 maximum_minimum_fusion
  4.3 0.7 pad_add_fusion.tiles_ref
  4.9 1.5 %pad_maximum_fusion.kv_ref = bf16[256,256]{1,0:T(8,128)(2,1)} fusion(bf16[256,128]{1,0:T(8,128)(2,1)} %param.10, bf16[256,128]{1,0:T(8,128)(2,1)} %param.9), kind=kLoop, calls=%fused_computation.1 | loop fusion | flops 262144 | bytes 262144 | tf_op jit(solution)/shard_map/concatenate | solution.py:263
  6.5 2.0 %broadcast_in_dim.29.zero_ref = bf16[4,6,256,256]{3,2,1,0:T(8,128)(2,1)} broadcast(bf16[]{:T(256)} %constant.87.clone.1), dimensions={} | broadcast | bytes 3145730 | tf_op jit(solution)/shard_map/broadcast_in_dim | solution.py:169
  8.5 62.7 %shard_map.64 = bf16[4,6,256,256]{3,2,1,0:T(8,128)(2,1)} custom-call(bf16[256,256]{1,0:T(8,128)(2,1)} %pad_maximum_fusion.kv_ref, bf16[4,6,256,256]{3,2,1,0:T(8,128)(2,1)} %broadcast_in_dim.29.zero_ref), custom_call_target="tpu_custom_call", output_to_operand_aliasing={{}: (1, {})} | custom-call | tf_op jit(solution)/shard_map/pallas_call | solution.py:170
  71.2 0.0 copy-start
  71.2 3.9 %copy.39 = bf16[6,4,256,256]{3,2,1,0:T(8,128)(2,1)} copy(bf16[6,4,256,256]{3,2,0,1:T(8,128)(2,1)} %bitcast.17) | data formatting | bytes 6291456 | tf_op jit(solution)/shard_map/transpose | solution.py:268
  75.1 0.0 copy-done
  75.1 1.0 reshape.208.q_ref
  76.1 23.9 %shard_map.65 = bf16[2048,128]{1,0:T(8,128)(2,1)} custom-call(s32[2,4]{1,0:T(2,128)} %pad_add_fusion.tiles_ref, bf16[2048,128]{1,0:T(8,128)(2,1)} %reshape.208.q_ref, bf16[6144,256]{1,0:T(8,128)(2,1)} %bitcast.18, s32[1,2048]{1,0:T(1,128)} %sub.104.qpos_ref, s32[1,2048]{1,0:T(1,128)} %sub.106.lo_ref), custom_call_target="tpu_custom_call" | custom-call | tf_op jit(solution)/shard_map/pallas_call | solution.py:76
  100.0 1.3 reshape.210
  101.3 7.1 %convolution_convert_fusion = bf16[256,4096]{1,0:T(8,128)(2,1)} fusion(bf16[256,1024]{1,0:T(8,128)(2,1)S(1)} %reshape.210, bf16[1024,4096]{1,0:T(8,128)(2,1)} %param.13), kind=kOutput, calls=%fused_computation | convolution fusion | flops 2148532224 | bytes 11010048 | tf_op jit(solution)/shard_map/dot_general | solution.py:279
  108.4 3.3 %copy.40 = bf16[256,4096]{0,1:T(8,128)(2,1)S(1)} copy(bf16[256,4096]{1,0:T(8,128)(2,1)} %convolution_convert_fusion) | data formatting | bytes 4194304 | tf_op jit(solution)/shard_map/convert_element_type | solution.py:279
  111.6 2.4 %copy.41 = bf16[256,8,512]{2,0,1:T(8,128)(2,1)} copy(bf16[256,8,512]{0,2,1:T(8,128)(2,1)S(1)} %bitcast.19) | data formatting | bytes 4194304 | tf_op jit(solution)/shard_map/reshape | solution.py:282
  114.0 29.8 %shard_map.66 = bf16[8,256,512]{2,1,0:T(8,128)(2,1)} custom-call(bf16[8,256,512]{2,1,0:T(8,128)(2,1)} %bitcast.20), custom_call_target="tpu_custom_call" | custom-call | tf_op jit(solution)/shard_map/pallas_call | solution.py:231
  143.8 2.7 %reduce_sum.12 = bf16[256,512]{1,0:T(8,128)(2,1)} reduce(bf16[8,256,512]{2,1,0:T(8,128)(2,1)} %shard_map.66, bf16[]{:T(256)} %constant.87.clone.1), dimensions={0}, to_apply=%region_4.5 | reduce | flops 917504 | bytes 2359298 | tf_op jit(solution)/shard_map/reduce_sum | solution.py:284
  (6 shorter events, 0.1 us)
Async XLA Ops:
  71.2 3.9 %copy-start = (bf16[256,1024]{1,0:T(8,128)(2,1)S(1)}, bf16[256,1024]{1,0:T(8,128)(2,1)}, u32[]{:S(2)}) copy-start(bf16[256,1024]{1,0:T(8,128)(2,1)} %param.8) | copy-start | bytes 1572868

commit v7 on v6

--- a/solution.py
+++ b/solution.py
@@ -136,6 +136,20 @@
         def _():
             down(d).start()
 
+    local.wait()
+
+    def across(e, col, slot):
+        return pltpu.make_async_remote_copy(
+            src_ref=win_ref.at[col, slot],
+            dst_ref=win_ref.at[col, slot],
+            send_sem=send2.at[e - 1, slot],
+            recv_sem=recv2.at[e - 1, slot],
+            device_id=(z * plane + lax.rem(r + e, plane), h),
+            device_id_type=MESH_ID,
+        )
+
+    for e in range(1, plane):
+        across(e, r, depth).start()
     for d in range(1, depth + 1):
         @pl.when(z + d < n_z)
         def _():
@@ -144,24 +158,15 @@
         @pl.when(z - d >= 0)
         def _():
             down(d).wait_recv()
-
-    local.wait()
-
-    def across(e, col):
-        return pltpu.make_async_remote_copy(
-            src_ref=win_ref.at[col],
-            dst_ref=win_ref.at[col],
-            send_sem=send2.at[e - 1],
-            recv_sem=recv2.at[e - 1],
-            device_id=(z * plane + lax.rem(r + e, plane), h),
-            device_id_type=MESH_ID,
-        )
-
-    for e in range(1, plane):
-        across(e, r).start()
-    for e in range(1, plane):
-        across(e, r).wait_send()
-        across(e, lax.rem(r + plane - e, plane)).wait_recv()
+            for e in range(1, plane):
+                across(e, r, depth - d).start()
+
+    for slot in range(depth + 1):
+        @pl.when(z - (depth - slot) >= 0)
+        def _():
+            for e in range(1, plane):
+                across(e, r, slot).wait_send()
+                across(e, lax.rem(r + plane - e, plane), slot).wait_recv()
 
 
 def gather_window(kv_local, depth, plane, n_ctx):
@@ -175,8 +180,8 @@
         scratch_shapes=[
             pltpu.SemaphoreType.DMA((depth,)),
             pltpu.SemaphoreType.DMA((depth,)),
-            pltpu.SemaphoreType.DMA((plane - 1,)),
-            pltpu.SemaphoreType.DMA((plane - 1,)),
+            pltpu.SemaphoreType.DMA((plane - 1, depth + 1)),
+            pltpu.SemaphoreType.DMA((plane - 1, depth + 1)),
             pltpu.SemaphoreType.DMA(()),
         ],
         input_output_aliases={1: 0},
@@ -184,8 +189,9 @@
     )(kv_local, zero)
 
 
-def swap_kernel(n_head, parts_ref, got_ref, send_sem, recv_sem, local_sem):
+def swap_kernel(n_head, partial_ref, got_ref, send_sem, recv_sem, local_sem):
     me = lax.axis_index("head")
+    cols = got_ref.shape[2]
     row = lax.axis_index("ctx")
     barrier = pltpu.get_barrier_semaphore()
     for d in range(1, n_head):
@@ -193,13 +199,15 @@
             barrier, 1, device_id=(row, lax.rem(me + d, n_head)), device_id_type=MESH_ID
         )
     pl.semaphore_wait(barrier, n_head - 1)
-    local = pltpu.make_async_copy(parts_ref.at[me], got_ref.at[me], local_sem)
+    local = pltpu.make_async_copy(
+        partial_ref.at[:, pl.ds(me * cols, cols)], got_ref.at[me], local_sem
+    )
     local.start()
 
     def send(d):
         dst = lax.rem(me + d, n_head)
         return pltpu.make_async_remote_copy(
-            src_ref=parts_ref.at[dst],
+            src_ref=partial_ref.at[:, pl.ds(dst * cols, cols)],
             dst_ref=got_ref.at[me],
             send_sem=send_sem.at[d - 1],
             recv_sem=recv_sem.at[d - 1],
@@ -210,7 +218,7 @@
     def arrival(d):
         src = lax.rem(me + n_head - d, n_head)
         return pltpu.make_async_remote_copy(
-            src_ref=parts_ref.at[src],
+            src_ref=partial_ref.at[:, pl.ds(src * cols, cols)],
             dst_ref=got_ref.at[src],
             send_sem=send_sem.at[d - 1],
             recv_sem=recv_sem.at[d - 1],
@@ -226,11 +234,11 @@
     local.wait()
 
 
-def swap_parts(parts):
-    n_head = parts.shape[0]
+def swap_parts(partial_value, n_head):
+    rows, width = partial_value.shape
     return pl.pallas_call(
         functools.partial(swap_kernel, n_head),
-        out_shape=jax.ShapeDtypeStruct(parts.shape, parts.dtype),
+        out_shape=jax.ShapeDtypeStruct((n_head, rows, width // n_head), partial_value.dtype),
         in_specs=[pl.BlockSpec(memory_space=pl.ANY)],
         out_specs=pl.BlockSpec(memory_space=pl.ANY),
         scratch_shapes=[
@@ -239,7 +247,7 @@
             pltpu.SemaphoreType.DMA(()),
         ],
         compiler_params=pltpu.CompilerParams(collective_id=1, has_side_effects=True),
-    )(parts)
+    )(partial_value)
 
 
 def on_device(queries, key_rows, values, lengths, block_plan, inverse, mask_lo, out_weight):
@@ -278,9 +286,7 @@
 
     partial_value = jnp.dot(att, out_weight, preferred_element_type=jnp.float32).astype(jnp.bfloat16)
     n_head = lax.axis_size("head")
-    cols = partial_value.shape[1] // n_head
-    parts = partial_value.reshape(row_count, n_head, cols).transpose(1, 0, 2)
-    got = swap_parts(parts)
+    got = swap_parts(partial_value, n_head)
     return jnp.sum(got.astype(jnp.float32), axis=0).astype(jnp.bfloat16)
 
 

time: 149 us -> 124 us (0.83); the launches traced: 146 us -> 123 us
  Pallas kernels: 116 us -> 98.6 us
  local copies, waits for them, and re-layouts: 16.9 us -> 11.2 us
    pallas_call x1, Pallas kernels: 62.7 us -> 43.1 us  [gather_window(): pl.pallas_call(functools.partial(window_kernel, depth, plane, n_ctx), out...]
    convert_element_type x1 -> x0, local copies, waits for them, and re-layouts: 3.27 us -> none  [on_device(): jnp.dot(att, out_weight, preferred_element_type=jnp.float32)]
    reshape x1 -> x0, local copies, waits for them, and re-layouts: 2.41 us -> none  [on_device(): parts = partial_value.reshape(row_count, n_head, cols).transpose(1, 0, 2)]
    pallas_call x1, Pallas kernels: 23.9 us -> 26.2 us  [attend(): pl.pallas_call(attn_kernel, out_shape=jax.ShapeDtypeStruct((rows, HD), jn...]
where the time goes in v7:
time: 124 us; the launch traced here: 123 us
  Pallas kernels  98.6 us (80%)
  local copies, waits for them, and re-layouts  11.2 us (9%)
  matrix products  7.07 us (6%)
  other arithmetic  6.13 us (5%)
    pallas_call x1, Pallas kernels, gather_window(): pl.pallas_call(functools.partial(window_kernel, depth, plane, n_ctx), out...  43.1 us
    pallas_call x1, Pallas kernels, swap_parts(): pl.pallas_call(functools.partial(swap_kernel, n_head), out_shape=jax.Shap...  29.2 us
    pallas_call x1, Pallas kernels, attend(): pl.pallas_call(attn_kernel, out_shape=jax.ShapeDtypeStruct((rows, HD), jn...  26.2 us
    dot_general x1, matrix products, on_device(): jnp.dot(att, out_weight, preferred_element_type=jnp.float32)  7.07 us
    transpose x1, local copies, waits for them, and re-layouts, on_device(): kv_win = kv_win.transpose(1, 0, 2, 3).reshape(-1, kv_win.shape[-1])  3.92 us
    reduce_sum x1, other arithmetic, on_device(): return jnp.sum(got.astype(jnp.float32), axis=0).astype(jnp.bfloat16)  2.66 us

profile of v7, /device:TPU:192, one launch (start us, length us, event | category | flops | bytes accessed | tf_op | source)
XLA Modules:
  0.0 123.0 jit_solution(3245955653269201665)
XLA Ops:
  0.0 0.7 copy.28
  0.8 0.1 reduce.1
  0.9 0.1 select_reduce_fusion
  1.0 0.8 dynamic-slice_multiply_fusion
  1.8 0.1 broadcast_in_dim.31
  1.8 0.1 mul.35
  1.9 0.1 broadcast_in_dim.32
  2.0 0.7 sub.106.lo_ref
  2.8 0.1 broadcast_in_dim.30
  2.8 0.7 sub.104.qpos_ref
  3.6 0.1 mul.31
  3.6 0.1 broadcast_in_dim.27
  3.7 0.1 mul.32
  3.8 0.2 fusion
  4.0 0.1 copy.29
  4.1 0.1 copy.33
  4.2 0.1 maximum_minimum_fusion
  4.3 0.7 pad_add_fusion.tiles_ref
  4.9 1.5 %pad_maximum_fusion.kv_ref = bf16[256,256]{1,0:T(8,128)(2,1)} fusion(bf16[256,128]{1,0:T(8,128)(2,1)} %param.10, bf16[256,128]{1,0:T(8,128)(2,1)} %param.9), kind=kLoop, calls=%fused_computation.1 | loop fusion | flops 262144 | bytes 262144 | tf_op jit(solution)/shard_map/concatenate | solution.py:271
  6.5 2.0 %broadcast_in_dim.29.zero_ref = bf16[4,6,256,256]{3,2,1,0:T(8,128)(2,1)} broadcast(bf16[]{:T(256)} %constant.87.clone.1), dimensions={} | broadcast | bytes 3145730 | tf_op jit(solution)/shard_map/broadcast_in_dim | solution.py:174
  8.5 43.1 %shard_map.64 = bf16[4,6,256,256]{3,2,1,0:T(8,128)(2,1)} custom-call(bf16[256,256]{1,0:T(8,128)(2,1)} %pad_maximum_fusion.kv_ref, bf16[4,6,256,256]{3,2,1,0:T(8,128)(2,1)} %broadcast_in_dim.29.zero_ref), custom_call_target="tpu_custom_call", output_to_operand_aliasing={{}: (1, {})} | custom-call | tf_op jit(solution)/shard_map/pallas_call | solution.py:175
  51.6 0.0 copy-start
  51.7 3.9 %copy.37 = bf16[6,4,256,256]{3,2,1,0:T(8,128)(2,1)} copy(bf16[6,4,256,256]{3,2,0,1:T(8,128)(2,1)} %bitcast.15) | data formatting | bytes 6291456 | tf_op jit(solution)/shard_map/transpose | solution.py:276
  55.6 0.0 copy-done
  55.6 1.0 reshape.205.q_ref
  56.6 26.2 %shard_map.65 = bf16[2048,128]{1,0:T(8,128)(2,1)} custom-call(s32[2,4]{1,0:T(2,128)} %pad_add_fusion.tiles_ref, bf16[2048,128]{1,0:T(8,128)(2,1)} %reshape.205.q_ref, bf16[6144,256]{1,0:T(8,128)(2,1)} %bitcast.16, s32[1,2048]{1,0:T(1,128)} %sub.104.qpos_ref, s32[1,2048]{1,0:T(1,128)} %sub.106.lo_ref), custom_call_target="tpu_custom_call" | custom-call | tf_op jit(solution)/shard_map/pallas_call | solution.py:76
  82.8 1.3 %reshape.207 = bf16[256,1024]{1,0:T(8,128)(2,1)S(1)} reshape(bf16[2048,128]{1,0:T(8,128)(2,1)} %shard_map.65) | data formatting | bytes 1048576 | tf_op jit(solution)/shard_map/reshape | solution.py:285
  84.1 7.1 %convolution_convert_fusion.partial_ref = bf16[256,4096]{1,0:T(8,128)(2,1)} fusion(bf16[256,1024]{1,0:T(8,128)(2,1)S(1)} %reshape.207, bf16[1024,4096]{1,0:T(8,128)(2,1)} %param.13), kind=kOutput, calls=%fused_computation | convolution fusion | flops 2148532224 | bytes 11010048 | tf_op jit(solution)/shard_map/dot_general | solution.py:287
  91.1 29.2 %shard_map.66 = bf16[8,256,512]{2,1,0:T(8,128)(2,1)} custom-call(bf16[256,4096]{1,0:T(8,128)(2,1)} %convolution_convert_fusion.partial_ref), custom_call_target="tpu_custom_call" | custom-call | tf_op jit(solution)/shard_map/pallas_call | solution.py:239
  120.4 2.7 %reduce_sum.12 = bf16[256,512]{1,0:T(8,128)(2,1)} reduce(bf16[8,256,512]{2,1,0:T(8,128)(2,1)} %shard_map.66, bf16[]{:T(256)} %constant.87.clone.1), dimensions={0}, to_apply=%region_4.5 | reduce | flops 917504 | bytes 2359298 | tf_op jit(solution)/shard_map/reduce_sum | solution.py:290
  (6 shorter events, 0.1 us)
Async XLA Ops:
  51.6 3.9 %copy-start = (bf16[256,1024]{1,0:T(8,128)(2,1)S(1)}, bf16[256,1024]{1,0:T(8,128)(2,1)}, u32[]{:S(2)}) copy-start(bf16[256,1024]{1,0:T(8,128)(2,1)} %param.8) | copy-start | bytes 1572868

commit v8 on v7

--- a/solution.py
+++ b/solution.py
@@ -95,13 +95,16 @@
 MESH_ID = pl.DeviceIdType.MESH
 
 
-def window_kernel(depth, plane, n_ctx, kv_ref, zero_ref, win_ref, send1, recv1, send2, recv2, local_sem):
+def window_kernel(depth, plane, n_ctx, need_col, kv_ref, zero_ref, win_ref, send1, recv1, send2, recv2, local_sem):
     del zero_ref
     me = lax.axis_index("ctx")
     h = lax.axis_index("head")
     z = me // plane
     r = me % plane
     n_z = n_ctx // plane
+    mate = r + 1 - 2 * (r % 2)
+    across = (r + 2) % plane
+    far = across + 1 - 2 * (across % 2)
     barrier = pltpu.get_barrier_semaphore()
     for d in range(1, depth + 1):
         @pl.when(z + d < n_z)
@@ -112,14 +115,14 @@
         def _():
             pl.semaphore_signal(barrier, 1, device_id=(me - d * plane, h), device_id_type=MESH_ID)
 
-    for e in range(1, plane):
-        peer = z * plane + lax.rem(r + e, plane)
-        pl.semaphore_signal(barrier, 1, device_id=(peer, h), device_id_type=MESH_ID)
-    pl.semaphore_wait(
-        barrier, jnp.minimum(depth, n_z - 1 - z) + jnp.minimum(depth, z) + (plane - 1)
-    )
+    for peer in (mate, across):
+        pl.semaphore_signal(barrier, 1, device_id=(z * plane + peer, h), device_id_type=MESH_ID)
+    pl.semaphore_wait(barrier, jnp.minimum(depth, n_z - 1 - z) + jnp.minimum(depth, z) + 2)
     local = pltpu.make_async_copy(kv_ref, win_ref.at[r, depth], local_sem)
     local.start()
+
+    def wanted(d):
+        return (d < depth) | (r >= need_col)
 
     def down(d):
         return pltpu.make_async_remote_copy(
@@ -132,56 +135,75 @@
         )
 
     for d in range(1, depth + 1):
-        @pl.when(z + d < n_z)
+        @pl.when((z + d < n_z) & wanted(d))
         def _():
             down(d).start()
 
-    local.wait()
-
-    def across(e, col, slot):
+    def has(slot, col):
+        return (z - (depth - slot) >= 0) & ((slot > 0) | (col >= need_col))
+
+    def hop(idx, col, slot, to):
         return pltpu.make_async_remote_copy(
             src_ref=win_ref.at[col, slot],
             dst_ref=win_ref.at[col, slot],
-            send_sem=send2.at[e - 1, slot],
-            recv_sem=recv2.at[e - 1, slot],
-            device_id=(z * plane + lax.rem(r + e, plane), h),
+            send_sem=send2.at[idx, slot],
+            recv_sem=recv2.at[idx, slot],
+            device_id=(z * plane + to, h),
             device_id_type=MESH_ID,
         )
 
-    for e in range(1, plane):
-        across(e, r, depth).start()
+    local.wait()
+    hop(0, r, depth, mate).start()
+    hop(1, r, depth, across).start()
     for d in range(1, depth + 1):
-        @pl.when(z + d < n_z)
+        @pl.when((z + d < n_z) & wanted(d))
         def _():
             down(d).wait_send()
 
-        @pl.when(z - d >= 0)
+        @pl.when((z - d >= 0) & wanted(d))
         def _():
             down(d).wait_recv()
-            for e in range(1, plane):
-                across(e, r, depth - d).start()
+            hop(0, r, depth - d, mate).start()
+            hop(1, r, depth - d, across).start()
+
+    for slot in range(depth, -1, -1):
+        @pl.when(has(slot, across))
+        def _():
+            hop(1, across, slot, across).wait_recv()
+            hop(2, across, slot, mate).start()
 
     for slot in range(depth + 1):
-        @pl.when(z - (depth - slot) >= 0)
-        def _():
-            for e in range(1, plane):
-                across(e, r, slot).wait_send()
-                across(e, lax.rem(r + plane - e, plane), slot).wait_recv()
-
-
-def gather_window(kv_local, depth, plane, n_ctx):
+        @pl.when(has(slot, r))
+        def _():
+            hop(0, r, slot, mate).wait_send()
+            hop(1, r, slot, across).wait_send()
+
+        @pl.when(has(slot, across))
+        def _():
+            hop(2, across, slot, mate).wait_send()
+
+        @pl.when(has(slot, mate))
+        def _():
+            hop(0, mate, slot, mate).wait_recv()
+
+        @pl.when(has(slot, far))
+        def _():
+            hop(2, far, slot, mate).wait_recv()
+
+
+def gather_window(kv_local, depth, plane, n_ctx, need_col):
     rows, width = kv_local.shape
     zero = jnp.zeros((plane, depth + 1, rows, width), kv_local.dtype)
     return pl.pallas_call(
-        functools.partial(window_kernel, depth, plane, n_ctx),
+        functools.partial(window_kernel, depth, plane, n_ctx, need_col),
         out_shape=jax.ShapeDtypeStruct(zero.shape, zero.dtype),
         in_specs=[pl.BlockSpec(memory_space=pl.ANY), pl.BlockSpec(memory_space=pl.ANY)],
         out_specs=pl.BlockSpec(memory_space=pl.ANY),
         scratch_shapes=[
             pltpu.SemaphoreType.DMA((depth,)),
             pltpu.SemaphoreType.DMA((depth,)),
-            pltpu.SemaphoreType.DMA((plane - 1, depth + 1)),
-            pltpu.SemaphoreType.DMA((plane - 1, depth + 1)),
+            pltpu.SemaphoreType.DMA((3, depth + 1)),
+            pltpu.SemaphoreType.DMA((3, depth + 1)),
             pltpu.SemaphoreType.DMA(()),
         ],
         input_output_aliases={1: 0},
@@ -272,7 +294,8 @@
     n_ctx = lax.axis_size("ctx")
     plane = PLANE
     depth = min(n_ctx // plane - 1, -(-(LONGEST - 1) // (plane * row_count)))
-    kv_win = gather_window(kv_local, depth, plane, n_ctx)
+    need_col = max(0, -(-(plane * row_count * depth - (LONGEST - 1) - (row_count - 1)) // row_count))
+    kv_win = gather_window(kv_local, depth, plane, n_ctx, need_col)
     kv_win = kv_win.transpose(1, 0, 2, 3).reshape(-1, kv_win.shape[-1])
     base = (here // plane - depth) * plane * row_count
     span = kv_win.shape[0]

time: 124 us -> 113 us (0.911)
  Pallas kernels: 98.6 us -> 88.6 us
    pallas_call x1, Pallas kernels: 43.1 us -> 38.3 us  [gather_window(): pl.pallas_call(functools.partial(window_kernel, depth, plane, n_ctx, need...]
    pallas_call x1, Pallas kernels: 26.2 us -> 21.6 us  [attend(): pl.pallas_call(attn_kernel, out_shape=jax.ShapeDtypeStruct((rows, HD), jn...]
where the time goes in v8:
time: 113 us
  Pallas kernels  88.6 us (78%)
  local copies, waits for them, and re-layouts  11.2 us (10%)
  matrix products  7.07 us (6%)
  other arithmetic  6.13 us (5%)
    pallas_call x1, Pallas kernels, gather_window(): pl.pallas_call(functools.partial(window_kernel, depth, plane, n_ctx, need...  38.3 us
    pallas_call x1, Pallas kernels, swap_parts(): pl.pallas_call(functools.partial(swap_kernel, n_head), out_shape=jax.Shap...  28.8 us
    pallas_call x1, Pallas kernels, attend(): pl.pallas_call(attn_kernel, out_shape=jax.ShapeDtypeStruct((rows, HD), jn...  21.6 us
    dot_general x1, matrix products, on_device(): jnp.dot(att, out_weight, preferred_element_type=jnp.float32)  7.07 us
    transpose x1, local copies, waits for them, and re-layouts, on_device(): kv_win = kv_win.transpose(1, 0, 2, 3).reshape(-1, kv_win.shape[-1])  3.92 us
    reduce_sum x1, other arithmetic, on_device(): return jnp.sum(got.astype(jnp.float32), axis=0).astype(jnp.bfloat16)  2.66 us

profile of v8, /device:TPU:192, one launch (start us, length us, event | category | flops | bytes accessed | tf_op | source)
XLA Modules:
  0.0 113.1 jit_solution(17743980145575745160)
XLA Ops:
  0.0 0.7 copy.28
  0.8 0.1 reduce.1
  0.9 0.1 select_reduce_fusion
  1.0 0.8 dynamic-slice_multiply_fusion
  1.8 0.1 broadcast_in_dim.31
  1.8 0.1 mul.35
  1.9 0.1 broadcast_in_dim.32
  2.0 0.7 sub.106.lo_ref
  2.8 0.1 broadcast_in_dim.30
  2.8 0.7 sub.104.qpos_ref
  3.6 0.1 mul.31
  3.6 0.1 broadcast_in_dim.27
  3.7 0.1 mul.32
  3.8 0.2 fusion
  4.0 0.1 copy.29
  4.1 0.1 copy.33
  4.2 0.1 maximum_minimum_fusion
  4.3 0.7 pad_add_fusion.tiles_ref
  4.9 1.5 %pad_maximum_fusion.kv_ref = bf16[256,256]{1,0:T(8,128)(2,1)} fusion(bf16[256,128]{1,0:T(8,128)(2,1)} %param.10, bf16[256,128]{1,0:T(8,128)(2,1)} %param.9), kind=kLoop, calls=%fused_computation.1 | loop fusion | flops 262144 | bytes 262144 | tf_op jit(solution)/shard_map/concatenate | solution.py:293
  6.5 2.0 %broadcast_in_dim.29.zero_ref = bf16[4,6,256,256]{3,2,1,0:T(8,128)(2,1)} broadcast(bf16[]{:T(256)} %constant.87.clone.1), dimensions={} | broadcast | bytes 3145730 | tf_op jit(solution)/shard_map/broadcast_in_dim | solution.py:196
  8.5 38.3 %shard_map.64 = bf16[4,6,256,256]{3,2,1,0:T(8,128)(2,1)} custom-call(bf16[256,256]{1,0:T(8,128)(2,1)} %pad_maximum_fusion.kv_ref, bf16[4,6,256,256]{3,2,1,0:T(8,128)(2,1)} %broadcast_in_dim.29.zero_ref), custom_call_target="tpu_custom_call", output_to_operand_aliasing={{}: (1, {})} | custom-call | tf_op jit(solution)/shard_map/pallas_call | solution.py:197
  46.8 0.0 copy-start
  46.8 3.9 %copy.37 = bf16[6,4,256,256]{3,2,1,0:T(8,128)(2,1)} copy(bf16[6,4,256,256]{3,2,0,1:T(8,128)(2,1)} %bitcast.15) | data formatting | bytes 6291456 | tf_op jit(solution)/shard_map/transpose | solution.py:299
  50.7 0.0 copy-done
  50.7 1.0 reshape.205.q_ref
  51.7 21.6 %shard_map.65 = bf16[2048,128]{1,0:T(8,128)(2,1)} custom-call(s32[2,4]{1,0:T(2,128)} %pad_add_fusion.tiles_ref, bf16[2048,128]{1,0:T(8,128)(2,1)} %reshape.205.q_ref, bf16[6144,256]{1,0:T(8,128)(2,1)} %bitcast.16, s32[1,2048]{1,0:T(1,128)} %sub.104.qpos_ref, s32[1,2048]{1,0:T(1,128)} %sub.106.lo_ref), custom_call_target="tpu_custom_call" | custom-call | tf_op jit(solution)/shard_map/pallas_call | solution.py:76
  73.3 1.3 %reshape.207 = bf16[256,1024]{1,0:T(8,128)(2,1)S(1)} reshape(bf16[2048,128]{1,0:T(8,128)(2,1)} %shard_map.65) | data formatting | bytes 1048576 | tf_op jit(solution)/shard_map/reshape | solution.py:308
  74.6 7.1 %convolution_convert_fusion.partial_ref = bf16[256,4096]{1,0:T(8,128)(2,1)} fusion(bf16[256,1024]{1,0:T(8,128)(2,1)S(1)} %reshape.207, bf16[1024,4096]{1,0:T(8,128)(2,1)} %param.13), kind=kOutput, calls=%fused_computation | convolution fusion | flops 2148532224 | bytes 11010048 | tf_op jit(solution)/shard_map/dot_general | solution.py:310
  81.7 28.8 %shard_map.66 = bf16[8,256,512]{2,1,0:T(8,128)(2,1)} custom-call(bf16[256,4096]{1,0:T(8,128)(2,1)} %convolution_convert_fusion.partial_ref), custom_call_target="tpu_custom_call" | custom-call | tf_op jit(solution)/shard_map/pallas_call | solution.py:261
  110.4 2.7 %reduce_sum.12 = bf16[256,512]{1,0:T(8,128)(2,1)} reduce(bf16[8,256,512]{2,1,0:T(8,128)(2,1)} %shard_map.66, bf16[]{:T(256)} %constant.87.clone.1), dimensions={0}, to_apply=%region_4.5 | reduce | flops 917504 | bytes 2359298 | tf_op jit(solution)/shard_map/reduce_sum | solution.py:313
  (6 shorter events, 0.1 us)
Async XLA Ops:
  46.8 3.9 %copy-start = (bf16[256,1024]{1,0:T(8,128)(2,1)S(1)}, bf16[256,1024]{1,0:T(8,128)(2,1)}, u32[]{:S(2)}) copy-start(bf16[256,1024]{1,0:T(8,128)(2,1)} %param.8) | copy-start | bytes 1572868

commit v9 on v8

--- a/solution.py
+++ b/solution.py
@@ -11,12 +11,13 @@
 BLK = 8
 TQ = 1024
 TK = 512
+SHARD = 256
 NEG_FILL = -1e30
 LONGEST = 4352
 PLANE = 4
 
 
-def attn_kernel(tiles_ref, q_ref, kv_ref, qpos_ref, lo_ref, o_ref, m_sc, l_sc, acc_sc):
+def attn_kernel(plane, slots, tiles_ref, q_ref, kv_ref, qpos_ref, lo_ref, o_ref, m_sc, l_sc, acc_sc):
     n_q = q_ref.shape[0] // TQ
     scale = HD ** (-0.5)
 
@@ -31,11 +32,17 @@
 
         def k_step(kj, masked):
             c0 = pl.multiple_of(kj * TK, TK)
-            k = kv_ref[pl.ds(c0, TK), pl.ds(0, HD)]
-            v = kv_ref[pl.ds(c0, TK), pl.ds(HD, HD)]
-            s = lax.dot_general(
-                k, q, (((1,), (1,)), ((), ())), preferred_element_type=jnp.float32
-            ) * scale
+            at = []
+            for piece in range(TK // SHARD):
+                i = kj * (TK // SHARD) + piece
+                at.append(pl.multiple_of((lax.rem(i, plane) * slots + i // plane) * SHARD, SHARD))
+            s = jnp.concatenate([
+                lax.dot_general(
+                    kv_ref[pl.ds(a, SHARD), pl.ds(0, HD)], q, (((1,), (1,)), ((), ())),
+                    preferred_element_type=jnp.float32,
+                )
+                for a in at
+            ], axis=0) * scale
             if masked:
                 kpos = c0 + lax.broadcasted_iota(jnp.int32, (TK, TQ), 0)
                 ok = (kpos >= lo) & (kpos <= qpos)
@@ -47,10 +54,14 @@
                 p = jnp.where(ok, p, 0.0)
             fade = jnp.exp(m_prev - m_new)
             l_sc[...] = l_sc[...] * fade + jnp.sum(p, axis=0, keepdims=True)
-            acc_sc[...] = acc_sc[...] * fade + lax.dot_general(
-                v, p.astype(jnp.bfloat16), (((0,), (0,)), ((), ())),
-                preferred_element_type=jnp.float32,
-            )
+            pb = p.astype(jnp.bfloat16)
+            update = acc_sc[...] * fade
+            for piece, a in enumerate(at):
+                update = update + lax.dot_general(
+                    kv_ref[pl.ds(a, SHARD), pl.ds(HD, HD)], pb[piece * SHARD:(piece + 1) * SHARD],
+                    (((0,), (0,)), ((), ())), preferred_element_type=jnp.float32,
+                )
+            acc_sc[...] = update
             m_sc[...] = m_new
 
         def masked_body(kj, c):
@@ -70,11 +81,11 @@
     lax.fori_loop(0, n_q, q_body, 0)
 
 
-def attend(q_rows, kv_all, qpos_rows, lo_rows, tiles):
+def attend(q_rows, kv_all, qpos_rows, lo_rows, tiles, plane, slots):
     rows = q_rows.shape[0]
     vmem = pltpu.MemorySpace.VMEM if hasattr(pltpu, "MemorySpace") else pltpu.VMEM
     return pl.pallas_call(
-        attn_kernel,
+        functools.partial(attn_kernel, plane, slots),
         out_shape=jax.ShapeDtypeStruct((rows, HD), jnp.bfloat16),
         in_specs=[
             pl.BlockSpec(memory_space=pltpu.SMEM),
@@ -211,26 +222,28 @@
     )(kv_local, zero)
 
 
-def swap_kernel(n_head, partial_ref, got_ref, send_sem, recv_sem, local_sem):
+def project_kernel(n_head, att_ref, w_ref, o_ref, send_buf, got, send_sem, recv_sem):
     me = lax.axis_index("head")
-    cols = got_ref.shape[2]
     row = lax.axis_index("ctx")
+    cols = o_ref.shape[1]
     barrier = pltpu.get_barrier_semaphore()
     for d in range(1, n_head):
         pl.semaphore_signal(
             barrier, 1, device_id=(row, lax.rem(me + d, n_head)), device_id_type=MESH_ID
         )
     pl.semaphore_wait(barrier, n_head - 1)
-    local = pltpu.make_async_copy(
-        partial_ref.at[:, pl.ds(me * cols, cols)], got_ref.at[me], local_sem
-    )
-    local.start()
+
+    def part(dst):
+        c0 = pl.multiple_of(dst * cols, cols)
+        return jnp.dot(
+            att_ref[...], w_ref[:, pl.ds(c0, cols)], preferred_element_type=jnp.float32
+        ).astype(jnp.bfloat16)
 
     def send(d):
         dst = lax.rem(me + d, n_head)
         return pltpu.make_async_remote_copy(
-            src_ref=partial_ref.at[:, pl.ds(dst * cols, cols)],
-            dst_ref=got_ref.at[me],
+            src_ref=send_buf.at[d - 1],
+            dst_ref=got.at[me],
             send_sem=send_sem.at[d - 1],
             recv_sem=recv_sem.at[d - 1],
             device_id=(row, dst),
@@ -240,36 +253,44 @@
     def arrival(d):
         src = lax.rem(me + n_head - d, n_head)
         return pltpu.make_async_remote_copy(
-            src_ref=partial_ref.at[:, pl.ds(src * cols, cols)],
-            dst_ref=got_ref.at[src],
+            src_ref=send_buf.at[d - 1],
+            dst_ref=got.at[src],
             send_sem=send_sem.at[d - 1],
             recv_sem=recv_sem.at[d - 1],
             device_id=(row, src),
             device_id_type=MESH_ID,
         )
 
+    send_buf[0] = part(lax.rem(me + 1, n_head))
     for d in range(1, n_head):
+        if d + 1 < n_head:
+            send_buf[d] = part(lax.rem(me + d + 1, n_head))
         send(d).start()
+    total = part(me).astype(jnp.float32)
     for d in range(1, n_head):
         send(d).wait_send()
         arrival(d).wait_recv()
-    local.wait()
-
-
-def swap_parts(partial_value, n_head):
-    rows, width = partial_value.shape
+        total = total + got[lax.rem(me + n_head - d, n_head)].astype(jnp.float32)
+    o_ref[...] = total.astype(o_ref.dtype)
+
+
+def project(att, out_weight, n_head):
+    rows = att.shape[0]
+    cols = out_weight.shape[1] // n_head
+    vmem = pltpu.MemorySpace.VMEM if hasattr(pltpu, "MemorySpace") else pltpu.VMEM
     return pl.pallas_call(
-        functools.partial(swap_kernel, n_head),
-        out_shape=jax.ShapeDtypeStruct((n_head, rows, width // n_head), partial_value.dtype),
-        in_specs=[pl.BlockSpec(memory_space=pl.ANY)],
-        out_specs=pl.BlockSpec(memory_space=pl.ANY),
+        functools.partial(project_kernel, n_head),
+        out_shape=jax.ShapeDtypeStruct((rows, cols), jnp.bfloat16),
+        in_specs=[pl.BlockSpec(memory_space=vmem), pl.BlockSpec(memory_space=vmem)],
+        out_specs=pl.BlockSpec(memory_space=vmem),
         scratch_shapes=[
+            pltpu.VMEM((n_head - 1, rows, cols), jnp.bfloat16),
+            pltpu.VMEM((n_head, rows, cols), jnp.bfloat16),
             pltpu.SemaphoreType.DMA((n_head - 1,)),
             pltpu.SemaphoreType.DMA((n_head - 1,)),
-            pltpu.SemaphoreType.DMA(()),
         ],
         compiler_params=pltpu.CompilerParams(collective_id=1, has_side_effects=True),
-    )(partial_value)
+    )(att, out_weight)
 
 
 def on_device(queries, key_rows, values, lengths, block_plan, inverse, mask_lo, out_weight):
@@ -296,7 +317,7 @@
     depth = min(n_ctx // plane - 1, -(-(LONGEST - 1) // (plane * row_count)))
     need_col = max(0, -(-(plane * row_count * depth - (LONGEST - 1) - (row_count - 1)) // row_count))
     kv_win = gather_window(kv_local, depth, plane, n_ctx, need_col)
-    kv_win = kv_win.transpose(1, 0, 2, 3).reshape(-1, kv_win.shape[-1])
+    kv_win = kv_win.reshape(-1, kv_win.shape[-1])
     base = (here // plane - depth) * plane * row_count
     span = kv_win.shape[0]
     t0 = (tile_lo - base) // TK
@@ -305,12 +326,9 @@
     t2 = jnp.clip((tile_hi_min - base + 1) // TK, t1, t3)
     tiles = jnp.stack([t0, t1, t2, t3], axis=1).astype(jnp.int32)
     q_rows = queries.reshape(row_count * group_size, HD)
-    att = attend(q_rows, kv_win, qpos_rows - base, lo_rows - base, tiles).reshape(row_count, query_width)
-
-    partial_value = jnp.dot(att, out_weight, preferred_element_type=jnp.float32).astype(jnp.bfloat16)
-    n_head = lax.axis_size("head")
-    got = swap_parts(partial_value, n_head)
-    return jnp.sum(got.astype(jnp.float32), axis=0).astype(jnp.bfloat16)
+    att = attend(q_rows, kv_win, qpos_rows - base, lo_rows - base, tiles, plane, depth + 1).reshape(row_count, query_width)
+
+    return project(att, out_weight, lax.axis_size("head"))
 
 
 def solution(mesh):

time: 113 us -> 110 us (0.973)
  Pallas kernels: 88.6 us -> 96.2 us
  matrix products: 7.07 us -> 0 us
  other arithmetic: 6.13 us -> 3.49 us
  local copies, waits for them, and re-layouts: 11.2 us -> 9.72 us
    pallas_call x2, Pallas kernels: 50.4 us -> 57.9 us  [the longest x1 33.9 us: project(): pl.pallas_call(functools.partial(project_kernel, n_head), out_shape=jax.S...]
    dot_general x1 -> x0, matrix products: 7.07 us -> none  [on_device(): jnp.dot(att, out_weight, preferred_element_type=jnp.float32)]
    transpose x1 -> x0, local copies, waits for them, and re-layouts: 3.92 us -> none  [on_device(): kv_win = kv_win.transpose(1, 0, 2, 3).reshape(-1, kv_win.shape[-1])]
    reduce_sum x1 -> x0, other arithmetic: 2.66 us -> none  [on_device(): return jnp.sum(got.astype(jnp.float32), axis=0).astype(jnp.bfloat16)]
    unnamed x2 -> x3, local copies, waits for them, and re-layouts: 0.01 us -> 1.67 us
where the time goes in v9:
time: 110 us; the launch traced here: 109 us
  Pallas kernels  96.2 us (87%)
  local copies, waits for them, and re-layouts  9.72 us (9%)
  other arithmetic  3.49 us (3%)
    pallas_call x1, Pallas kernels, gather_window(): pl.pallas_call(functools.partial(window_kernel, depth, plane, n_ctx, need...  38.3 us
    pallas_call x1, Pallas kernels, project(): pl.pallas_call(functools.partial(project_kernel, n_head), out_shape=jax.S...  33.9 us
    pallas_call x1, Pallas kernels, attend(): pl.pallas_call(functools.partial(attn_kernel, plane, slots), out_shape=ja...  24 us

profile of v9, /device:TPU:192, one launch (start us, length us, event | category | flops | bytes accessed | tf_op | source)
XLA Modules:
  0.0 109.4 jit_solution(2366145052597177913)
XLA Ops:
  0.0 0.7 copy.26
  0.8 0.1 reduce
  0.9 0.1 select_reduce_fusion
  1.0 0.8 dynamic-slice_multiply_fusion
  1.8 0.1 broadcast_in_dim.31
  1.8 0.1 mul.35
  1.9 0.1 broadcast_in_dim.32
  2.0 0.7 sub.106.lo_ref
  2.8 0.1 broadcast_in_dim.30
  2.9 0.7 sub.104.qpos_ref
  3.6 0.1 mul.31
  3.7 0.1 broadcast_in_dim.27
  3.7 0.1 mul.32
  3.8 0.2 fusion
  4.0 0.1 copy.27
  4.1 0.1 copy.31
  4.2 0.1 maximum_minimum_fusion
  4.3 0.7 pad_add_fusion.tiles_ref
  4.9 1.5 %pad_maximum_fusion.kv_ref = bf16[256,256]{1,0:T(8,128)(2,1)} fusion(bf16[256,128]{1,0:T(8,128)(2,1)} %param.10, bf16[256,128]{1,0:T(8,128)(2,1)} %param.9), kind=kLoop, calls=%fused_computation | loop fusion | flops 262144 | bytes 262144 | tf_op jit(solution)/shard_map/concatenate | solution.py:314
  6.5 2.0 %broadcast_in_dim.29.zero_ref = bf16[4,6,256,256]{3,2,1,0:T(8,128)(2,1)} broadcast(bf16[]{:T(256)} %constant.85.clone.1), dimensions={} | broadcast | bytes 3145730 | tf_op jit(solution)/shard_map/broadcast_in_dim | solution.py:207
  8.5 0.0 copy-start
  8.5 38.3 %shard_map.64 = bf16[4,6,256,256]{3,2,1,0:T(8,128)(2,1)} custom-call(bf16[256,256]{1,0:T(8,128)(2,1)} %pad_maximum_fusion.kv_ref, bf16[4,6,256,256]{3,2,1,0:T(8,128)(2,1)} %broadcast_in_dim.29.zero_ref), custom_call_target="tpu_custom_call", output_to_operand_aliasing={{}: (1, {})} | custom-call | tf_op jit(solution)/shard_map/pallas_call | solution.py:208
  46.8 0.0 copy-done
  46.8 1.0 reshape.205.q_ref
  47.8 24.0 %shard_map.65 = bf16[2048,128]{1,0:T(8,128)(2,1)} custom-call(s32[2,4]{1,0:T(2,128)} %pad_add_fusion.tiles_ref, bf16[2048,128]{1,0:T(8,128)(2,1)} %reshape.205.q_ref, bf16[6144,256]{1,0:T(8,128)(2,1)} %bitcast.12, s32[1,2048]{1,0:T(1,128)} %sub.104.qpos_ref, s32[1,2048]{1,0:T(1,128)} %sub.106.lo_ref), custom_call_target="tpu_custom_call" | custom-call | tf_op jit(solution)/shard_map/pallas_call | solution.py:87
  71.8 2.1 %reshape.207.att_ref = bf16[256,1024]{1,0:T(8,128)(2,1)} reshape(bf16[2048,128]{1,0:T(8,128)(2,1)} %shard_map.65) | data formatting | bytes 1048576 | tf_op jit(solution)/shard_map/reshape | solution.py:329
  73.9 33.9 %shard_map.66 = bf16[256,512]{1,0:T(8,128)(2,1)} custom-call(bf16[256,1024]{1,0:T(8,128)(2,1)} %reshape.207.att_ref, bf16[1024,4096]{1,0:T(8,128)(2,1)} %w_ref.1), custom_call_target="tpu_custom_call" | custom-call | tf_op jit(solution)/shard_map/pallas_call | solution.py:281
  107.8 1.7 %copy.37 = bf16[256,512]{1,0:T(8,128)(2,1)} copy(bf16[256,512]{1,0:T(8,128)(2,1)} %shard_map.66) | data formatting | bytes 524288
  (6 shorter events, 0.1 us)
Async XLA Ops:
  8.5 38.3 %copy-start = (bf16[256,1024]{1,0:T(8,128)(2,1)S(1)}, bf16[256,1024]{1,0:T(8,128)(2,1)}, u32[]{:S(2)}) copy-start(bf16[256,1024]{1,0:T(8,128)(2,1)} %param.8) | copy-start | bytes 1572868

commit v10 on v9

--- a/solution.py
+++ b/solution.py
@@ -222,6 +222,187 @@
     )(kv_local, zero)
 
 
+def window_attend_kernel(depth, plane, n_ctx, need_col, kv_ref, q_ref, qpos_ref, lo_ref, o_ref,
+                         win, send1, recv1, send2, recv2, local_sem, m_sc, l_sc, acc_sc):
+    me = lax.axis_index("ctx")
+    h = lax.axis_index("head")
+    z = me // plane
+    r = me % plane
+    n_z = n_ctx // plane
+    slots = depth + 1
+    mate = r + 1 - 2 * (r % 2)
+    across = (r + 2) % plane
+    far = across + 1 - 2 * (across % 2)
+    rows = kv_ref.shape[0]
+    tq = q_ref.shape[0] // 2
+    scale = HD ** (-0.5)
+
+    def wanted(d):
+        return (d < depth) | (r >= need_col)
+
+    def has(slot, col):
+        return (z - (depth - slot) >= 0) & ((slot > 0) | (col >= need_col))
+
+    for col in range(plane):
+        for slot in range(slots):
+            @pl.when(jnp.logical_not(has(slot, col)))
+            def _():
+                win[col, slot] = jnp.zeros(win.shape[2:], win.dtype)
+
+    barrier = pltpu.get_barrier_semaphore()
+    for d in range(1, depth + 1):
+        @pl.when(z + d < n_z)
+        def _():
+            pl.semaphore_signal(barrier, 1, device_id=(me + d * plane, h), device_id_type=MESH_ID)
+
+        @pl.when(z - d >= 0)
+        def _():
+            pl.semaphore_signal(barrier, 1, device_id=(me - d * plane, h), device_id_type=MESH_ID)
+
+    for peer in (mate, across):
+        pl.semaphore_signal(barrier, 1, device_id=(z * plane + peer, h), device_id_type=MESH_ID)
+    pl.semaphore_wait(barrier, jnp.minimum(depth, n_z - 1 - z) + jnp.minimum(depth, z) + 2)
+    local = pltpu.make_async_copy(kv_ref, win.at[r, depth], local_sem)
+    local.start()
+
+    def down(d):
+        return pltpu.make_async_remote_copy(
+            src_ref=kv_ref,
+            dst_ref=win.at[r, depth - d],
+            send_sem=send1.at[d - 1],
+            recv_sem=recv1.at[d - 1],
+            device_id=(me + d * plane, h),
+            device_id_type=MESH_ID,
+        )
+
+    for d in range(1, depth + 1):
+        @pl.when((z + d < n_z) & wanted(d))
+        def _():
+            down(d).start()
+
+    def hop(idx, col, slot, to):
+        return pltpu.make_async_remote_copy(
+            src_ref=win.at[col, slot],
+            dst_ref=win.at[col, slot],
+            send_sem=send2.at[idx, slot],
+            recv_sem=recv2.at[idx, slot],
+            device_id=(z * plane + to, h),
+            device_id_type=MESH_ID,
+        )
+
+    m_sc[...] = jnp.full(m_sc.shape, NEG_FILL, jnp.float32)
+    l_sc[...] = jnp.zeros(l_sc.shape, jnp.float32)
+    acc_sc[...] = jnp.zeros(acc_sc.shape, jnp.float32)
+    first_shard = (r * rows + plane * rows * depth - (LONGEST - 1)) // rows
+    last_shard = plane * depth + r
+
+    def tile_step(j, carry, slot):
+        half = j // 2
+        qt = j % 2
+        i0 = slot * plane + 2 * half
+
+        @pl.when((i0 + 1 >= first_shard) & (i0 <= last_shard))
+        def _():
+            r0 = pl.multiple_of(qt * tq, tq)
+            q = q_ref[pl.ds(r0, tq), :]
+            qpos = qpos_ref[:, pl.ds(r0, tq)]
+            lo = lo_ref[:, pl.ds(r0, tq)]
+            k0 = win[2 * half, slot, :, pl.ds(0, HD)]
+            k1 = win[2 * half + 1, slot, :, pl.ds(0, HD)]
+            s = jnp.concatenate([
+                lax.dot_general(k, q, (((1,), (1,)), ((), ())), preferred_element_type=jnp.float32)
+                for k in (k0, k1)
+            ], axis=0) * scale
+            kpos = i0 * rows + lax.broadcasted_iota(jnp.int32, s.shape, 0)
+            ok = (kpos >= lo) & (kpos <= qpos)
+            s = jnp.where(ok, s, NEG_FILL)
+            m_prev = m_sc[:, pl.ds(r0, tq)]
+            m_new = jnp.maximum(m_prev, jnp.max(s, axis=0, keepdims=True))
+            p = jnp.where(ok, jnp.exp(s - m_new), 0.0)
+            fade = jnp.exp(m_prev - m_new)
+            l_sc[:, pl.ds(r0, tq)] = l_sc[:, pl.ds(r0, tq)] * fade + jnp.sum(p, axis=0, keepdims=True)
+            pb = p.astype(jnp.bfloat16)
+            update = acc_sc[:, pl.ds(r0, tq)] * fade
+            for piece in range(2):
+                v = win[2 * half + piece, slot, :, pl.ds(HD, HD)]
+                update = update + lax.dot_general(
+                    v, pb[piece * rows:(piece + 1) * rows], (((0,), (0,)), ((), ())),
+                    preferred_element_type=jnp.float32,
+                )
+            acc_sc[:, pl.ds(r0, tq)] = update
+            m_sc[:, pl.ds(r0, tq)] = m_new
+
+        return carry
+
+    local.wait()
+    hop(0, r, depth, mate).start()
+    hop(1, r, depth, across).start()
+    for slot in range(depth, -1, -1):
+        d = depth - slot
+        if d > 0:
+            @pl.when((z - d >= 0) & wanted(d))
+            def _():
+                down(d).wait_recv()
+                hop(0, r, slot, mate).start()
+                hop(1, r, slot, across).start()
+
+        @pl.when(has(slot, across))
+        def _():
+            hop(1, across, slot, across).wait_recv()
+            hop(2, across, slot, mate).start()
+
+        @pl.when(has(slot, mate))
+        def _():
+            hop(0, mate, slot, mate).wait_recv()
+
+        @pl.when(has(slot, far))
+        def _():
+            hop(2, far, slot, mate).wait_recv()
+
+        lax.fori_loop(0, plane, functools.partial(tile_step, slot=slot), 0)
+
+    for d in range(1, depth + 1):
+        @pl.when((z + d < n_z) & wanted(d))
+        def _():
+            down(d).wait_send()
+
+    for slot in range(slots):
+        @pl.when(has(slot, r))
+        def _():
+            hop(0, r, slot, mate).wait_send()
+            hop(1, r, slot, across).wait_send()
+
+        @pl.when(has(slot, across))
+        def _():
+            hop(2, across, slot, mate).wait_send()
+
+    o_ref[...] = (acc_sc[...] / l_sc[...]).T.astype(o_ref.dtype)
+
+
+def window_attend(kv_local, q_rows, qpos_rows, lo_rows, depth, plane, n_ctx, need_col):
+    rows, width = kv_local.shape
+    n_rows = q_rows.shape[0]
+    vmem = pltpu.MemorySpace.VMEM if hasattr(pltpu, "MemorySpace") else pltpu.VMEM
+    return pl.pallas_call(
+        functools.partial(window_attend_kernel, depth, plane, n_ctx, need_col),
+        out_shape=jax.ShapeDtypeStruct((n_rows, HD), jnp.bfloat16),
+        in_specs=[pl.BlockSpec(memory_space=vmem)] * 4,
+        out_specs=pl.BlockSpec(memory_space=vmem),
+        scratch_shapes=[
+            pltpu.VMEM((plane, depth + 1, rows, width), kv_local.dtype),
+            pltpu.SemaphoreType.DMA((depth,)),
+            pltpu.SemaphoreType.DMA((depth,)),
+            pltpu.SemaphoreType.DMA((3, depth + 1)),
+            pltpu.SemaphoreType.DMA((3, depth + 1)),
+            pltpu.SemaphoreType.DMA(()),
+            pltpu.VMEM((1, n_rows), jnp.float32),
+            pltpu.VMEM((1, n_rows), jnp.float32),
+            pltpu.VMEM((HD, n_rows), jnp.float32),
+        ],
+        compiler_params=pltpu.CompilerParams(collective_id=0, has_side_effects=True),
+    )(kv_local, q_rows, qpos_rows, lo_rows)
+
+
 def project_kernel(n_head, att_ref, w_ref, o_ref, send_buf, got, send_sem, recv_sem):
     me = lax.axis_index("head")
     row = lax.axis_index("ctx")
@@ -316,17 +497,11 @@
     plane = PLANE
     depth = min(n_ctx // plane - 1, -(-(LONGEST - 1) // (plane * row_count)))
     need_col = max(0, -(-(plane * row_count * depth - (LONGEST - 1) - (row_count - 1)) // row_count))
-    kv_win = gather_window(kv_local, depth, plane, n_ctx, need_col)
-    kv_win = kv_win.reshape(-1, kv_win.shape[-1])
     base = (here // plane - depth) * plane * row_count
-    span = kv_win.shape[0]
-    t0 = (tile_lo - base) // TK
-    t3 = jnp.minimum((tile_hi - base) // TK + 1, span // TK)
-    t1 = jnp.clip((tile_lo_max - base + TK - 1) // TK, t0, t3)
-    t2 = jnp.clip((tile_hi_min - base + 1) // TK, t1, t3)
-    tiles = jnp.stack([t0, t1, t2, t3], axis=1).astype(jnp.int32)
     q_rows = queries.reshape(row_count * group_size, HD)
-    att = attend(q_rows, kv_win, qpos_rows - base, lo_rows - base, tiles, plane, depth + 1).reshape(row_count, query_width)
+    att = window_attend(
+        kv_local, q_rows, qpos_rows - base, lo_rows - base, depth, plane, n_ctx, need_col
+    ).reshape(row_count, query_width)
 
     return project(att, out_weight, lax.axis_size("head"))
 

time: 110 us -> 118 us (1.073)
  Pallas kernels: 96.2 us -> 106 us
  local copies, waits for them, and re-layouts: 9.72 us -> 8.34 us
    pallas_call x2 -> x1, Pallas kernels: 62.3 us -> 75.6 us  [window_attend(): pl.pallas_call(functools.partial(window_attend_kernel, depth, plane, n_ct...]
    pallas_call x1, Pallas kernels: 33.9 us -> 30.1 us  [project(): pl.pallas_call(functools.partial(project_kernel, n_head), out_shape=jax.S...]
    broadcast_in_dim x1 -> x0, local copies, waits for them, and re-layouts: 2.01 us -> none  [gather_window(): zero = jnp.zeros((plane, depth + 1, rows, width), kv_local.dtype)]
where the time goes in v10:
time: 118 us; the launch traced here: 117 us
  Pallas kernels  106 us (90%)
  local copies, waits for them, and re-layouts  8.34 us (7%)
  other arithmetic  2.56 us (2%)
    pallas_call x1, Pallas kernels, window_attend(): pl.pallas_call(functools.partial(window_attend_kernel, depth, plane, n_ct...  75.6 us
    pallas_call x1, Pallas kernels, project(): pl.pallas_call(functools.partial(project_kernel, n_head), out_shape=jax.S...  30.1 us

profile of v10, /device:TPU:192, one launch (start us, length us, event | category | flops | bytes accessed | tf_op | source)
XLA Modules:
  0.0 116.6 jit_solution(13206310268308751310)
XLA Ops:
  0.0 0.8 dynamic-slice_multiply_fusion
  0.8 0.7 copy.9
  1.5 0.1 reduce
  1.7 0.1 select_reduce_fusion
  1.8 0.1 broadcast_in_dim.23
  1.8 0.1 mul.25
  1.9 0.1 broadcast_in_dim.25
  2.0 0.7 sub.27.lo_ref
  2.8 0.1 broadcast_in_dim.22
  2.9 0.7 sub.25.qpos_ref
  3.6 1.5 %pad_maximum_fusion.kv_ref = bf16[256,256]{1,0:T(8,128)(2,1)} fusion(bf16[256,128]{1,0:T(8,128)(2,1)} %param.10, bf16[256,128]{1,0:T(8,128)(2,1)} %param.9), kind=kLoop, calls=%fused_computation | loop fusion | flops 262144 | bytes 262144 | tf_op jit(solution)/shard_map/concatenate | solution.py:495
  5.1 2.1 %reshape.65.q_ref = bf16[2048,128]{1,0:T(8,128)(2,1)} reshape(bf16[256,1024]{1,0:T(8,128)(2,1)} %param.8) | data formatting | bytes 1048576 | tf_op jit(solution)/shard_map/reshape | solution.py:501
  7.2 75.6 %shard_map.64 = bf16[2048,128]{1,0:T(8,128)(2,1)} custom-call(bf16[256,256]{1,0:T(8,128)(2,1)} %pad_maximum_fusion.kv_ref, bf16[2048,128]{1,0:T(8,128)(2,1)} %reshape.65.q_ref, s32[1,2048]{1,0:T(1,128)} %sub.25.qpos_ref, s32[1,2048]{1,0:T(1,128)} %sub.27.lo_ref), custom_call_target="tpu_custom_call" | custom-call | tf_op jit(solution)/shard_map/pallas_call | solution.py:386
  82.8 2.1 %reshape.68.att_ref = bf16[256,1024]{1,0:T(8,128)(2,1)} reshape(bf16[2048,128]{1,0:T(8,128)(2,1)} %shard_map.64) | data formatting | bytes 1048576 | tf_op jit(solution)/shard_map/reshape | solution.py:504
  84.8 30.1 %shard_map.65 = bf16[256,512]{1,0:T(8,128)(2,1)} custom-call(bf16[256,1024]{1,0:T(8,128)(2,1)} %reshape.68.att_ref, bf16[1024,4096]{1,0:T(8,128)(2,1)} %w_ref.1), custom_call_target="tpu_custom_call" | custom-call | tf_op jit(solution)/shard_map/pallas_call | solution.py:462
  114.9 1.7 %copy.11 = bf16[256,512]{1,0:T(8,128)(2,1)} copy(bf16[256,512]{1,0:T(8,128)(2,1)} %shard_map.65) | data formatting | bytes 524288
  (3 shorter events, 0.0 us)

commit v11 on v9

--- a/solution.py
+++ b/solution.py
@@ -117,38 +117,43 @@
     across = (r + 2) % plane
     far = across + 1 - 2 * (across % 2)
     barrier = pltpu.get_barrier_semaphore()
-    for d in range(1, depth + 1):
-        @pl.when(z + d < n_z)
-        def _():
-            pl.semaphore_signal(barrier, 1, device_id=(me + d * plane, h), device_id_type=MESH_ID)
-
-        @pl.when(z - d >= 0)
-        def _():
-            pl.semaphore_signal(barrier, 1, device_id=(me - d * plane, h), device_id_type=MESH_ID)
+
+    @pl.when(z + 1 < n_z)
+    def _():
+        pl.semaphore_signal(barrier, 1, device_id=(me + plane, h), device_id_type=MESH_ID)
+
+    @pl.when(z - 1 >= 0)
+    def _():
+        pl.semaphore_signal(barrier, 1, device_id=(me - plane, h), device_id_type=MESH_ID)
 
     for peer in (mate, across):
         pl.semaphore_signal(barrier, 1, device_id=(z * plane + peer, h), device_id_type=MESH_ID)
-    pl.semaphore_wait(barrier, jnp.minimum(depth, n_z - 1 - z) + jnp.minimum(depth, z) + 2)
+    pl.semaphore_wait(barrier, jnp.minimum(1, n_z - 1 - z) + jnp.minimum(1, z) + 2)
     local = pltpu.make_async_copy(kv_ref, win_ref.at[r, depth], local_sem)
     local.start()
 
     def wanted(d):
         return (d < depth) | (r >= need_col)
 
-    def down(d):
+    def up(k):
         return pltpu.make_async_remote_copy(
-            src_ref=kv_ref,
-            dst_ref=win_ref.at[r, depth - d],
-            send_sem=send1.at[d - 1],
-            recv_sem=recv1.at[d - 1],
-            device_id=(me + d * plane, h),
+            src_ref=kv_ref if k == 1 else win_ref.at[r, depth - k + 1],
+            dst_ref=win_ref.at[r, depth - k],
+            send_sem=send1.at[k - 1],
+            recv_sem=recv1.at[k - 1],
+            device_id=(me + plane, h),
             device_id_type=MESH_ID,
         )
 
-    for d in range(1, depth + 1):
-        @pl.when((z + d < n_z) & wanted(d))
-        def _():
-            down(d).start()
+    def sends(k):
+        return (z + 1 < n_z) & (z - (k - 1) >= 0) & wanted(k)
+
+    def gets(k):
+        return (z - k >= 0) & wanted(k)
+
+    @pl.when(sends(1))
+    def _():
+        up(1).start()
 
     def has(slot, col):
         return (z - (depth - slot) >= 0) & ((slot > 0) | (col >= need_col))
@@ -166,16 +171,22 @@
     local.wait()
     hop(0, r, depth, mate).start()
     hop(1, r, depth, across).start()
-    for d in range(1, depth + 1):
-        @pl.when((z + d < n_z) & wanted(d))
-        def _():
-            down(d).wait_send()
-
-        @pl.when((z - d >= 0) & wanted(d))
-        def _():
-            down(d).wait_recv()
-            hop(0, r, depth - d, mate).start()
-            hop(1, r, depth - d, across).start()
+    for k in range(1, depth + 1):
+        @pl.when(gets(k))
+        def _():
+            up(k).wait_recv()
+            hop(0, r, depth - k, mate).start()
+            hop(1, r, depth - k, across).start()
+
+        if k < depth:
+            @pl.when(sends(k + 1))
+            def _():
+                up(k + 1).start()
+
+    for k in range(1, depth + 1):
+        @pl.when(sends(k))
+        def _():
+            up(k).wait_send()
 
     for slot in range(depth, -1, -1):
         @pl.when(has(slot, across))

time: 110 us -> 107 us (0.973)
  Pallas kernels: 96.2 us -> 92.5 us
    pallas_call x1, Pallas kernels: 38.3 us -> 32.4 us  [gather_window(): pl.pallas_call(functools.partial(window_kernel, depth, plane, n_ctx, need...]
    pallas_call x1, Pallas kernels: 24 us -> 26.3 us  [attend(): pl.pallas_call(functools.partial(attn_kernel, plane, slots), out_shape=ja...]
where the time goes in v11:
time: 107 us; the launch traced here: 106 us
  Pallas kernels  92.5 us (86%)
  local copies, waits for them, and re-layouts  9.72 us (9%)
  other arithmetic  3.49 us (3%)
    pallas_call x1, Pallas kernels, project(): pl.pallas_call(functools.partial(project_kernel, n_head), out_shape=jax.S...  33.7 us
    pallas_call x1, Pallas kernels, gather_window(): pl.pallas_call(functools.partial(window_kernel, depth, plane, n_ctx, need...  32.4 us
    pallas_call x1, Pallas kernels, attend(): pl.pallas_call(functools.partial(attn_kernel, plane, slots), out_shape=ja...  26.3 us

profile of v11, /device:TPU:192, one launch (start us, length us, event | category | flops | bytes accessed | tf_op | source)
XLA Modules:
  0.0 105.7 jit_solution(2600255241503374199)
XLA Ops:
  0.0 0.7 copy.26
  0.8 0.1 reduce
  0.9 0.1 select_reduce_fusion
  1.0 0.8 dynamic-slice_multiply_fusion
  1.8 0.1 broadcast_in_dim.31
  1.8 0.1 mul.35
  1.9 0.1 broadcast_in_dim.32
  2.0 0.7 sub.106.lo_ref
  2.8 0.1 broadcast_in_dim.30
  2.9 0.7 sub.104.qpos_ref
  3.6 0.1 mul.31
  3.7 0.1 broadcast_in_dim.27
  3.7 0.1 mul.32
  3.8 0.2 fusion
  4.0 0.1 copy.27
  4.1 0.1 copy.31
  4.2 0.1 maximum_minimum_fusion
  4.3 0.7 pad_add_fusion.tiles_ref
  4.9 1.5 %pad_maximum_fusion.kv_ref = bf16[256,256]{1,0:T(8,128)(2,1)} fusion(bf16[256,128]{1,0:T(8,128)(2,1)} %param.10, bf16[256,128]{1,0:T(8,128)(2,1)} %param.9), kind=kLoop, calls=%fused_computation | loop fusion | flops 262144 | bytes 262144 | tf_op jit(solution)/shard_map/concatenate | solution.py:325
  6.5 2.0 %broadcast_in_dim.29.zero_ref = bf16[4,6,256,256]{3,2,1,0:T(8,128)(2,1)} broadcast(bf16[]{:T(256)} %constant.85.clone.1), dimensions={} | broadcast | bytes 3145730 | tf_op jit(solution)/shard_map/broadcast_in_dim | solution.py:218
  8.5 0.0 copy-start
  8.5 32.4 %shard_map.64 = bf16[4,6,256,256]{3,2,1,0:T(8,128)(2,1)} custom-call(bf16[256,256]{1,0:T(8,128)(2,1)} %pad_maximum_fusion.kv_ref, bf16[4,6,256,256]{3,2,1,0:T(8,128)(2,1)} %broadcast_in_dim.29.zero_ref), custom_call_target="tpu_custom_call", output_to_operand_aliasing={{}: (1, {})} | custom-call | tf_op jit(solution)/shard_map/pallas_call | solution.py:219
  40.9 0.0 copy-done
  40.9 1.0 reshape.205.q_ref
  42.0 26.3 %shard_map.65 = bf16[2048,128]{1,0:T(8,128)(2,1)} custom-call(s32[2,4]{1,0:T(2,128)} %pad_add_fusion.tiles_ref, bf16[2048,128]{1,0:T(8,128)(2,1)} %reshape.205.q_ref, bf16[6144,256]{1,0:T(8,128)(2,1)} %bitcast.12, s32[1,2048]{1,0:T(1,128)} %sub.104.qpos_ref, s32[1,2048]{1,0:T(1,128)} %sub.106.lo_ref), custom_call_target="tpu_custom_call" | custom-call | tf_op jit(solution)/shard_map/pallas_call | solution.py:87
  68.3 2.1 %reshape.207.att_ref = bf16[256,1024]{1,0:T(8,128)(2,1)} reshape(bf16[2048,128]{1,0:T(8,128)(2,1)} %shard_map.65) | data formatting | bytes 1048576 | tf_op jit(solution)/shard_map/reshape | solution.py:340
  70.3 33.7 %shard_map.66 = bf16[256,512]{1,0:T(8,128)(2,1)} custom-call(bf16[256,1024]{1,0:T(8,128)(2,1)} %reshape.207.att_ref, bf16[1024,4096]{1,0:T(8,128)(2,1)} %w_ref.1), custom_call_target="tpu_custom_call" | custom-call | tf_op jit(solution)/shard_map/pallas_call | solution.py:292
  104.1 1.7 %copy.37 = bf16[256,512]{1,0:T(8,128)(2,1)} copy(bf16[256,512]{1,0:T(8,128)(2,1)} %shard_map.66) | data formatting | bytes 524288
  (6 shorter events, 0.1 us)
Async XLA Ops:
  8.5 32.4 %copy-start = (bf16[256,1024]{1,0:T(8,128)(2,1)S(1)}, bf16[256,1024]{1,0:T(8,128)(2,1)}, u32[]{:S(2)}) copy-start(bf16[256,1024]{1,0:T(8,128)(2,1)} %param.8) | copy-start | bytes 1572868

commit v12 on v11

--- a/solution.py
+++ b/solution.py
@@ -106,8 +106,7 @@
 MESH_ID = pl.DeviceIdType.MESH
 
 
-def window_kernel(depth, plane, n_ctx, need_col, kv_ref, zero_ref, win_ref, send1, recv1, send2, recv2, local_sem):
-    del zero_ref
+def window_kernel(depth, plane, n_ctx, need_col, kv_ref, win_ref, send1, recv1, send2, recv2, local_sem):
     me = lax.axis_index("ctx")
     h = lax.axis_index("head")
     z = me // plane
@@ -215,11 +214,10 @@
 
 def gather_window(kv_local, depth, plane, n_ctx, need_col):
     rows, width = kv_local.shape
-    zero = jnp.zeros((plane, depth + 1, rows, width), kv_local.dtype)
     return pl.pallas_call(
         functools.partial(window_kernel, depth, plane, n_ctx, need_col),
-        out_shape=jax.ShapeDtypeStruct(zero.shape, zero.dtype),
-        in_specs=[pl.BlockSpec(memory_space=pl.ANY), pl.BlockSpec(memory_space=pl.ANY)],
+        out_shape=jax.ShapeDtypeStruct((plane, depth + 1, rows, width), kv_local.dtype),
+        in_specs=[pl.BlockSpec(memory_space=pl.ANY)],
         out_specs=pl.BlockSpec(memory_space=pl.ANY),
         scratch_shapes=[
             pltpu.SemaphoreType.DMA((depth,)),
@@ -228,77 +226,101 @@
             pltpu.SemaphoreType.DMA((3, depth + 1)),
             pltpu.SemaphoreType.DMA(()),
         ],
-        input_output_aliases={1: 0},
         compiler_params=pltpu.CompilerParams(collective_id=0, has_side_effects=True),
-    )(kv_local, zero)
-
-
-def project_kernel(n_head, att_ref, w_ref, o_ref, send_buf, got, send_sem, recv_sem):
+    )(kv_local)
+
+
+def project_kernel(ny, att_ref, w_ref, o_ref, sbuf, got1, tot, s2buf, got2, send1, recv1, send2, recv2):
     me = lax.axis_index("head")
     row = lax.axis_index("ctx")
+    y = me // 2
+    xl = me % 2
+    other = 1 - xl
     cols = o_ref.shape[1]
+    wide = 2 * cols
     barrier = pltpu.get_barrier_semaphore()
-    for d in range(1, n_head):
+    for e in range(1, ny):
         pl.semaphore_signal(
-            barrier, 1, device_id=(row, lax.rem(me + d, n_head)), device_id_type=MESH_ID
-        )
-    pl.semaphore_wait(barrier, n_head - 1)
-
-    def part(dst):
-        c0 = pl.multiple_of(dst * cols, cols)
+            barrier, 1, device_id=(row, lax.rem(y + e, ny) * 2 + xl), device_id_type=MESH_ID
+        )
+    pl.semaphore_signal(barrier, 1, device_id=(row, y * 2 + other), device_id_type=MESH_ID)
+    pl.semaphore_wait(barrier, ny)
+
+    def part(yy):
+        c0 = pl.multiple_of(yy * wide, wide)
         return jnp.dot(
-            att_ref[...], w_ref[:, pl.ds(c0, cols)], preferred_element_type=jnp.float32
+            att_ref[...], w_ref[:, pl.ds(c0, wide)], preferred_element_type=jnp.float32
         ).astype(jnp.bfloat16)
 
-    def send(d):
-        dst = lax.rem(me + d, n_head)
+    def send(e):
         return pltpu.make_async_remote_copy(
-            src_ref=send_buf.at[d - 1],
-            dst_ref=got.at[me],
-            send_sem=send_sem.at[d - 1],
-            recv_sem=recv_sem.at[d - 1],
-            device_id=(row, dst),
+            src_ref=sbuf.at[e - 1],
+            dst_ref=got1.at[y],
+            send_sem=send1.at[e - 1],
+            recv_sem=recv1.at[e - 1],
+            device_id=(row, lax.rem(y + e, ny) * 2 + xl),
             device_id_type=MESH_ID,
         )
 
-    def arrival(d):
-        src = lax.rem(me + n_head - d, n_head)
+    def arrival(e):
+        src = lax.rem(y + ny - e, ny)
         return pltpu.make_async_remote_copy(
-            src_ref=send_buf.at[d - 1],
-            dst_ref=got.at[src],
-            send_sem=send_sem.at[d - 1],
-            recv_sem=recv_sem.at[d - 1],
-            device_id=(row, src),
+            src_ref=sbuf.at[e - 1],
+            dst_ref=got1.at[src],
+            send_sem=send1.at[e - 1],
+            recv_sem=recv1.at[e - 1],
+            device_id=(row, src * 2 + xl),
             device_id_type=MESH_ID,
         )
 
-    send_buf[0] = part(lax.rem(me + 1, n_head))
-    for d in range(1, n_head):
-        if d + 1 < n_head:
-            send_buf[d] = part(lax.rem(me + d + 1, n_head))
-        send(d).start()
-    total = part(me).astype(jnp.float32)
-    for d in range(1, n_head):
-        send(d).wait_send()
-        arrival(d).wait_recv()
-        total = total + got[lax.rem(me + n_head - d, n_head)].astype(jnp.float32)
-    o_ref[...] = total.astype(o_ref.dtype)
+    sbuf[0] = part(lax.rem(y + 1, ny))
+    for e in range(1, ny):
+        if e + 1 < ny:
+            sbuf[e] = part(lax.rem(y + e + 1, ny))
+        send(e).start()
+    total = part(y).astype(jnp.float32)
+    for e in range(1, ny):
+        send(e).wait_send()
+        arrival(e).wait_recv()
+        total = total + got1[lax.rem(y + ny - e, ny)].astype(jnp.float32)
+    tot[...] = total
+    s2buf[...] = tot[:, pl.ds(pl.multiple_of(other * cols, cols), cols)]
+    cross = pltpu.make_async_remote_copy(
+        src_ref=s2buf,
+        dst_ref=got2,
+        send_sem=send2,
+        recv_sem=recv2,
+        device_id=(row, y * 2 + other),
+        device_id_type=MESH_ID,
+    )
+    cross.start()
+    cross.wait_send()
+    cross.wait_recv()
+    o_ref[...] = (
+        tot[:, pl.ds(pl.multiple_of(xl * cols, cols), cols)] + got2[...]
+    ).astype(o_ref.dtype)
 
 
 def project(att, out_weight, n_head):
     rows = att.shape[0]
     cols = out_weight.shape[1] // n_head
+    ny = n_head // 2
     vmem = pltpu.MemorySpace.VMEM if hasattr(pltpu, "MemorySpace") else pltpu.VMEM
     return pl.pallas_call(
-        functools.partial(project_kernel, n_head),
+        functools.partial(project_kernel, ny),
         out_shape=jax.ShapeDtypeStruct((rows, cols), jnp.bfloat16),
         in_specs=[pl.BlockSpec(memory_space=vmem), pl.BlockSpec(memory_space=vmem)],
         out_specs=pl.BlockSpec(memory_space=vmem),
         scratch_shapes=[
-            pltpu.VMEM((n_head - 1, rows, cols), jnp.bfloat16),
-            pltpu.VMEM((n_head, rows, cols), jnp.bfloat16),
-            pltpu.SemaphoreType.DMA((n_head - 1,)),
-            pltpu.SemaphoreType.DMA((n_head - 1,)),
+            pltpu.VMEM((ny - 1, rows, 2 * cols), jnp.bfloat16),
+            pltpu.VMEM((ny, rows, 2 * cols), jnp.bfloat16),
+            pltpu.VMEM((rows, 2 * cols), jnp.float32),
+            pltpu.VMEM((rows, cols), jnp.float32),
+            pltpu.VMEM((rows, cols), jnp.float32),
+            pltpu.SemaphoreType.DMA((ny - 1,)),
+            pltpu.SemaphoreType.DMA((ny - 1,)),
+            pltpu.SemaphoreType.DMA(()),
+            pltpu.SemaphoreType.DMA(()),
         ],
         compiler_params=pltpu.CompilerParams(collective_id=1, has_side_effects=True),
     )(att, out_weight)
@@ -327,6 +349,7 @@
     plane = PLANE
     depth = min(n_ctx // plane - 1, -(-(LONGEST - 1) // (plane * row_count)))
     need_col = max(0, -(-(plane * row_count * depth - (LONGEST - 1) - (row_count - 1)) // row_count))
+    need_col = need_col // (TK // SHARD) * (TK // SHARD)
     kv_win = gather_window(kv_local, depth, plane, n_ctx, need_col)
     kv_win = kv_win.reshape(-1, kv_win.shape[-1])
     base = (here // plane - depth) * plane * row_count

time: 107 us -> 119 us (1.11)
  Pallas kernels: 92.5 us -> 106 us
    pallas_call x1, Pallas kernels: 33.7 us -> 46.3 us  [project(): pl.pallas_call(functools.partial(project_kernel, ny), out_shape=jax.Shape...]
    broadcast_in_dim x1 -> x0, local copies, waits for them, and re-layouts: 2.01 us -> none  [gather_window(): zero = jnp.zeros((plane, depth + 1, rows, width), kv_local.dtype)]
    pallas_call x1, Pallas kernels: 32.4 us -> 33.8 us  [gather_window(): pl.pallas_call(functools.partial(window_kernel, depth, plane, n_ctx, need...]
where the time goes in v12:
time: 119 us
  Pallas kernels  106 us (89%)
  local copies, waits for them, and re-layouts  8.75 us (7%)
  other arithmetic  3.48 us (3%)
    pallas_call x1, Pallas kernels, project(): pl.pallas_call(functools.partial(project_kernel, ny), out_shape=jax.Shape...  46.3 us
    pallas_call x1, Pallas kernels, gather_window(): pl.pallas_call(functools.partial(window_kernel, depth, plane, n_ctx, need...  33.8 us
    pallas_call x1, Pallas kernels, attend(): pl.pallas_call(functools.partial(attn_kernel, plane, slots), out_shape=ja...  26.3 us

profile of v12, /device:TPU:192, one launch (start us, length us, event | category | flops | bytes accessed | tf_op | source)
XLA Modules:
  0.0 118.7 jit_solution(10277253543826455483)
XLA Ops:
  0.0 0.8 dynamic-slice_multiply_fusion
  0.8 0.1 mul.31
  0.9 0.7 copy.25
  1.6 0.1 reduce
  1.8 0.1 select_reduce_fusion
  1.8 0.1 broadcast_in_dim.24
  1.9 0.1 mul.32
  2.0 0.2 fusion
  2.2 0.1 copy.30
  2.3 0.1 copy.26
  2.4 0.1 maximum_minimum_fusion
  2.5 0.7 pad_add_fusion.tiles_ref
  3.1 0.1 broadcast_in_dim.27
  3.2 0.1 mul.35
  3.3 0.1 broadcast_in_dim.28
  3.4 0.7 sub.106.lo_ref
  4.1 0.1 broadcast_in_dim.26
  4.2 0.7 sub.104.qpos_ref
  4.9 1.5 %pad_maximum_fusion.kv_ref = bf16[256,256]{1,0:T(8,128)(2,1)} fusion(bf16[256,128]{1,0:T(8,128)(2,1)} %param.10, bf16[256,128]{1,0:T(8,128)(2,1)} %param.9), kind=kLoop, calls=%fused_computation | loop fusion | flops 262144 | bytes 262144 | tf_op jit(solution)/shard_map/concatenate | solution.py:347
  6.5 2.1 %reshape.205.q_ref = bf16[2048,128]{1,0:T(8,128)(2,1)} reshape(bf16[256,1024]{1,0:T(8,128)(2,1)} %param.8) | data formatting | bytes 1048576 | tf_op jit(solution)/shard_map/reshape | solution.py:362
  8.6 33.8 %shard_map.64 = bf16[4,6,256,256]{3,2,1,0:T(8,128)(2,1)} custom-call(bf16[256,256]{1,0:T(8,128)(2,1)} %pad_maximum_fusion.kv_ref), custom_call_target="tpu_custom_call" | custom-call | tf_op jit(solution)/shard_map/pallas_call | solution.py:217
  42.4 26.3 %shard_map.65 = bf16[2048,128]{1,0:T(8,128)(2,1)} custom-call(s32[2,4]{1,0:T(2,128)} %pad_add_fusion.tiles_ref, bf16[2048,128]{1,0:T(8,128)(2,1)} %reshape.205.q_ref, bf16[6144,256]{1,0:T(8,128)(2,1)} %bitcast.12, s32[1,2048]{1,0:T(1,128)} %sub.104.qpos_ref, s32[1,2048]{1,0:T(1,128)} %sub.106.lo_ref), custom_call_target="tpu_custom_call" | custom-call | tf_op jit(solution)/shard_map/pallas_call | solution.py:87
  68.7 2.1 %reshape.207.att_ref = bf16[256,1024]{1,0:T(8,128)(2,1)} reshape(bf16[2048,128]{1,0:T(8,128)(2,1)} %shard_map.65) | data formatting | bytes 1048576 | tf_op jit(solution)/shard_map/reshape | solution.py:363
  70.8 46.3 %shard_map.66 = bf16[256,512]{1,0:T(8,128)(2,1)} custom-call(bf16[256,1024]{1,0:T(8,128)(2,1)} %reshape.207.att_ref, bf16[1024,4096]{1,0:T(8,128)(2,1)} %w_ref.1), custom_call_target="tpu_custom_call" | custom-call | tf_op jit(solution)/shard_map/pallas_call | solution.py:309
  117.0 1.7 %copy.35 = bf16[256,512]{1,0:T(8,128)(2,1)} copy(bf16[256,512]{1,0:T(8,128)(2,1)} %shard_map.66) | data formatting | bytes 524288
  (6 shorter events, 0.1 us)

commit v13 on v11

--- a/solution.py
+++ b/solution.py
@@ -18,12 +18,15 @@
 
 
 def attn_kernel(plane, slots, tiles_ref, q_ref, kv_ref, qpos_ref, lo_ref, o_ref, m_sc, l_sc, acc_sc):
-    n_q = q_ref.shape[0] // TQ
+    n_q = q_ref.shape[0] * q_ref.shape[1] // (HD * TQ)
     scale = HD ** (-0.5)
 
     def q_body(qi, carry):
         r0 = pl.multiple_of(qi * TQ, TQ)
-        q = q_ref[pl.ds(r0, TQ), :]
+        heads = TQ // q_ref.shape[0]
+        q = jnp.concatenate([
+            q_ref[:, pl.ds(pl.multiple_of((qi * heads + g) * HD, HD), HD)] for g in range(heads)
+        ], axis=0)
         qpos = qpos_ref[:, pl.ds(r0, TQ)]
         lo = lo_ref[:, pl.ds(r0, TQ)]
         m_sc[...] = jnp.full(m_sc.shape, NEG_FILL, jnp.float32)
@@ -75,18 +78,20 @@
         lax.fori_loop(tiles_ref[qi, 0], tiles_ref[qi, 1], masked_body, 0)
         lax.fori_loop(tiles_ref[qi, 1], tiles_ref[qi, 2], open_body, 0)
         lax.fori_loop(tiles_ref[qi, 2], tiles_ref[qi, 3], masked_body, 0)
-        o_ref[pl.ds(r0, TQ), :] = (acc_sc[...] / l_sc[...]).T.astype(o_ref.dtype)
+        out = (acc_sc[...] / l_sc[...]).T.astype(o_ref.dtype)
+        tokens = q_ref.shape[0]
+        for g in range(heads):
+            o_ref[:, pl.ds(pl.multiple_of((qi * heads + g) * HD, HD), HD)] = out[g * tokens:(g + 1) * tokens]
         return carry
 
     lax.fori_loop(0, n_q, q_body, 0)
 
 
 def attend(q_rows, kv_all, qpos_rows, lo_rows, tiles, plane, slots):
-    rows = q_rows.shape[0]
     vmem = pltpu.MemorySpace.VMEM if hasattr(pltpu, "MemorySpace") else pltpu.VMEM
     return pl.pallas_call(
         functools.partial(attn_kernel, plane, slots),
-        out_shape=jax.ShapeDtypeStruct((rows, HD), jnp.bfloat16),
+        out_shape=jax.ShapeDtypeStruct(q_rows.shape, jnp.bfloat16),
         in_specs=[
             pl.BlockSpec(memory_space=pltpu.SMEM),
             pl.BlockSpec(memory_space=vmem),
@@ -314,13 +319,13 @@
     doc_start = jnp.max(jnp.where(doc_ends[None, :] <= pos[:, None], doc_ends[None, :], 0), axis=1)
     block_lo = lax.dynamic_slice_in_dim(mask_lo, here * (row_count // BLK), row_count // BLK)
     lo_tok = jnp.maximum(jnp.repeat(block_lo, BLK) * BLK, doc_start)
-    qpos_rows = jnp.repeat(pos, group_size)[None, :]
-    lo_rows = jnp.repeat(lo_tok, group_size)[None, :]
-    tok_per_tile = TQ // group_size
-    tile_lo = jnp.min(lo_tok.reshape(-1, tok_per_tile), axis=1)
-    tile_hi = pos.reshape(-1, tok_per_tile)[:, -1]
-    tile_lo_max = jnp.max(lo_tok.reshape(-1, tok_per_tile), axis=1)
-    tile_hi_min = pos.reshape(-1, tok_per_tile)[:, 0]
+    qpos_rows = jnp.tile(pos, group_size)[None, :]
+    lo_rows = jnp.tile(lo_tok, group_size)[None, :]
+    n_q = row_count * group_size // TQ
+    tile_lo = jnp.full((n_q,), jnp.min(lo_tok))
+    tile_hi = jnp.full((n_q,), pos[-1])
+    tile_lo_max = jnp.full((n_q,), jnp.max(lo_tok))
+    tile_hi_min = jnp.full((n_q,), pos[0])
 
     kv_local = jnp.concatenate([key_rows, values], axis=1)
     n_ctx = lax.axis_size("ctx")
@@ -336,8 +341,7 @@
     t1 = jnp.clip((tile_lo_max - base + TK - 1) // TK, t0, t3)
     t2 = jnp.clip((tile_hi_min - base + 1) // TK, t1, t3)
     tiles = jnp.stack([t0, t1, t2, t3], axis=1).astype(jnp.int32)
-    q_rows = queries.reshape(row_count * group_size, HD)
-    att = attend(q_rows, kv_win, qpos_rows - base, lo_rows - base, tiles, plane, depth + 1).reshape(row_count, query_width)
+    att = attend(queries, kv_win, qpos_rows - base, lo_rows - base, tiles, plane, depth + 1)
 
     return project(att, out_weight, lax.axis_size("head"))
 

time: 107 us -> 104 us (0.972)
  the two profiles are of different devices: /device:TPU:192 before, /device:TPU:160 now
where the time goes in v13:
time: 104 us
  Pallas kernels  90.6 us (87%)
  local copies, waits for them, and re-layouts  7.07 us (7%)
  other arithmetic  3.3 us (3%)
  between operations  2.68 us (3%)
    pallas_call x1, Pallas kernels, project(): pl.pallas_call(functools.partial(project_kernel, n_head), out_shape=jax.S...  33.9 us
    pallas_call x1, Pallas kernels, gather_window(): pl.pallas_call(functools.partial(window_kernel, depth, plane, n_ctx, need...  30.3 us
    pallas_call x1, Pallas kernels, attend(): pl.pallas_call(functools.partial(attn_kernel, plane, slots), out_shape=ja...  26.4 us
    unnamed x5, local copies, waits for them, and re-layouts  2.89 us

profile of v13, /device:TPU:160, one launch (start us, length us, event | category | flops | bytes accessed | tf_op | source)
XLA Modules:
  0.0 103.6 jit_solution(8659621791666389744)
XLA Ops:
  0.0 0.7 fusion
  1.4 0.8 dynamic-slice_multiply_fusion
  2.2 0.1 broadcast_in_dim.27
  2.2 0.1 broadcast_in_dim.28
  2.3 0.7 copy.10
  3.1 0.1 reduce.8
  3.2 0.1 select_reduce_fusion
  3.3 0.7 maximum_reduce_fusion
  5.9 0.1 add_add_fusion
  6.0 0.6 broadcast.348.tiles_ref
  6.6 1.5 %pad_maximum_fusion.kv_ref = bf16[256,256]{1,0:T(8,128)(2,1)} fusion(bf16[256,128]{1,0:T(8,128)(2,1)} %param.10, bf16[256,128]{1,0:T(8,128)(2,1)} %param.9), kind=kLoop, calls=%fused_computation | loop fusion | flops 262144 | bytes 262144 | tf_op jit(solution)/shard_map/concatenate | solution.py:330
  8.1 2.0 %broadcast_in_dim.31.zero_ref = bf16[4,6,256,256]{3,2,1,0:T(8,128)(2,1)} broadcast(bf16[]{:T(256)} %constant.91.clone.1), dimensions={} | broadcast | bytes 3145730 | tf_op jit(solution)/shard_map/broadcast_in_dim | solution.py:223
  10.1 30.3 %shard_map.64 = bf16[4,6,256,256]{3,2,1,0:T(8,128)(2,1)} custom-call(bf16[256,256]{1,0:T(8,128)(2,1)} %pad_maximum_fusion.kv_ref, bf16[4,6,256,256]{3,2,1,0:T(8,128)(2,1)} %broadcast_in_dim.31.zero_ref), custom_call_target="tpu_custom_call", output_to_operand_aliasing={{}: (1, {})} | custom-call | tf_op jit(solution)/shard_map/pallas_call | solution.py:224
  40.5 0.6 copy.11
  41.1 0.6 copy.12
  41.7 26.4 %shard_map.65.att_ref = bf16[256,1024]{1,0:T(8,128)(2,1)} custom-call(s32[2,4]{1,0:T(2,128)} %broadcast.348.tiles_ref, bf16[256,1024]{1,0:T(8,128)(2,1)} %q_ref.1, bf16[6144,256]{1,0:T(8,128)(2,1)} %bitcast.16, s32[1,2048]{1,0:T(1,128)} %bitcast.17, s32[1,2048]{1,0:T(1,128)} %bitcast.18), custom_call_target="tpu_custom_call" | custom-call | tf_op jit(solution)/shard_map/pallas_call | solution.py:92
  68.1 33.9 %shard_map.66 = bf16[256,512]{1,0:T(8,128)(2,1)} custom-call(bf16[256,1024]{1,0:T(8,128)(2,1)} %shard_map.65.att_ref, bf16[1024,4096]{1,0:T(8,128)(2,1)} %w_ref.1), custom_call_target="tpu_custom_call" | custom-call | tf_op jit(solution)/shard_map/pallas_call | solution.py:297
  102.0 1.7 %copy.15 = bf16[256,512]{1,0:T(8,128)(2,1)} copy(bf16[256,512]{1,0:T(8,128)(2,1)} %shard_map.66) | data formatting | bytes 524288
  (4 shorter events, 0.0 us)
